TPU v7x, 512 devices: a whole 4x4x16 slice. The times are simulated.
512 devices in a mesh: dp: 8 (over y, x_hi), seq: 64 (over x_lo, z, core).
Axes of the slice: x: 4 (x_hi: 2, x_lo: 2; x = x_hi * 2 + x_lo), y: 4, z: 16, core: 2. Of those that a mesh axis runs over, the one named last changes fastest.
Arguments:
- signal: bfloat16 [8, 16, 512, 512], P(None, 'dp', 'seq'), may hold values from -6 to 6
- cotangent: bfloat16 [8, 16, 512, 512], P(None, 'dp', 'seq'), may hold values from -6 to 6
- filter_spec: bfloat16 [2, 8, 512, 512], P(None, None, 'seq'), may hold values from -4.1875 to 4.1875
Outputs:
- output: bfloat16 [8, 16, 512, 512], P(None, 'dp', 'seq')
- grad_signal: bfloat16 [8, 16, 512, 512], P(None, 'dp', 'seq')
- grad_filter: bfloat16 [2, 8, 512, 512], P(None, None, 'seq')
All inputs are finite; a program needn't handle non-finite values.
Results may differ from a plain program's by a relative error of at most 0.0091.
Values may be sent and summed in bfloat16 or wider, within the bound.
No kernel may reach another device: no remote copies, remote signals or barrier semaphores. Data moves between devices by JAX's collectives and lax.ppermute only.
A program may use at most 64 MiB of HBM per device.

v0:
```python
import math

import jax
import jax.numpy as jnp
from jax import lax
from jax.sharding import PartitionSpec as P

NB = 512


def unit_tables(block_size):
    steps_index = jnp.arange(block_size, dtype=jnp.int32)
    product_index = steps_index[:, None] * steps_index[None, :] % block_size
    phases = product_index.astype(jnp.float32) * (2.0 * math.pi / block_size)
    factor = 1.0 / math.sqrt(block_size)
    return (
        (jnp.cos(phases) * factor).astype(jnp.bfloat16),
        (-jnp.sin(phases) * factor).astype(jnp.bfloat16),
    )


def twiddle(row_index, col_index, length_all, orient):
    phases = (row_index[:, None] * col_index[None, :]).astype(jnp.float32) * (
        orient * 2.0 * math.pi / length_all
    )
    return (jnp.cos(phases), jnp.sin(phases))


def forward_rows(signal, tables, first_row, length_all):
    big_cos, big_sin, small_cos, small_sin = tables
    real_part = jnp.einsum("ncrs,as->ncra", signal, big_cos, preferred_element_type=jnp.float32)
    imaginary = jnp.einsum("ncrs,as->ncra", signal, big_sin, preferred_element_type=jnp.float32)
    row_index = first_row + jnp.arange(signal.shape[2], dtype=jnp.int32)
    col_index = jnp.arange(signal.shape[3], dtype=jnp.int32)
    turn_cos, turn_sin = twiddle(row_index, col_index, length_all, -1.0)
    middle = jnp.stack(
        [real_part * turn_cos - imaginary * turn_sin, real_part * turn_sin + imaginary * turn_cos]
    ).astype(jnp.bfloat16)
    received = lax.all_to_all(middle, "seq", split_axis=4, concat_axis=3, tiled=True)
    real_received = received[0]
    imaginary_received = received[1]
    out_real = jnp.einsum(
        "ncra,qr->ncaq", real_received, small_cos, preferred_element_type=jnp.float32
    ) - jnp.einsum(
        "ncra,qr->ncaq", imaginary_received, small_sin, preferred_element_type=jnp.float32
    )
    out_imaginary = jnp.einsum(
        "ncra,qr->ncaq", imaginary_received, small_cos, preferred_element_type=jnp.float32
    ) + jnp.einsum("ncra,qr->ncaq", real_received, small_sin, preferred_element_type=jnp.float32)
    return jnp.stack([out_real, out_imaginary])


def inverse_rows(spectrum, tables, first_freq, length_all):
    big_cos, big_sin, small_cos, small_sin = tables
    real_part = jnp.einsum(
        "ncaq,rq->ncar", spectrum[0], small_cos, preferred_element_type=jnp.float32
    ) + jnp.einsum("ncaq,rq->ncar", spectrum[1], small_sin, preferred_element_type=jnp.float32)
    imaginary = jnp.einsum(
        "ncaq,rq->ncar", spectrum[1], small_cos, preferred_element_type=jnp.float32
    ) - jnp.einsum("ncaq,rq->ncar", spectrum[0], small_sin, preferred_element_type=jnp.float32)
    row_index = first_freq + jnp.arange(spectrum.shape[3], dtype=jnp.int32)
    col_index = jnp.arange(spectrum.shape[4], dtype=jnp.int32)
    turn_cos, turn_sin = twiddle(row_index, col_index, length_all, 1.0)
    middle = jnp.stack(
        [real_part * turn_cos - imaginary * turn_sin, real_part * turn_sin + imaginary * turn_cos]
    ).astype(jnp.bfloat16)
    received = lax.all_to_all(middle, "seq", split_axis=4, concat_axis=3, tiled=True)
    total = jnp.einsum(
        "ncar,sa->ncrs", received[0], big_cos, preferred_element_type=jnp.float32
    ) + jnp.einsum("ncar,sa->ncrs", received[1], big_sin, preferred_element_type=jnp.float32)
    return total.astype(jnp.bfloat16)


def body(signal, cotangent, filter_spec):
    rows_total = signal.shape[2] * lax.axis_size("seq")
    big_cos, big_sin = unit_tables(NB)
    small_cos, small_sin = unit_tables(rows_total)
    tables = (big_cos, big_sin, small_cos, small_sin)
    length_all = NB * rows_total
    first_row = lax.axis_index("seq") * signal.shape[2]
    first_freq = lax.axis_index("seq") * (NB // lax.axis_size("seq"))
    filter_real = filter_spec[0].astype(jnp.float32)[:, None]
    filter_imaginary = filter_spec[1].astype(jnp.float32)[:, None]
    signal_spec = forward_rows(signal, tables, first_row, length_all)
    output = inverse_rows(
        jnp.stack(
            [
                filter_real * signal_spec[0] - filter_imaginary * signal_spec[1],
                filter_real * signal_spec[1] + filter_imaginary * signal_spec[0],
            ]
        ).astype(jnp.bfloat16),
        tables,
        first_freq,
        length_all,
    )
    cotangent_spec = forward_rows(cotangent, tables, first_row, length_all)
    grad_signal = inverse_rows(
        jnp.stack(
            [
                filter_real * cotangent_spec[0] + filter_imaginary * cotangent_spec[1],
                filter_real * cotangent_spec[1] - filter_imaginary * cotangent_spec[0],
            ]
        ).astype(jnp.bfloat16),
        tables,
        first_freq,
        length_all,
    )
    grad_terms = jnp.stack(
        [
            jnp.sum(
                cotangent_spec[0] * signal_spec[0] + cotangent_spec[1] * signal_spec[1], axis=1
            ),
            jnp.sum(
                cotangent_spec[1] * signal_spec[0] - cotangent_spec[0] * signal_spec[1], axis=1
            ),
        ]
    )
    grad_filter = lax.psum(grad_terms, "dp")
    return (output, grad_signal, grad_filter.astype(jnp.bfloat16))


def solution(mesh):
    placed = (P(None, "dp", "seq", None), P(None, "dp", "seq", None), P(None, None, "seq", None))
    return jax.shard_map(
        body,
        mesh=mesh,
        in_specs=placed,
        out_specs=(
            P(None, "dp", "seq", None),
            P(None, "dp", "seq", None),
            P(None, None, "seq", None),
        ),
        check_vma=False,
    )
```

profile of v0, /device:TPU:32, one launch (start us, length us, event | category | flops | bytes accessed | tf_op | source)
XLA Modules:
  0.0 469.7 jit_solution(13341119563249871920)
XLA Ops:
  19.4 7.5 %copy.30 = bf16[2,8,2,8,512]{3,2,1,0,4:T(2,128)(2,1)} copy(bf16[2,8,2,8,512]{4,3,2,1,0:T(8,128)(2,1)S(1)} %get-tuple-element.40) | data formatting | bytes 524288 | tf_op jit(solution)/shard_map/stack | solution.py:36
  26.9 12.7 %reshape.129 = bf16[64,2,1024]{2,1,0:T(2,128)(2,1)} reshape(bf16[512,2,8,2,8]{4,3,2,1,0:T(2,128)(2,1)} %bitcast.148) | data formatting | bytes 524288
  39.7 17.2 %all-to-all-start.2 = ((bf16[64,2,1024]{2,1,0:T(2,128)(2,1)}), bf16[64,2,1024]{2,1,0:T(2,128)(2,1)S(1)}, u32[]{:S(2)}, u32[]{:S(2)}) async-start(bf16[64,2,1024]{2,1,0:T(2,128)(2,1)} %reshape.129), calls=%async_computation.2 | async-start | bytes 524288 | tf_op jit(solution)/shard_map/all_to_all | solution.py:39
  56.9 7.5 %copy.22 = bf16[2,8,2,8,512]{3,2,1,0,4:T(2,128)(2,1)} copy(bf16[2,8,2,8,512]{4,3,2,1,0:T(8,128)(2,1)S(1)} %get-tuple-element.39) | data formatting | bytes 524288 | tf_op jit(solution)/shard_map/stack | solution.py:36
  64.4 12.8 %reshape.125 = bf16[64,2,1024]{2,1,0:T(2,128)(2,1)} reshape(bf16[512,2,8,2,8]{4,3,2,1,0:T(2,128)(2,1)} %bitcast.149) | data formatting | bytes 524288
  78.1 12.8 %all-to-all-start = ((bf16[64,2,1024]{2,1,0:T(2,128)(2,1)}), bf16[64,2,1024]{2,1,0:T(2,128)(2,1)S(1)}, u32[]{:S(2)}, u32[]{:S(2)}) async-start(bf16[64,2,1024]{2,1,0:T(2,128)(2,1)} %reshape.125), calls=%async_computation | async-start | bytes 524288 | tf_op jit(solution)/shard_map/all_to_all | solution.py:39
  90.9 6.0 %reshape.130 = bf16[512,2,8,2,8]{4,3,2,1,0:T(2,128)(2,1)} reshape(bf16[64,2,1024]{2,1,0:T(2,128)(2,1)S(1)} %all-to-all-done.2) | data formatting | bytes 524288
  96.9 13.4 %copy.42 = bf16[2,8,2,8,64,8]{5,4,3,2,1,0:T(8,128)(2,1)} copy(bf16[2,8,2,8,64,8]{3,2,1,0,5,4:T(2,128)(2,1)} %bitcast.150) | data formatting | bytes 524288 | tf_op jit(solution)/shard_map/all_to_all | solution.py:39
  110.3 5.8 %fusion.177 = (bf16[1,8,2,64,8,8]{5,3,4,2,1,0:T(8,128)(2,1)}, bf16[1,8,2,64,8,8]{5,3,4,2,1,0:T(8,128)(2,1)}) fusion(bf16[2,8,2,64,8,8]{5,3,4,2,1,0:T(8,128)(2,1)} %bitcast.144), kind=kLoop, calls=%fused_computation.197 | loop fusion | bytes 524288 | tf_op jit(solution)/shard_map/slice | solution.py:41
  116.1 6.1 %copy.32 = bf16[1,8,2,64,8,8]{4,3,5,2,1,0:T(8,128)(2,1)S(1)} copy(bf16[1,8,2,64,8,8]{5,3,4,2,1,0:T(8,128)(2,1)} %get-tuple-element.8) | data formatting | bytes 262144 | tf_op jit(solution)/shard_map/slice | solution.py:40
  125.1 6.1 %copy.33 = bf16[1,8,2,64,8,8]{4,3,5,2,1,0:T(8,128)(2,1)S(1)} copy(bf16[1,8,2,64,8,8]{5,3,4,2,1,0:T(8,128)(2,1)} %get-tuple-element.7) | data formatting | bytes 262144 | tf_op jit(solution)/shard_map/slice | solution.py:41
  147.1 6.0 %reshape.126 = bf16[512,2,8,2,8]{4,3,2,1,0:T(2,128)(2,1)} reshape(bf16[64,2,1024]{2,1,0:T(2,128)(2,1)S(1)} %all-to-all-done) | data formatting | bytes 524288
  153.1 13.4 %copy.40 = bf16[2,8,2,8,64,8]{5,4,3,2,1,0:T(8,128)(2,1)} copy(bf16[2,8,2,8,64,8]{3,2,1,0,5,4:T(2,128)(2,1)} %bitcast.151) | data formatting | bytes 524288 | tf_op jit(solution)/shard_map/all_to_all | solution.py:39
  166.6 5.8 %fusion.179 = (bf16[1,8,2,64,8,8]{5,3,4,2,1,0:T(8,128)(2,1)}, bf16[1,8,2,64,8,8]{5,3,4,2,1,0:T(8,128)(2,1)}) fusion(bf16[2,8,2,64,8,8]{5,3,4,2,1,0:T(8,128)(2,1)} %bitcast.145), kind=kLoop, calls=%fused_computation.199 | loop fusion | bytes 524288 | tf_op jit(solution)/shard_map/slice | solution.py:41
  172.3 6.1 %copy.24 = bf16[1,8,2,64,8,8]{4,3,5,2,1,0:T(8,128)(2,1)S(1)} copy(bf16[1,8,2,64,8,8]{5,3,4,2,1,0:T(8,128)(2,1)} %get-tuple-element.12) | data formatting | bytes 262144 | tf_op jit(solution)/shard_map/slice | solution.py:40
  186.6 6.1 %copy.25 = bf16[1,8,2,64,8,8]{4,3,5,2,1,0:T(8,128)(2,1)S(1)} copy(bf16[1,8,2,64,8,8]{5,3,4,2,1,0:T(8,128)(2,1)} %get-tuple-element.11) | data formatting | bytes 262144 | tf_op jit(solution)/shard_map/slice | solution.py:41
  248.2 7.5 %copy.34 = bf16[2,8,2,8,512]{3,2,1,0,4:T(2,128)(2,1)} copy(bf16[2,8,2,8,512]{4,3,2,1,0:T(8,128)(2,1)S(1)} %pad_maximum_fusion.3) | data formatting | bytes 524288 | tf_op jit(solution)/shard_map/stack | solution.py:64
  255.7 12.7 %reshape.131 = bf16[64,2,1024]{2,1,0:T(2,128)(2,1)} reshape(bf16[512,2,8,2,8]{4,3,2,1,0:T(2,128)(2,1)} %bitcast.152) | data formatting | bytes 524288
  268.4 13.7 %all-to-all-start.3 = ((bf16[64,2,1024]{2,1,0:T(2,128)(2,1)}), bf16[64,2,1024]{2,1,0:T(2,128)(2,1)S(1)}, u32[]{:S(2)}, u32[]{:S(2)}) async-start(bf16[64,2,1024]{2,1,0:T(2,128)(2,1)} %reshape.131), calls=%async_computation.3 | async-start | bytes 524288 | tf_op jit(solution)/shard_map/all_to_all | solution.py:67
  282.1 7.5 %copy.26 = bf16[2,8,2,8,512]{3,2,1,0,4:T(2,128)(2,1)} copy(bf16[2,8,2,8,512]{4,3,2,1,0:T(8,128)(2,1)S(1)} %pad_maximum_fusion.1) | data formatting | bytes 524288 | tf_op jit(solution)/shard_map/stack | solution.py:64
  289.6 12.7 %reshape.127 = bf16[64,2,1024]{2,1,0:T(2,128)(2,1)} reshape(bf16[512,2,8,2,8]{4,3,2,1,0:T(2,128)(2,1)} %bitcast.153) | data formatting | bytes 524288
  303.4 13.0 %all-to-all-start.1 = ((bf16[64,2,1024]{2,1,0:T(2,128)(2,1)}), bf16[64,2,1024]{2,1,0:T(2,128)(2,1)S(1)}, u32[]{:S(2)}, u32[]{:S(2)}) async-start(bf16[64,2,1024]{2,1,0:T(2,128)(2,1)} %reshape.127), calls=%async_computation.1 | async-start | bytes 524288 | tf_op jit(solution)/shard_map/all_to_all | solution.py:67
  316.4 47.0 %all-reduce.1 = bf16[2,8,8,512]{3,2,1,0:T(8,128)(2,1)} all-reduce(f32[2,8,8,512]{3,2,1,0:T(8,128)S(1)} %pad_maximum_fusion.4), channel_id=1, replica_groups=mesh['dp'=8,'seq'=64] {'dp'}, use_global_device_ids=true, to_apply=%region_2.3 | all-reduce | flops 65536 | bytes 393216 | tf_op jit(solution)/shard_map/psum | solution.py:118
  363.4 6.0 %reshape.132 = bf16[512,2,8,2,8]{4,3,2,1,0:T(2,128)(2,1)} reshape(bf16[64,2,1024]{2,1,0:T(2,128)(2,1)S(1)} %all-to-all-done.3) | data formatting | bytes 524288
  369.4 13.4 %copy.43 = bf16[2,8,2,8,64,8]{5,4,3,2,1,0:T(8,128)(2,1)} copy(bf16[2,8,2,8,64,8]{3,2,1,0,5,4:T(2,128)(2,1)} %bitcast.154) | data formatting | bytes 524288 | tf_op jit(solution)/shard_map/all_to_all | solution.py:67
  388.6 6.1 %copy.36 = bf16[1,8,2,64,8,8]{4,3,5,2,1,0:T(8,128)(2,1)S(1)} copy(bf16[1,8,2,64,8,8]{5,3,4,2,1,0:T(8,128)(2,1)} %get-tuple-element.6) | data formatting | bytes 262144 | tf_op jit(solution)/shard_map/slice | solution.py:69
  397.7 6.1 %copy.37 = bf16[1,8,2,64,8,8]{4,3,5,2,1,0:T(8,128)(2,1)S(1)} copy(bf16[1,8,2,64,8,8]{5,3,4,2,1,0:T(8,128)(2,1)} %get-tuple-element.5) | data formatting | bytes 262144 | tf_op jit(solution)/shard_map/slice | solution.py:70
  411.0 6.0 %reshape.128 = bf16[512,2,8,2,8]{4,3,2,1,0:T(2,128)(2,1)} reshape(bf16[64,2,1024]{2,1,0:T(2,128)(2,1)S(1)} %all-to-all-done.1) | data formatting | bytes 524288
  417.0 13.7 %copy.41 = bf16[2,8,2,8,64,8]{5,4,3,2,1,0:T(8,128)(2,1)} copy(bf16[2,8,2,8,64,8]{3,2,1,0,5,4:T(2,128)(2,1)} %bitcast.155) | data formatting | bytes 524288 | tf_op jit(solution)/shard_map/all_to_all | solution.py:67
  430.7 5.8 %fusion.178 = (bf16[1,8,2,64,8,8]{5,3,4,2,1,0:T(8,128)(2,1)}, bf16[1,8,2,64,8,8]{5,3,4,2,1,0:T(8,128)(2,1)}) fusion(bf16[2,8,2,64,8,8]{5,3,4,2,1,0:T(8,128)(2,1)} %bitcast.147), kind=kLoop, calls=%fused_computation.198 | loop fusion | bytes 524288 | tf_op jit(solution)/shard_map/slice | solution.py:70
  436.4 6.1 %copy.28 = bf16[1,8,2,64,8,8]{4,3,5,2,1,0:T(8,128)(2,1)S(1)} copy(bf16[1,8,2,64,8,8]{5,3,4,2,1,0:T(8,128)(2,1)} %get-tuple-element.10) | data formatting | bytes 262144 | tf_op jit(solution)/shard_map/slice | solution.py:69
  449.7 6.1 %copy.29 = bf16[1,8,2,64,8,8]{4,3,5,2,1,0:T(8,128)(2,1)S(1)} copy(bf16[1,8,2,64,8,8]{5,3,4,2,1,0:T(8,128)(2,1)} %get-tuple-element.9) | data formatting | bytes 262144 | tf_op jit(solution)/shard_map/slice | solution.py:70
  (54 shorter events, 139.2 us)
Async XLA Ops:
  0.6 9.8 %copy-start = (bf16[8,2,8,512]{3,2,1,0:T(8,128)(2,1)S(1)}, bf16[8,2,8,512]{3,2,1,0:T(8,128)(2,1)}, u32[]{:S(2)}) copy-start(bf16[8,2,8,512]{3,2,1,0:T(8,128)(2,1)} %param.3) | copy-start | bytes 393220
  0.7 5.1 %copy-start.3 = (bf16[8,2,8,512]{3,2,1,0:T(8,128)(2,1)S(1)}, bf16[8,2,8,512]{3,2,1,0:T(8,128)(2,1)}, u32[]{:S(2)}) copy-start(bf16[8,2,8,512]{3,2,1,0:T(8,128)(2,1)} %param.4) | copy-start | bytes 393220
  39.7 38.4 %all-to-all-start.2 = ((bf16[64,2,1024]{2,1,0:T(2,128)(2,1)}), bf16[64,2,1024]{2,1,0:T(2,128)(2,1)S(1)}, u32[]{:S(2)}, u32[]{:S(2)}) async-start(bf16[64,2,1024]{2,1,0:T(2,128)(2,1)} %reshape.129), calls=%async_computation.2 | async-start | bytes 524288 | tf_op jit(solution)/shard_map/all_to_all | solution.py:39
  64.4 12.8 %copy-start.2 = (bf16[2,8,8,512]{3,2,1,0:T(8,128)(2,1)S(1)}, bf16[2,8,8,512]{3,2,1,0:T(8,128)(2,1)}, u32[]{:S(2)}) copy-start(bf16[2,8,8,512]{3,2,1,0:T(8,128)(2,1)} %param.5) | copy-start | bytes 393220
  78.1 69.1 %all-to-all-start = ((bf16[64,2,1024]{2,1,0:T(2,128)(2,1)}), bf16[64,2,1024]{2,1,0:T(2,128)(2,1)S(1)}, u32[]{:S(2)}, u32[]{:S(2)}) async-start(bf16[64,2,1024]{2,1,0:T(2,128)(2,1)} %reshape.125), calls=%async_computation | async-start | bytes 524288 | tf_op jit(solution)/shard_map/all_to_all | solution.py:39
  195.9 4.2 copy-start.4
  268.4 35.0 %all-to-all-start.3 = ((bf16[64,2,1024]{2,1,0:T(2,128)(2,1)}), bf16[64,2,1024]{2,1,0:T(2,128)(2,1)S(1)}, u32[]{:S(2)}, u32[]{:S(2)}) async-start(bf16[64,2,1024]{2,1,0:T(2,128)(2,1)} %reshape.131), calls=%async_computation.3 | async-start | bytes 524288 | tf_op jit(solution)/shard_map/all_to_all | solution.py:67
  303.4 107.6 %all-to-all-start.1 = ((bf16[64,2,1024]{2,1,0:T(2,128)(2,1)}), bf16[64,2,1024]{2,1,0:T(2,128)(2,1)S(1)}, u32[]{:S(2)}, u32[]{:S(2)}) async-start(bf16[64,2,1024]{2,1,0:T(2,128)(2,1)} %reshape.127), calls=%async_computation.1 | async-start | bytes 524288 | tf_op jit(solution)/shard_map/all_to_all | solution.py:67
  458.8 10.4 %copy-start.1 = (bf16[8,2,8,512]{3,2,1,0:T(8,128)(2,1)S(1)}, bf16[8,2,8,512]{3,2,1,0:T(8,128)(2,1)}, u32[]{:S(2)}) copy-start(bf16[8,2,8,512]{3,2,1,0:T(8,128)(2,1)} %param.3) | copy-start | bytes 393220
where the time goes:
time: 475 us; the launch traced here: 470 us
  local copies, waits for them, and re-layouts  255 us (54%)
  matrix products  107 us (23%)
  starting transfers between devices  56.7 us (12%)
  blocking collectives  47 us (10%)
    unnamed x18, local copies, waits for them, and re-layouts  74.9 us
    psum x1, blocking collectives, body(): grad_filter = lax.psum(grad_terms, 'dp')  47 us
    all_to_all x2, starting transfers between devices, forward_rows(): lax.all_to_all(middle, 'seq', split_axis=4, concat_axis=3, tiled=True)  30 us
    all_to_all x2, local copies, waits for them, and re-layouts, inverse_rows(): lax.all_to_all(middle, 'seq', split_axis=4, concat_axis=3, tiled=True)  27.1 us
    all_to_all x2, local copies, waits for them, and re-layouts, forward_rows(): lax.all_to_all(middle, 'seq', split_axis=4, concat_axis=3, tiled=True)  26.9 us
    all_to_all x2, starting transfers between devices, inverse_rows(): lax.all_to_all(middle, 'seq', split_axis=4, concat_axis=3, tiled=True)  26.7 us
    slice x4, local copies, waits for them, and re-layouts, inverse_rows(): received[1]  23.8 us
    slice x4, local copies, waits for them, and re-layouts, forward_rows(): imaginary_received = received[1]  23.7 us
  transfers between devices with their start and end apart: 4, of which 2 were waited for; matrix products, arithmetic and copies ran while one was open for 31% of the time, Pallas kernels for 0%

commit v1 on v0

v1 whole, which is shorter than its diff:
```python
import math

import jax
import jax.numpy as jnp
import numpy as np
from jax import lax
from jax.experimental import pallas as pl
from jax.experimental.pallas import tpu as pltpu
from jax.sharding import PartitionSpec as P

N = 512
SEQ = 64
ROWS = N // SEQ
BF = jnp.bfloat16
F32 = jnp.float32
VMEM = pl.BlockSpec(memory_space=pltpu.VMEM)
SMEM = pl.BlockSpec(memory_space=pltpu.SMEM)


def unit_tables():
    steps = np.arange(N, dtype=np.int32)
    phases = (steps[:, None] * steps[None, :] % N).astype(np.float32) * np.float32(
        2.0 * math.pi / N
    )
    factor = np.float32(1.0 / math.sqrt(N))
    return (np.cos(phases) * factor).astype(BF), (-np.sin(phases) * factor).astype(BF)


def row_order():
    lane = np.arange(N)
    return 8 * (lane % 64) + 2 * (lane // 128) + (lane // 64) % 2


def first_table():
    cos_t, sin_t = unit_tables()
    order = row_order()
    return np.concatenate([cos_t[:, order], sin_t[:, order]], axis=1)


def selectors():
    lane = np.arange(256)
    row = 2 * (lane // 32 % 4) + lane // 128
    kind = lane // 16 % 2
    filt = lane // 2 % 8
    hit = (filt * 8 + row)[None, :] == np.arange(64)[:, None]
    expand = hit.astype(np.float32)
    signed = expand * np.where(kind == 1, -1.0, 1.0)[None, :]
    gather = expand * (kind == 0)[None, :]
    return (
        np.concatenate([expand, signed], axis=1).astype(BF),
        gather.astype(np.float32),
    )


def dot(a, b, dims=((1,), (0,)), precision=None):
    return lax.dot_general(a, b, (dims, ((), ())), precision=precision, preferred_element_type=F32)


def turn(idx_ref):
    shape = (ROWS, N)
    lane = lax.broadcasted_iota(jnp.int32, shape, 1)
    row = idx_ref[0] * ROWS + lax.broadcasted_iota(jnp.int32, shape, 0)
    col = 8 * (lane & 63) + 2 * (lane >> 7) + ((lane >> 6) & 1)
    phases = (row * col).astype(F32) * (-2.0 * math.pi / (N * N))
    return jnp.cos(phases), jnp.sin(phases)


def kernel_a(idx_ref, sig_ref, cot_ref, t_ref, out_ref, yre, yim, z):
    tc, ts = turn(idx_ref)
    for half, ref in enumerate((sig_ref, cot_ref)):
        x = ref[...]
        re = dot(x, t_ref[:, :N]).reshape(16, ROWS, N)
        im = dot(x, t_ref[:, N:]).reshape(16, ROWS, N)
        at = pl.ds(half * 128, 128)
        for y, v in ((yre, re * tc - im * ts), (yim, re * ts + im * tc)):
            v = v.reshape(128, N)
            for s in range(4):
                y[s, at, :] = v[:, s * 128 : (s + 1) * 128]
    for r in range(ROWS):
        for ri, y in enumerate((yre, yim)):
            rows = [y[s, pl.ds(r, 32, stride=ROWS), :] for s in range(4)]
            block = jnp.concatenate(rows, axis=0).T
            for p in range(2):
                z[ri * 2 + p, pl.ds(r, 64, stride=ROWS), :] = block[p * 64 : (p + 1) * 64]
    for k in range(4):
        out_ref[:, k * 128 : (k + 1) * 128] = z[k].astype(BF)


def kernel_f(f_ref, sel_ref, h_ref):
    for ri in range(2):
        cols = pl.ds(ri * 256, 256)
        h_ref[:, cols] = dot(f_ref[ri], sel_ref[:, cols], ((0,), (0,))).astype(BF)


def kernel_b(r_ref, wc_ref, ws_ref, h_ref, gather_ref, v_ref, g_ref, prod):
    for k in range(4):
        at = pl.ds(k * 128, 128)
        p1 = dot(wc_ref[at, :], r_ref[...])
        p2 = dot(ws_ref[at, :], r_ref[...])
        xre = p1[:, :256] - p2[:, 256:]
        xim = p1[:, 256:] + p2[:, :256]
        hre = h_ref[at, :256].astype(F32)
        him = h_ref[at, 256:].astype(F32)
        prod[at, :256] = (hre * xre - him * xim).astype(BF)
        prod[at, 256:] = (hre * xim + him * xre).astype(BF)
        cre = pltpu.roll(xre, 240, 1)
        cim = pltpu.roll(xim, 240, 1)
        for ri, g in enumerate((cre * xre + cim * xim, cim * xre - cre * xim)):
            g_ref[ri, :, at] = dot(
                gather_ref[...], g, ((1,), (1,)), lax.Precision.HIGHEST
            ).astype(BF)
    for k in range(4):
        at = pl.ds(k * 128, 128)
        q1 = dot(wc_ref[at, :], prod[...])
        q2 = dot(ws_ref[at, :], prod[...])
        v_ref[at, :256] = (q1[:, :256] + q2[:, 256:]).astype(BF)
        v_ref[at, 256:] = (q1[:, 256:] - q2[:, :256]).astype(BF)


def kernel_c(idx_ref, v_ref, t_ref, out_ref, grad_ref, z, yre, yim):
    for k in range(4):
        z[k] = v_ref[:, k * 128 : (k + 1) * 128].astype(F32)
    for r in range(ROWS):
        for ri, y in enumerate((yre, yim)):
            rows = [z[ri * 2 + p, pl.ds(r, 64, stride=ROWS), :] for p in range(2)]
            block = jnp.concatenate(rows, axis=0).T
            for s in range(4):
                y[s, pl.ds(r, 32, stride=ROWS), :] = block[s * 32 : (s + 1) * 32]
    tc, ts = turn(idx_ref)
    for half, ref in enumerate((out_ref, grad_ref)):
        at = pl.ds(half * 128, 128)
        re, im = (
            jnp.concatenate([y[s, at, :] for s in range(4)], axis=1).reshape(16, ROWS, N)
            for y in (yre, yim)
        )
        mid_re = (re * tc + im * ts).reshape(128, N).astype(BF)
        mid_im = (im * tc - re * ts).reshape(128, N).astype(BF)
        total = dot(mid_re, t_ref[:, :N], ((1,), (1,))) + dot(mid_im, t_ref[:, N:], ((1,), (1,)))
        ref[...] = total.astype(BF)


def body(signal, cotangent, filter_spec):
    shape = signal.shape
    place = lax.axis_index("seq").astype(jnp.int32).reshape(1)
    table = jnp.asarray(first_table())
    cos_t, sin_t = (jnp.asarray(t) for t in unit_tables())
    expand, gather = (jnp.asarray(t) for t in selectors())
    with jax.named_scope("kernel_a"):
        sent = pl.pallas_call(
            kernel_a,
            in_specs=[SMEM, VMEM, VMEM, VMEM],
            out_specs=VMEM,
            out_shape=jax.ShapeDtypeStruct((N, N), BF),
            scratch_shapes=[
                pltpu.VMEM((4, 256, 128), F32),
                pltpu.VMEM((4, 256, 128), F32),
                pltpu.VMEM((4, N, 128), F32),
            ],
        )(place, signal.reshape(128, N), cotangent.reshape(128, N), table)
    with jax.named_scope("first_exchange"):
        got = lax.all_to_all(sent.reshape(SEQ, ROWS, N), "seq", 0, 0, tiled=True).reshape(N, N)
    with jax.named_scope("kernel_f"):
        spread = pl.pallas_call(
            kernel_f,
            in_specs=[VMEM, VMEM],
            out_specs=VMEM,
            out_shape=jax.ShapeDtypeStruct((N, N), BF),
            cost_estimate=pl.CostEstimate(flops=67108864, bytes_accessed=720896, transcendentals=0),
        )(filter_spec.reshape(2, 64, N), expand)
    with jax.named_scope("kernel_b"):
        back, grad = pl.pallas_call(
            kernel_b,
            in_specs=[VMEM] * 5,
            out_specs=[VMEM, VMEM],
            out_shape=[
                jax.ShapeDtypeStruct((N, N), BF),
                jax.ShapeDtypeStruct((2, 64, N), BF),
            ],
            scratch_shapes=[pltpu.VMEM((N, N), BF)],
        )(got, cos_t, sin_t, spread, gather)
    with jax.named_scope("second_exchange"):
        mid = lax.all_to_all(back.reshape(SEQ, ROWS, N), "seq", 0, 0, tiled=True).reshape(N, N)
    for bit in (1, 2, 4):
        with jax.named_scope(f"grad_sum_{bit}"):
            other = lax.ppermute(grad, "dp", [(d, d ^ bit) for d in range(8)])
            grad = (grad.astype(F32) + other.astype(F32)).astype(BF)
    with jax.named_scope("kernel_c"):
        output, grad_signal = pl.pallas_call(
            kernel_c,
            in_specs=[SMEM, VMEM, VMEM],
            out_specs=[VMEM, VMEM],
            out_shape=[jax.ShapeDtypeStruct((128, N), BF)] * 2,
            scratch_shapes=[
                pltpu.VMEM((4, N, 128), F32),
                pltpu.VMEM((4, 256, 128), F32),
                pltpu.VMEM((4, 256, 128), F32),
            ],
        )(place, mid, table)
    return output.reshape(shape), grad_signal.reshape(shape), grad.reshape(2, 8, 8, N)


def solution(mesh):
    placed = (P(None, "dp", "seq", None), P(None, "dp", "seq", None), P(None, None, "seq", None))
    return jax.shard_map(
        body, mesh=mesh, in_specs=placed, out_specs=placed, check_vma=False
    )
```

time: 475 us -> 102 us (0.21)
  the two profiles are of different devices: /device:TPU:32 before, /device:TPU:1 now
where the time goes in v1:
time: 102 us
  waiting for transfers between devices  48.4 us (47%)
  starting transfers between devices  36.3 us (36%)
  Pallas kernels  14 us (14%)
  local copies, waits for them, and re-layouts  1.57 us (2%)
    all_to_all x1, waiting for transfers between devices, body(): lax.all_to_all(sent.reshape(SEQ, ROWS, N), 'seq', 0, 0, tiled=True)  29.8 us
    all_to_all x1, starting transfers between devices, body(): lax.all_to_all(sent.reshape(SEQ, ROWS, N), 'seq', 0, 0, tiled=True)  18.1 us
    ppermute x3, starting transfers between devices, body(): other = lax.ppermute(grad, 'dp', [(d, d ^ bit) for d in range(8)])  12.4 us
    all_to_all x1, waiting for transfers between devices, body(): lax.all_to_all(back.reshape(SEQ, ROWS, N), 'seq', 0, 0, tiled=True)  9.52 us
    ppermute x3, waiting for transfers between devices, body(): other = lax.ppermute(grad, 'dp', [(d, d ^ bit) for d in range(8)])  9.13 us
    all_to_all x1, starting transfers between devices, body(): lax.all_to_all(back.reshape(SEQ, ROWS, N), 'seq', 0, 0, tiled=True)  5.82 us
    pallas_call x1, Pallas kernels, body(): pl.pallas_call(kernel_b, in_specs=[VMEM] * 5, out_specs=[VMEM, VMEM], out...  5.64 us
    pallas_call x1, Pallas kernels, body(): pl.pallas_call(kernel_c, in_specs=[SMEM, VMEM, VMEM], out_specs=[VMEM, VM...  3.24 us
  transfers between devices with their start and end apart: 5, of which 5 were waited for; matrix products, arithmetic and copies ran while one was open for 1% of the time, Pallas kernels for 2%

profile of v1, /device:TPU:1, one launch (start us, length us, event | category | flops | bytes accessed | tf_op | source)
XLA Modules:
  0.0 101.7 jit_solution(7018310940506774051)
XLA Ops:
  0.6 3.1 %kernel_a.1 = bf16[512,512]{1,0:T(8,128)(2,1)} custom-call(s32[1]{0:T(128)} %bitcast.idx_ref, bf16[128,512]{1,0:T(8,128)(2,1)} %bitcast.17, bf16[128,512]{1,0:T(8,128)(2,1)} %bitcast.18, bf16[512,1024]{1,0:T(8,128)(2,1)} %constant.14.clone.t_ref), custom_call_target="tpu_custom_call" | custom-call | tf_op jit(solution)/shard_map/kernel_a/pallas_call | solution.py:149
  3.7 18.1 %all-to-all-start = ((bf16[64,8,512]{2,1,0:T(8,128)(2,1)}), bf16[64,8,512]{2,1,0:T(8,128)(2,1)S(1)}, u32[]{:S(2)}, u32[]{:S(2)}) async-start(bf16[64,8,512]{2,1,0:T(8,128)(2,1)} %bitcast.14), calls=%async_computation | async-start | bytes 1048576 | tf_op jit(solution)/shard_map/first_exchange/all_to_all | solution.py:161
  21.8 2.0 %kernel_f.1.h_ref = bf16[512,512]{1,0:T(8,128)(2,1)} custom-call(bf16[2,64,512]{2,1,0:T(8,128)(2,1)} %bitcast.16, bf16[64,512]{1,0:T(8,128)(2,1)} %constant.17.clone.sel_ref), custom_call_target="tpu_custom_call" | custom-call | flops 67108864 | bytes 720896 | tf_op jit(solution)/shard_map/kernel_f/pallas_call | solution.py:163
  23.8 29.8 %all-to-all-done = bf16[64,8,512]{2,1,0:T(8,128)(2,1)S(1)} async-done(((bf16[64,8,512]{2,1,0:T(8,128)(2,1)}), bf16[64,8,512]{2,1,0:T(8,128)(2,1)S(1)}, u32[]{:S(2)}, u32[]{:S(2)}) %all-to-all-start) | async-done | bytes 524320 | tf_op jit(solution)/shard_map/first_exchange/all_to_all | solution.py:161
  53.6 0.0 copy-start.1
  53.6 0.8 copy-done.1
  54.4 5.6 %kernel_b.1 = (bf16[512,512]{1,0:T(8,128)(2,1)}, bf16[2,64,512]{2,1,0:T(8,128)(2,1)}) custom-call(bf16[512,512]{1,0:T(8,128)(2,1)} %bitcast.13, bf16[512,512]{1,0:T(8,128)(2,1)} %constant.15.clone.wc_ref, bf16[512,512]{1,0:T(8,128)(2,1)} %constant.16.clone.ws_ref, bf16[512,512]{1,0:T(8,128)(2,1)} %kernel_f.1.h_ref, f32[64,256]{1,0:T(8,128)} %constant.18.clone.gather_ref), custom_call_target="tpu_custom_call" | custom-call | tf_op jit(solution)/shard_map/kernel_b/pallas_call | solution.py:171
  60.0 0.0 copy-start.2
  60.0 5.8 %all-to-all-start.1 = ((bf16[64,8,512]{2,1,0:T(8,128)(2,1)}), bf16[64,8,512]{2,1,0:T(8,128)(2,1)S(1)}, u32[]{:S(2)}, u32[]{:S(2)}) async-start(bf16[64,8,512]{2,1,0:T(8,128)(2,1)} %bitcast.15), calls=%async_computation.1 | async-start | bytes 1048576 | tf_op jit(solution)/shard_map/second_exchange/all_to_all | solution.py:182
  65.9 0.0 copy-done.2
  65.9 4.3 %collective-permute-start = (bf16[2,64,512]{2,1,0:T(8,128)(2,1)S(1)}, bf16[2,64,512]{2,1,0:T(8,128)(2,1)S(1)}, u32[]{:S(2)}, u32[]{:S(2)}) collective-permute-start(bf16[2,64,512]{2,1,0:T(8,128)(2,1)S(1)} %copy-done.2), channel_id=1, source_target_pairs={{0,64},{64,0},{128,192},{192,128},{256,320},{320,256},{384,448},{4... | collective-permute-start | bytes 393224 | tf_op jit(solution)/shard_map/grad_sum_1/ppermute | solution.py:185
  70.2 3.6 %collective-permute-done = bf16[2,64,512]{2,1,0:T(8,128)(2,1)S(1)} collective-permute-done((bf16[2,64,512]{2,1,0:T(8,128)(2,1)S(1)}, bf16[2,64,512]{2,1,0:T(8,128)(2,1)S(1)}, u32[]{:S(2)}, u32[]{:S(2)}) %collective-permute-start) | collective-permute-done | bytes 131104 | tf_op jit(solution)/shard_map/grad_sum_1/ppermute | solution.py:185
  73.9 3.2 %collective-permute-start.1 = (bf16[2,64,512]{2,1,0:T(8,128)(2,1)S(1)}, bf16[2,64,512]{2,1,0:T(8,128)(2,1)S(1)}, u32[]{:S(2)}, u32[]{:S(2)}) collective-permute-start(bf16[2,64,512]{2,1,0:T(8,128)(2,1)S(1)} %add_convert_fusion.2), channel_id=1, source_target_pairs={{0,128},{64,192},{128,0},{192,64},{256,384},{320,448},{384,256},{4... | collective-permute-start | bytes 393224 | tf_op jit(solution)/shard_map/grad_sum_2/ppermute | solution.py:185
  77.1 2.8 %collective-permute-done.1 = bf16[2,64,512]{2,1,0:T(8,128)(2,1)S(1)} collective-permute-done((bf16[2,64,512]{2,1,0:T(8,128)(2,1)S(1)}, bf16[2,64,512]{2,1,0:T(8,128)(2,1)S(1)}, u32[]{:S(2)}, u32[]{:S(2)}) %collective-permute-start.1) | collective-permute-done | bytes 131104 | tf_op jit(solution)/shard_map/grad_sum_2/ppermute | solution.py:185
  80.0 4.8 %collective-permute-start.2 = (bf16[2,64,512]{2,1,0:T(8,128)(2,1)S(1)}, bf16[2,64,512]{2,1,0:T(8,128)(2,1)S(1)}, u32[]{:S(2)}, u32[]{:S(2)}) collective-permute-start(bf16[2,64,512]{2,1,0:T(8,128)(2,1)S(1)} %add_convert_fusion.1), channel_id=1, source_target_pairs={{0,256},{64,320},{128,384},{192,448},{256,0},{320,64},{384,128},{4... | collective-permute-start | bytes 393224 | tf_op jit(solution)/shard_map/grad_sum_4/ppermute | solution.py:185
  84.8 2.7 %collective-permute-done.2 = bf16[2,64,512]{2,1,0:T(8,128)(2,1)S(1)} collective-permute-done((bf16[2,64,512]{2,1,0:T(8,128)(2,1)S(1)}, bf16[2,64,512]{2,1,0:T(8,128)(2,1)S(1)}, u32[]{:S(2)}, u32[]{:S(2)}) %collective-permute-start.2) | collective-permute-done | bytes 131104 | tf_op jit(solution)/shard_map/grad_sum_4/ppermute | solution.py:185
  87.5 0.7 fusion
  88.2 9.5 %all-to-all-done.1 = bf16[64,8,512]{2,1,0:T(8,128)(2,1)S(1)} async-done(((bf16[64,8,512]{2,1,0:T(8,128)(2,1)}), bf16[64,8,512]{2,1,0:T(8,128)(2,1)S(1)}, u32[]{:S(2)}, u32[]{:S(2)}) %all-to-all-start.1) | async-done | bytes 524320 | tf_op jit(solution)/shard_map/second_exchange/all_to_all | solution.py:182
  97.7 0.0 copy-start
  97.7 0.8 copy-done
  98.5 3.2 %kernel_c.1 = (bf16[128,512]{1,0:T(8,128)(2,1)}, bf16[128,512]{1,0:T(8,128)(2,1)}) custom-call(s32[1]{0:T(128)} %bitcast.idx_ref, bf16[512,512]{1,0:T(8,128)(2,1)} %bitcast.12, bf16[512,1024]{1,0:T(8,128)(2,1)} %constant.14.clone.t_ref), custom_call_target="tpu_custom_call" | custom-call | tf_op jit(solution)/shard_map/kernel_c/pallas_call | solution.py:188
  (2 shorter events, 0.1 us)
Async XLA Ops:
  3.7 49.9 %all-to-all-start = ((bf16[64,8,512]{2,1,0:T(8,128)(2,1)}), bf16[64,8,512]{2,1,0:T(8,128)(2,1)S(1)}, u32[]{:S(2)}, u32[]{:S(2)}) async-start(bf16[64,8,512]{2,1,0:T(8,128)(2,1)} %bitcast.14), calls=%async_computation | async-start | bytes 1048576 | tf_op jit(solution)/shard_map/first_exchange/all_to_all | solution.py:161
  53.6 0.8 copy-start.1
  60.0 5.8 %copy-start.2 = (bf16[2,64,512]{2,1,0:T(8,128)(2,1)S(1)}, bf16[2,64,512]{2,1,0:T(8,128)(2,1)}, u32[]{:S(2)}) copy-start(bf16[2,64,512]{2,1,0:T(8,128)(2,1)} %get-tuple-element.10) | copy-start | bytes 393220
  60.0 37.6 %all-to-all-start.1 = ((bf16[64,8,512]{2,1,0:T(8,128)(2,1)}), bf16[64,8,512]{2,1,0:T(8,128)(2,1)S(1)}, u32[]{:S(2)}, u32[]{:S(2)}) async-start(bf16[64,8,512]{2,1,0:T(8,128)(2,1)} %bitcast.15), calls=%async_computation.1 | async-start | bytes 1048576 | tf_op jit(solution)/shard_map/second_exchange/all_to_all | solution.py:182
  65.9 8.0 %collective-permute-start = (bf16[2,64,512]{2,1,0:T(8,128)(2,1)S(1)}, bf16[2,64,512]{2,1,0:T(8,128)(2,1)S(1)}, u32[]{:S(2)}, u32[]{:S(2)}) collective-permute-start(bf16[2,64,512]{2,1,0:T(8,128)(2,1)S(1)} %copy-done.2), channel_id=1, source_target_pairs={{0,64},{64,0},{128,192},{192,128},{256,320},{320,256},{384,448},{4... | collective-permute-start | bytes 393224 | tf_op jit(solution)/shard_map/grad_sum_1/ppermute | solution.py:185
  73.9 6.0 %collective-permute-start.1 = (bf16[2,64,512]{2,1,0:T(8,128)(2,1)S(1)}, bf16[2,64,512]{2,1,0:T(8,128)(2,1)S(1)}, u32[]{:S(2)}, u32[]{:S(2)}) collective-permute-start(bf16[2,64,512]{2,1,0:T(8,128)(2,1)S(1)} %add_convert_fusion.2), channel_id=1, source_target_pairs={{0,128},{64,192},{128,0},{192,64},{256,384},{320,448},{384,256},{4... | collective-permute-start | bytes 393224 | tf_op jit(solution)/shard_map/grad_sum_2/ppermute | solution.py:185
  80.0 7.5 %collective-permute-start.2 = (bf16[2,64,512]{2,1,0:T(8,128)(2,1)S(1)}, bf16[2,64,512]{2,1,0:T(8,128)(2,1)S(1)}, u32[]{:S(2)}, u32[]{:S(2)}) collective-permute-start(bf16[2,64,512]{2,1,0:T(8,128)(2,1)S(1)} %add_convert_fusion.1), channel_id=1, source_target_pairs={{0,256},{64,320},{128,384},{192,448},{256,0},{320,64},{384,128},{4... | collective-permute-start | bytes 393224 | tf_op jit(solution)/shard_map/grad_sum_4/ppermute | solution.py:185
  97.7 0.8 copy-start

commit v2 on v1

v2 whole, which is shorter than its diff:
```python
import math

import jax
import jax.numpy as jnp
import numpy as np
from jax import lax
from jax.experimental import pallas as pl
from jax.experimental.pallas import tpu as pltpu
from jax.sharding import PartitionSpec as P

N = 512
SEQ = 64
ROWS = N // SEQ
HALF = N // 2
BF = jnp.bfloat16
F32 = jnp.float32
VMEM = pl.BlockSpec(memory_space=pltpu.VMEM)
SMEM = pl.BlockSpec(memory_space=pltpu.SMEM)
PARAMS = pltpu.CompilerParams(vmem_limit_bytes=20 * 2**20)


def unit_tables():
    steps = np.arange(N, dtype=np.int32)
    phases = (steps[:, None] * steps[None, :] % N).astype(np.float32) * np.float32(
        2.0 * math.pi / N
    )
    factor = np.float32(1.0 / math.sqrt(N))
    return (np.cos(phases) * factor).astype(BF), (-np.sin(phases) * factor).astype(BF)


def first_table():
    cos_t, sin_t = unit_tables()
    col = np.arange(HALF)
    place = col % 64
    row = 8 * place + 2 * (col // 128) + col // 64 % 2 + (place >= 32)
    re, im = cos_t[:, row], sin_t[:, row]
    im[:, 0] = cos_t[:, HALF]
    return np.concatenate([re, im], axis=1)


def lanes():
    lane = np.arange(HALF)
    slot = 2 * (lane // 32 % 2) + lane // 128
    return slot, lane // 64 % 2, lane // 16 % 2, lane // 2 % 8, lane % 2


def filter_selectors():
    slot, _, _, filt, chan = lanes()
    own = np.zeros((3, 112, HALF), np.float32)
    mirror = np.zeros((3, 112, HALF), np.float32)
    for lane in range(HALF):
        k, f = slot[lane], filt[lane]
        for kind in (0, 1):
            own[kind, f * 8 + k, lane] = 0.5
            mirror[kind, 96 + f if k == 0 else 64 + f * 4 + 4 - k, lane] = 0.5
        own[2, f * 8 + k + 1, lane] = 0.5
        mirror[2, 64 + f * 4 + 3 - k, lane] = 0.5
        if k == 0:
            own[0, :, lane] = 0
            mirror[0, :, lane] = 0
            source = 96 + f if chan[lane] else f * 8
            own[0, source, lane] = 0.5
            mirror[0, source, lane] = 0.5
    return own.astype(BF), mirror.astype(BF)


def gather_tables():
    slot, part, kind, filt, chan = lanes()
    out = np.zeros((2, 2, 48, HALF), np.float32)
    for lane in range(HALF):
        if kind[lane]:
            continue
        for first in range(2):
            for ri in range(2):
                sign = -1.0 if ri and part[lane] else 1.0
                extra = slot[lane] == 0 and chan[lane] == 1
                if not (first and extra):
                    out[first, ri, slot[lane] * 8 + filt[lane], lane] = sign
                if extra:
                    out[first, ri, 32 + filt[lane], lane] = sign
    return out


def grad_selectors():
    own = np.zeros((4, 64, 112), np.float32)
    mirror = np.zeros((4, 64, 112), np.float32)
    for f in range(8):
        for row in range(8):
            at = f * 8 + row
            for kind in (0, 1):
                if row < 4:
                    own[kind, at, row * 8 + f] = 1
                else:
                    mirror[kind, at, 48 + (7 - row) * 8 + f] = 1
            for kind in (2, 3):
                if row == 0:
                    mirror[kind, at, 96 + f] = 1
                elif row < 5:
                    own[kind, at, (row - 1) * 8 + f] = 1
                else:
                    mirror[kind, at, 48 + (8 - row) * 8 + f] = 1
        own[0, f * 8, f] = 0.5
        mirror[0, f * 8, f] = 0.5
        own[3, f * 8, 96 + f] = 0.5
        mirror[3, f * 8, 96 + f] = 0.5
    return own.astype(BF), mirror.astype(BF)


def payload_selectors():
    tail = np.zeros((32, 64), np.float32)
    head = np.zeros((8, 64), np.float32)
    for f in range(8):
        head[f, f * 8] = 1
        for row in range(4):
            tail[f * 4 + row, f * 8 + 4 + row] = 1
    return tail.astype(BF), head.astype(BF)


def dot(a, b, dims=((1,), (0,)), precision=None):
    return lax.dot_general(a, b, (dims, ((), ())), precision=precision, preferred_element_type=F32)


def turn(idx_ref, chan):
    shape = (ROWS, HALF)
    lane = lax.broadcasted_iota(jnp.int32, shape, 1)
    row = idx_ref[0] * ROWS + lax.broadcasted_iota(jnp.int32, shape, 0)
    place = lane & 63
    col = 8 * place + 2 * (lane >> 7) + ((lane >> 6) & 1) + (place >> 5)
    if chan:
        col = jnp.where(lane == 0, HALF, col)
    phases = (row * col).astype(F32) * (-2.0 * math.pi / (N * N))
    return jnp.cos(phases), jnp.sin(phases)


def swap_first(re, im):
    first = lax.broadcasted_iota(jnp.int32, re[0].shape, 2) == 0
    return (re[0], jnp.where(first, im[0], re[1])), (jnp.where(first, re[1], im[0]), im[1])


def kernel_a(idx_ref, sig_ref, cot_ref, t_ref, f_ref, tail_ref, head_ref, out_ref, tails_ref,
             heads_ref, yre, yim, z):
    for ri in range(2):
        tails_ref[ri] = dot(tail_ref[...], f_ref[ri]).astype(BF)
        heads_ref[ri] = dot(head_ref[...], f_ref[ri]).astype(BF)
    turns = [turn(idx_ref, chan) for chan in range(2)]
    for half, ref in enumerate((sig_ref, cot_ref)):
        x = ref[...]
        re = dot(x, t_ref[:, :HALF]).reshape(8, 2, ROWS, HALF)
        im = dot(x, t_ref[:, HALF:]).reshape(8, 2, ROWS, HALF)
        re, im = swap_first((re[:, 0], re[:, 1]), (im[:, 0], im[:, 1]))
        at = pl.ds(half * 128, 128)
        out_re = [re[c] * turns[c][0] - im[c] * turns[c][1] for c in range(2)]
        out_im = [re[c] * turns[c][1] + im[c] * turns[c][0] for c in range(2)]
        for y, v in ((yre, out_re), (yim, out_im)):
            v = jnp.stack(v, axis=1).reshape(128, HALF)
            for s in range(2):
                y[s, at, :] = v[:, s * 128 : (s + 1) * 128]
    for r in range(ROWS):
        rows = [y[s, pl.ds(r, 32, stride=ROWS), :] for y in (yre, yim) for s in range(2)]
        block = jnp.concatenate(rows, axis=0).T
        for p in range(2):
            z[p, pl.ds(r, 64, stride=ROWS), :] = block[p * 64 : (p + 1) * 64]
    for p in range(2):
        out_ref[:, p * 128 : (p + 1) * 128] = z[p].astype(BF)


def kernel_f(idx_ref, f_ref, tail_ref, head_ref, own_ref, mirror_ref, flip_ref, h_ref, rows):
    place = idx_ref[0]
    kind = jnp.where(place == 0, 0, jnp.where(place < 32, 1, 2))
    rows[:, :64, :] = f_ref[...]
    rows[:, 64:96, :] = tail_ref[...]
    rows[:, 96:, :] = jnp.zeros((2, 16, N), BF)
    rows[:, 96:104, :] = head_ref[...]
    lane = lax.broadcasted_iota(jnp.int32, (N, HALF), 1)
    shifted = ((lane & ~30) == 0) | ((lane & ~30) == 64)
    shifted = shifted & (place == 0)
    negative = ((lane >> 6) & 1) == ((lane >> 4) & 1)
    for ri in range(2):
        near = dot(rows[ri], own_ref[kind], ((0,), (0,)))
        far = dot(rows[ri], mirror_ref[kind], ((0,), (0,))).astype(BF)
        far = dot(flip_ref[...], far)
        far = jnp.where(shifted, pltpu.roll(far, 1, 0), far)
        if ri == 0:
            h_ref[:, :HALF] = near + far
        else:
            value = near - far
            h_ref[:, HALF:] = jnp.where(negative, -value, value)


def kernel_b(idx_ref, r_ref, wc_ref, ws_ref, h_ref, gather_ref, v_ref, g_ref, prod):
    first = jnp.where(idx_ref[0] == 0, 1, 0)
    sign = jnp.where(lax.broadcasted_iota(jnp.int32, (128, 128), 1) < 64, -1.0, 1.0)
    for k in range(4):
        at = pl.ds(k * 128, 128)
        p1 = dot(wc_ref[at, :], r_ref[...])
        p2 = dot(ws_ref[at, :], r_ref[...])
        pairs = []
        for p in range(2):
            cols = slice(p * 128, (p + 1) * 128)
            x = p1[:, cols] + sign * pltpu.roll(p2[:, cols], 64, 1)
            swapped = pltpu.roll(x, 64, 1)
            h1 = h_ref[at, p * 128 : (p + 1) * 128]
            h2 = h_ref[at, HALF + p * 128 : HALF + (p + 1) * 128]
            prod[at, cols] = (h1 * x + h2 * swapped).astype(BF)
            pairs.append((pltpu.roll(x, 112, 1) * x, pltpu.roll(x, 48, 1) * x))
        for ri in range(2):
            terms = jnp.concatenate([pairs[0][ri], pairs[1][ri]], axis=1)
            g_ref[ri, :, at] = dot(
                gather_ref[first, ri], terms, ((1,), (1,)), lax.Precision.HIGHEST
            ).astype(BF)
    for k in range(4):
        at = pl.ds(k * 128, 128)
        q1 = dot(wc_ref[at, :], prod[...])
        q2 = dot(ws_ref[at, :], prod[...])
        for p in range(2):
            cols = slice(p * 128, (p + 1) * 128)
            v_ref[at, cols] = (q1[:, cols] - sign * pltpu.roll(q2[:, cols], 64, 1)).astype(BF)


def kernel_c(idx_ref, v_ref, t_ref, out_ref, grad_ref, z, yre, yim):
    for p in range(2):
        z[p] = v_ref[:, p * 128 : (p + 1) * 128].astype(F32)
    for r in range(ROWS):
        rows = [z[p, pl.ds(r, 64, stride=ROWS), :] for p in range(2)]
        block = jnp.concatenate(rows, axis=0).T
        for ri, y in enumerate((yre, yim)):
            for s in range(2):
                at = ri * 64 + s * 32
                y[s, pl.ds(r, 32, stride=ROWS), :] = block[at : at + 32]
    double = jnp.where(lax.broadcasted_iota(jnp.int32, (ROWS, HALF), 1) == 0, 1.0, 2.0)
    turns = [[t * double for t in turn(idx_ref, chan)] for chan in range(2)]
    for half, ref in enumerate((out_ref, grad_ref)):
        at = pl.ds(half * 128, 128)
        re, im = (
            jnp.concatenate([y[s, at, :] for s in range(2)], axis=1).reshape(8, 2, ROWS, HALF)
            for y in (yre, yim)
        )
        mid_re = [re[:, c] * turns[c][0] + im[:, c] * turns[c][1] for c in range(2)]
        mid_im = [im[:, c] * turns[c][0] - re[:, c] * turns[c][1] for c in range(2)]
        mid_re, mid_im = (
            jnp.stack(v, axis=1).reshape(128, HALF).astype(BF) for v in swap_first(mid_re, mid_im)
        )
        total = dot(mid_re, t_ref[:, :HALF], ((1,), (1,)))
        total = total + dot(mid_im, t_ref[:, HALF:], ((1,), (1,)))
        ref[...] = total.astype(BF)


def kernel_g(idx_ref, g0_ref, g1_ref, far0_ref, far1_ref, head0_ref, head1_ref, own_ref,
             mirror_ref, flip_ref, out_ref, rows):
    place = idx_ref[0]
    kind = jnp.where(
        place == 0, 0, jnp.where(place == 32, 3, jnp.where(place < 32, 1, 2))
    )
    sources = ((g0_ref, far0_ref, head0_ref), (g1_ref, far1_ref, head1_ref))
    for k, (g_ref, far_ref, head_ref) in enumerate(sources):
        rows[k, :, :48, :] = g_ref[...]
        rows[k, :, 48:96, :] = far_ref[...]
        rows[k, :, 96:, :] = jnp.zeros((2, 16, N), BF)
        rows[k, :, 96:104, :] = head_ref[...]
    row = lax.broadcasted_iota(jnp.int32, (64, N), 0)
    shifted = ((row & 7) == 0) & (place == 0)
    for ri in range(2):
        near = dot(own_ref[kind], rows[0, ri]) + dot(own_ref[kind], rows[1, ri])
        far = [
            dot(dot(mirror_ref[kind], rows[k, ri]).astype(BF), flip_ref[...]) for k in range(2)
        ]
        far = far[0] + far[1]
        far = jnp.where(shifted, pltpu.roll(far, 1, 1), far)
        out_ref[ri] = (near + far if ri == 0 else near - far).astype(BF)


def across(moves):
    return [(d * SEQ + a, (d ^ 1) * SEQ + b) for d in range(8) for a, b in moves]


def body(signal, cotangent, filter_spec):
    shape = signal.shape
    place = lax.axis_index("seq").astype(jnp.int32).reshape(1)
    table = jnp.asarray(first_table())
    cos_t, sin_t = (jnp.asarray(t) for t in unit_tables())
    flip = jnp.asarray(np.eye(N, dtype=np.float32)[::-1].astype(BF))
    tail, head = (jnp.asarray(t) for t in payload_selectors())
    f_own, f_mirror = (jnp.asarray(t) for t in filter_selectors())
    g_own, g_mirror = (jnp.asarray(t) for t in grad_selectors())
    gather = jnp.asarray(gather_tables())
    opposite = [(d, SEQ - 1 - d) for d in range(SEQ)]
    heads_to = [(d, {0: 32, 32: 0}.get(d, SEQ - d)) for d in range(SEQ)]
    filt = filter_spec.reshape(2, 64, N)
    with jax.named_scope("kernel_a"):
        sent, tails, heads = pl.pallas_call(
            kernel_a,
            in_specs=[SMEM] + [VMEM] * 6,
            out_specs=[VMEM] * 3,
            out_shape=[
                jax.ShapeDtypeStruct((N, HALF), BF),
                jax.ShapeDtypeStruct((2, 32, N), BF),
                jax.ShapeDtypeStruct((2, 8, N), BF),
            ],
            scratch_shapes=[
                pltpu.VMEM((2, 256, 128), F32),
                pltpu.VMEM((2, 256, 128), F32),
                pltpu.VMEM((2, N, 128), F32),
            ],
        )(place, signal.reshape(128, N), cotangent.reshape(128, N), table, filt, tail, head)
    with jax.named_scope("first_exchange"):
        got = lax.all_to_all(sent.reshape(SEQ, ROWS, HALF), "seq", 0, 0, tiled=True)
    with jax.named_scope("filter_mirror"):
        tails = lax.ppermute(tails, "seq", opposite)
        heads = lax.ppermute(heads, "seq", heads_to)
    with jax.named_scope("kernel_f"):
        spread = pl.pallas_call(
            kernel_f,
            in_specs=[SMEM] + [VMEM] * 6,
            out_specs=VMEM,
            out_shape=jax.ShapeDtypeStruct((N, N), F32),
            scratch_shapes=[pltpu.VMEM((2, 112, N), BF)],
            compiler_params=PARAMS,
            cost_estimate=pl.CostEstimate(
                flops=400000000, bytes_accessed=2000000, transcendentals=0
            ),
        )(place, filt, tails, heads, f_own, f_mirror, flip)
    with jax.named_scope("kernel_b"):
        back, grad = pl.pallas_call(
            kernel_b,
            in_specs=[SMEM] + [VMEM] * 5,
            out_specs=[VMEM, VMEM],
            out_shape=[
                jax.ShapeDtypeStruct((N, HALF), BF),
                jax.ShapeDtypeStruct((2, 48, N), BF),
            ],
            scratch_shapes=[pltpu.VMEM((N, HALF), BF)],
            compiler_params=PARAMS,
        )(place, got.reshape(N, HALF), cos_t, sin_t, spread, gather)
    with jax.named_scope("second_exchange"):
        mid = lax.all_to_all(back.reshape(SEQ, ROWS, HALF), "seq", 0, 0, tiled=True)
    with jax.named_scope("grad_sum"):
        parts = [lax.ppermute(grad, "dp", [(d, d ^ bit) for d in range(8)]) for bit in (2, 4, 6)]
        wide = [v.astype(F32) for v in [grad] + parts]
        grad = ((wide[0] + wide[1]) + (wide[2] + wide[3])).astype(BF)
    with jax.named_scope("grad_mirror"):
        slot = jnp.where(place[0] == 0, grad[:, 32:40], grad[:, :8])
        both = ("dp", "seq")
        far0 = lax.ppermute(grad, "seq", opposite)
        far1 = lax.ppermute(grad, both, across(opposite))
        slot0 = lax.ppermute(slot, "seq", heads_to)
        slot1 = lax.ppermute(slot, both, across(heads_to))
        grad1 = lax.ppermute(grad, "dp", [(d, d ^ 1) for d in range(8)])
    with jax.named_scope("kernel_c"):
        output, grad_signal = pl.pallas_call(
            kernel_c,
            in_specs=[SMEM, VMEM, VMEM],
            out_specs=[VMEM, VMEM],
            out_shape=[jax.ShapeDtypeStruct((128, N), BF)] * 2,
            scratch_shapes=[
                pltpu.VMEM((2, N, 128), F32),
                pltpu.VMEM((2, 256, 128), F32),
                pltpu.VMEM((2, 256, 128), F32),
            ],
            compiler_params=PARAMS,
            cost_estimate=pl.CostEstimate(
                flops=400000000, bytes_accessed=2000000, transcendentals=0
            ),
        )(place, mid.reshape(N, HALF), table)
    with jax.named_scope("kernel_g"):
        grad_filter = pl.pallas_call(
            kernel_g,
            in_specs=[SMEM] + [VMEM] * 9,
            out_specs=VMEM,
            out_shape=jax.ShapeDtypeStruct((2, 64, N), BF),
            scratch_shapes=[pltpu.VMEM((2, 2, 112, N), BF)],
            compiler_params=PARAMS,
            cost_estimate=pl.CostEstimate(
                flops=100000000, bytes_accessed=1000000, transcendentals=0
            ),
        )(place, grad, grad1, far0, far1, slot0, slot1, g_own, g_mirror, flip)
    return output.reshape(shape), grad_signal.reshape(shape), grad_filter.reshape(2, 8, 8, N)


def solution(mesh):
    placed = (P(None, "dp", "seq", None), P(None, "dp", "seq", None), P(None, None, "seq", None))
    return jax.shard_map(
        body, mesh=mesh, in_specs=placed, out_specs=placed, check_vma=False
    )
```

time: 102 us -> 119 us (1.17)
  the two profiles are of different devices: /device:TPU:1 before, /device:TPU:128 now
where the time goes in v2:
time: 119 us; the launch traced here: 118 us
  starting transfers between devices  82.7 us (69%)
  waiting for transfers between devices  24.1 us (20%)
  Pallas kernels  10.2 us (9%)
    all_to_all x1, starting transfers between devices, body(): got = lax.all_to_all(sent.reshape(SEQ, ROWS, HALF), 'seq', 0, 0, tiled=True)  15.5 us
    ppermute x3, starting transfers between devices, body(): lax.ppermute(grad, 'dp', [(d, d ^ bit) for d in range(8)])  10.4 us
    ppermute x1, waiting for transfers between devices, body(): heads = lax.ppermute(heads, 'seq', heads_to)  10.3 us
    all_to_all x1, starting transfers between devices, body(): mid = lax.all_to_all(back.reshape(SEQ, ROWS, HALF), 'seq', 0, 0, tiled=True)  9.7 us
    ppermute x1, starting transfers between devices, body(): slot0 = lax.ppermute(slot, 'seq', heads_to)  8.57 us
    ppermute x1, starting transfers between devices, body(): slot1 = lax.ppermute(slot, both, across(heads_to))  8.28 us
    ppermute x1, waiting for transfers between devices, body(): slot1 = lax.ppermute(slot, both, across(heads_to))  8.16 us
    ppermute x1, starting transfers between devices, body(): tails = lax.ppermute(tails, 'seq', opposite)  8.15 us
  transfers between devices with their start and end apart: 12, of which 4 were waited for; matrix products, arithmetic and copies ran while one was open for 0% of the time, Pallas kernels for 2%

profile of v2, /device:TPU:128, one launch (start us, length us, event | category | flops | bytes accessed | tf_op | source)
XLA Modules:
  0.0 118.0 jit_solution(6483642450738742908)
XLA Ops:
  0.6 0.0 copy-start
  0.6 2.6 %kernel_a.1 = (bf16[512,256]{1,0:T(8,128)(2,1)}, bf16[2,32,512]{2,1,0:T(8,128)(2,1)}, bf16[2,8,512]{2,1,0:T(8,128)(2,1)}) custom-call(s32[1]{0:T(128)} %bitcast.idx_ref, bf16[128,512]{1,0:T(8,128)(2,1)} %bitcast.16, bf16[128,512]{1,0:T(8,128)(2,1)} %bitcast.17, bf16[512,512]{1,0:T(8,128)(2,1)} %constant.28.clone.t_ref, bf16[2,64,512]{2,1,0:T(8,128)(2,1)} %bitcast.12, ...), custom_call_target="tpu_custom_call" | custom-call | tf_op jit(solution)/shard_map/kernel_a/pallas_call | solution.py:290
  3.3 0.0 copy-start.7
  3.3 15.5 %all-to-all-start = ((bf16[64,8,256]{2,1,0:T(8,128)(2,1)}), bf16[64,8,256]{2,1,0:T(8,128)(2,1)S(1)}, u32[]{:S(2)}, u32[]{:S(2)}) async-start(bf16[64,8,256]{2,1,0:T(8,128)(2,1)} %bitcast.15), calls=%async_computation | async-start | bytes 524288 | tf_op jit(solution)/shard_map/first_exchange/all_to_all | solution.py:306
  18.7 8.2 %collective-permute-start = (bf16[2,32,512]{2,1,0:T(8,128)(2,1)}, bf16[2,32,512]{2,1,0:T(8,128)(2,1)S(1)}, u32[]{:S(2)}, u32[]{:S(2)}) collective-permute-start(bf16[2,32,512]{2,1,0:T(8,128)(2,1)} %get-tuple-element.11), channel_id=1, source_target_pairs={{0,63},{1,62},{2,61},{3,60},{4,59},{5,58},{6,57},{7,56},{8,55},{9,... | collective-permute-start | bytes 196616 | tf_op jit(solution)/shard_map/filter_mirror/ppermute | solution.py:308
  26.9 0.0 copy-start.3
  26.9 0.0 copy-start.4
  26.9 0.0 copy-start.5
  26.9 5.0 %collective-permute-start.1 = (bf16[2,8,512]{2,1,0:T(8,128)(2,1)S(1)}, bf16[2,8,512]{2,1,0:T(8,128)(2,1)S(1)}, u32[]{:S(2)}, u32[]{:S(2)}) collective-permute-start(bf16[2,8,512]{2,1,0:T(8,128)(2,1)S(1)} %copy-done.10), channel_id=1, source_target_pairs={{0,32},{1,63},{2,62},{3,61},{4,60},{5,59},{6,58},{7,57},{8,56},{9,... | collective-permute-start | bytes 49160 | tf_op jit(solution)/shard_map/filter_mirror/ppermute | solution.py:309
  32.0 10.3 %collective-permute-done.1.head_ref = bf16[2,8,512]{2,1,0:T(8,128)(2,1)S(1)} collective-permute-done((bf16[2,8,512]{2,1,0:T(8,128)(2,1)S(1)}, bf16[2,8,512]{2,1,0:T(8,128)(2,1)S(1)}, u32[]{:S(2)}, u32[]{:S(2)}) %collective-permute-start.1) | collective-permute-done | bytes 16416 | tf_op jit(solution)/shard_map/filter_mirror/ppermute | solution.py:309
  42.3 0.0 collective-permute-done.tail_ref
  42.4 1.1 kernel_f.1.h_ref
  43.5 0.0 all-to-all-done
  43.5 3.6 %kernel_b.1 = (bf16[512,256]{1,0:T(8,128)(2,1)}, bf16[2,48,512]{2,1,0:T(8,128)(2,1)S(1)}) custom-call(s32[1]{0:T(128)} %bitcast.idx_ref, bf16[512,256]{1,0:T(8,128)(2,1)S(1)} %bitcast.11, bf16[512,512]{1,0:T(8,128)(2,1)S(1)} %copy-done.3, bf16[512,512]{1,0:T(8,128)(2,1)S(1)} %copy-done.4, f32[512,512]{1,0:T(8,128)S(1)} %kernel_f.1.h_ref, ...), custom_call_target="tpu_custom_call" | custom-call | tf_op jit(solution)/shard_map/kernel_b/pallas_call | solution.py:323
  47.1 9.7 %all-to-all-start.1 = ((bf16[64,8,256]{2,1,0:T(8,128)(2,1)}), bf16[64,8,256]{2,1,0:T(8,128)(2,1)S(1)}, u32[]{:S(2)}, u32[]{:S(2)}) async-start(bf16[64,8,256]{2,1,0:T(8,128)(2,1)} %bitcast.6), calls=%async_computation.1 | async-start | bytes 524288 | tf_op jit(solution)/shard_map/second_exchange/all_to_all | solution.py:335
  56.8 3.5 %collective-permute-start.2 = (bf16[2,48,512]{2,1,0:T(8,128)(2,1)S(1)}, bf16[2,48,512]{2,1,0:T(8,128)(2,1)S(1)}, u32[]{:S(2)}, u32[]{:S(2)}) collective-permute-start(bf16[2,48,512]{2,1,0:T(8,128)(2,1)S(1)} %get-tuple-element.16), channel_id=1, source_target_pairs={{0,128},{64,192},{128,0},{192,64},{256,384},{320,448},{384,256},{4... | collective-permute-start | bytes 294920 | tf_op jit(solution)/shard_map/grad_sum/ppermute | solution.py:337
  60.3 4.8 %collective-permute-start.3 = (bf16[2,48,512]{2,1,0:T(8,128)(2,1)S(1)}, bf16[2,48,512]{2,1,0:T(8,128)(2,1)S(1)}, u32[]{:S(2)}, u32[]{:S(2)}) collective-permute-start(bf16[2,48,512]{2,1,0:T(8,128)(2,1)S(1)} %get-tuple-element.16), channel_id=1, source_target_pairs={{0,256},{64,320},{128,384},{192,448},{256,0},{320,64},{384,128},{4... | collective-permute-start | bytes 294920 | tf_op jit(solution)/shard_map/grad_sum/ppermute | solution.py:337
  65.1 2.1 %collective-permute-start.4 = (bf16[2,48,512]{2,1,0:T(8,128)(2,1)S(1)}, bf16[2,48,512]{2,1,0:T(8,128)(2,1)S(1)}, u32[]{:S(2)}, u32[]{:S(2)}) collective-permute-start(bf16[2,48,512]{2,1,0:T(8,128)(2,1)S(1)} %get-tuple-element.16), channel_id=1, source_target_pairs={{0,384},{64,448},{128,256},{192,320},{256,128},{320,192},{384,0},{... | collective-permute-start | bytes 294920 | tf_op jit(solution)/shard_map/grad_sum/ppermute | solution.py:337
  67.3 0.0 collective-permute-done.2
  67.3 1.0 collective-permute-done.3
  68.3 4.5 %collective-permute-done.4 = bf16[2,48,512]{2,1,0:T(8,128)(2,1)S(1)} collective-permute-done((bf16[2,48,512]{2,1,0:T(8,128)(2,1)S(1)}, bf16[2,48,512]{2,1,0:T(8,128)(2,1)S(1)}, u32[]{:S(2)}, u32[]{:S(2)}) %collective-permute-start.4) | collective-permute-done | bytes 98336 | tf_op jit(solution)/shard_map/grad_sum/ppermute | solution.py:337
  72.9 0.1 add_convert_fusion.g0_ref
  72.9 4.6 %collective-permute-start.5 = (bf16[2,48,512]{2,1,0:T(8,128)(2,1)S(1)}, bf16[2,48,512]{2,1,0:T(8,128)(2,1)S(1)}, u32[]{:S(2)}, u32[]{:S(2)}) collective-permute-start(bf16[2,48,512]{2,1,0:T(8,128)(2,1)S(1)} %add_convert_fusion.g0_ref), channel_id=1, source_target_pairs={{0,64},{64,0},{128,192},{192,128},{256,320},{320,256},{384,448},{4... | collective-permute-start | bytes 294920 | tf_op jit(solution)/shard_map/grad_mirror/ppermute | solution.py:347
  77.6 5.9 %collective-permute-start.6 = (bf16[2,48,512]{2,1,0:T(8,128)(2,1)S(1)}, bf16[2,48,512]{2,1,0:T(8,128)(2,1)S(1)}, u32[]{:S(2)}, u32[]{:S(2)}) collective-permute-start(bf16[2,48,512]{2,1,0:T(8,128)(2,1)S(1)} %add_convert_fusion.g0_ref), channel_id=1, source_target_pairs={{0,63},{1,62},{2,61},{3,60},{4,59},{5,58},{6,57},{7,56},{8,55},{9,... | collective-permute-start | bytes 294920 | tf_op jit(solution)/shard_map/grad_mirror/ppermute | solution.py:343
  83.4 6.6 %collective-permute-start.7 = (bf16[2,48,512]{2,1,0:T(8,128)(2,1)S(1)}, bf16[2,48,512]{2,1,0:T(8,128)(2,1)S(1)}, u32[]{:S(2)}, u32[]{:S(2)}) collective-permute-start(bf16[2,48,512]{2,1,0:T(8,128)(2,1)S(1)} %add_convert_fusion.g0_ref), channel_id=1, source_target_pairs={{0,127},{1,126},{2,125},{3,124},{4,123},{5,122},{6,121},{7,120},{8... | collective-permute-start | bytes 294920 | tf_op jit(solution)/shard_map/grad_mirror/ppermute | solution.py:344
  90.0 0.0 copy-start.2
  90.0 8.6 %collective-permute-start.8 = (bf16[2,8,512]{2,1,0:T(8,128)(2,1)S(1)}, bf16[2,8,512]{2,1,0:T(8,128)(2,1)S(1)}, u32[]{:S(2)}, u32[]{:S(2)}) collective-permute-start(bf16[2,8,512]{2,1,0:T(8,128)(2,1)S(1)} %slice_select_fusion), channel_id=1, source_target_pairs={{0,32},{1,63},{2,62},{3,61},{4,60},{5,59},{6,58},{7,57},{8,56},{9,... | collective-permute-start | bytes 49160 | tf_op jit(solution)/shard_map/grad_mirror/ppermute | solution.py:345
  98.6 8.3 %collective-permute-start.9 = (bf16[2,8,512]{2,1,0:T(8,128)(2,1)S(1)}, bf16[2,8,512]{2,1,0:T(8,128)(2,1)S(1)}, u32[]{:S(2)}, u32[]{:S(2)}) collective-permute-start(bf16[2,8,512]{2,1,0:T(8,128)(2,1)S(1)} %slice_select_fusion), channel_id=1, source_target_pairs={{0,96},{1,127},{2,126},{3,125},{4,124},{5,123},{6,122},{7,121},{8,... | collective-permute-start | bytes 49160 | tf_op jit(solution)/shard_map/grad_mirror/ppermute | solution.py:346
  106.9 8.2 %collective-permute-done.9.head1_ref = bf16[2,8,512]{2,1,0:T(8,128)(2,1)S(1)} collective-permute-done((bf16[2,8,512]{2,1,0:T(8,128)(2,1)S(1)}, bf16[2,8,512]{2,1,0:T(8,128)(2,1)S(1)}, u32[]{:S(2)}, u32[]{:S(2)}) %collective-permute-start.9) | collective-permute-done | bytes 16416 | tf_op jit(solution)/shard_map/grad_mirror/ppermute | solution.py:346
  115.1 1.6 %kernel_g.1 = bf16[2,64,512]{2,1,0:T(8,128)(2,1)} custom-call(s32[1]{0:T(128)} %bitcast.idx_ref, bf16[2,48,512]{2,1,0:T(8,128)(2,1)S(1)} %add_convert_fusion.g0_ref, bf16[2,48,512]{2,1,0:T(8,128)(2,1)S(1)} %collective-permute-done.5.g1_ref, bf16[2,48,512]{2,1,0:T(8,128)(2,1)S(1)} %collective-permute-done.6.far0_ref, ...), custom_call_target="tpu_custom_call" | custom-call | flops 100000000 | bytes 1000000 | tf_op jit(solution)/shard_map/kernel_g/pallas_call | solution.py:365
  116.6 0.0 all-to-all-done.1
  116.7 1.3 %kernel_c.1 = (bf16[128,512]{1,0:T(8,128)(2,1)}, bf16[128,512]{1,0:T(8,128)(2,1)}) custom-call(s32[1]{0:T(128)} %bitcast.idx_ref, bf16[512,256]{1,0:T(8,128)(2,1)S(1)} %bitcast.14, bf16[512,512]{1,0:T(8,128)(2,1)S(1)} %copy-done.2), custom_call_target="tpu_custom_call" | custom-call | flops 400000000 | bytes 2000000 | tf_op jit(solution)/shard_map/kernel_c/pallas_call | solution.py:349
  (21 shorter events, 0.0 us)
Async XLA Ops:
  0.6 41.7 %copy-start = (bf16[512,512]{1,0:T(8,128)(2,1)S(1)}, bf16[512,512]{1,0:T(8,128)(2,1)}, u32[]{:S(2)}) copy-start(bf16[512,512]{1,0:T(8,128)(2,1)} %constant.31.clone.flip_ref) | copy-start | bytes 1572868
  3.2 23.7 %copy-start.10 = (bf16[2,8,512]{2,1,0:T(8,128)(2,1)S(1)}, bf16[2,8,512]{2,1,0:T(8,128)(2,1)}, u32[]{:S(2)}) copy-start(bf16[2,8,512]{2,1,0:T(8,128)(2,1)} %get-tuple-element.12) | copy-start | bytes 49156
  3.2 39.1 %copy-start.1 = (bf16[2,8,8,512]{3,2,1,0:T(8,128)(2,1)S(1)}, bf16[2,8,8,512]{3,2,1,0:T(8,128)(2,1)}, u32[]{:S(2)}) copy-start(bf16[2,8,8,512]{3,2,1,0:T(8,128)(2,1)} %param.16) | copy-start | bytes 393220
  3.2 39.1 %copy-start.6 = (bf16[3,112,256]{2,1,0:T(8,128)(2,1)S(1)}, bf16[3,112,256]{2,1,0:T(8,128)(2,1)}, u32[]{:S(2)}) copy-start(bf16[3,112,256]{2,1,0:T(8,128)(2,1)} %constant.34.clone.own_ref) | copy-start | bytes 516100
  3.3 39.1 %copy-start.7 = (bf16[3,112,256]{2,1,0:T(8,128)(2,1)S(1)}, bf16[3,112,256]{2,1,0:T(8,128)(2,1)}, u32[]{:S(2)}) copy-start(bf16[3,112,256]{2,1,0:T(8,128)(2,1)} %constant.35.clone.mirror_ref) | copy-start | bytes 516100
  3.3 40.2 %all-to-all-start = ((bf16[64,8,256]{2,1,0:T(8,128)(2,1)}), bf16[64,8,256]{2,1,0:T(8,128)(2,1)S(1)}, u32[]{:S(2)}, u32[]{:S(2)}) async-start(bf16[64,8,256]{2,1,0:T(8,128)(2,1)} %bitcast.15), calls=%async_computation | async-start | bytes 524288 | tf_op jit(solution)/shard_map/first_exchange/all_to_all | solution.py:306
  18.7 23.6 %collective-permute-start = (bf16[2,32,512]{2,1,0:T(8,128)(2,1)}, bf16[2,32,512]{2,1,0:T(8,128)(2,1)S(1)}, u32[]{:S(2)}, u32[]{:S(2)}) collective-permute-start(bf16[2,32,512]{2,1,0:T(8,128)(2,1)} %get-tuple-element.11), channel_id=1, source_target_pairs={{0,63},{1,62},{2,61},{3,60},{4,59},{5,58},{6,57},{7,56},{8,55},{9,... | collective-permute-start | bytes 196616 | tf_op jit(solution)/shard_map/filter_mirror/ppermute | solution.py:308
  26.9 16.6 %copy-start.3 = (bf16[512,512]{1,0:T(8,128)(2,1)S(1)}, bf16[512,512]{1,0:T(8,128)(2,1)}, u32[]{:S(2)}) copy-start(bf16[512,512]{1,0:T(8,128)(2,1)} %constant.29.clone.wc_ref) | copy-start | bytes 1572868
  26.9 16.6 %copy-start.4 = (bf16[512,512]{1,0:T(8,128)(2,1)S(1)}, bf16[512,512]{1,0:T(8,128)(2,1)}, u32[]{:S(2)}) copy-start(bf16[512,512]{1,0:T(8,128)(2,1)} %constant.30.clone.ws_ref) | copy-start | bytes 1572868
  26.9 16.6 %copy-start.5 = (f32[2,2,48,256]{3,2,1,0:T(8,128)S(1)}, f32[2,2,48,256]{3,2,1,0:T(8,128)}, u32[]{:S(2)}) copy-start(f32[2,2,48,256]{3,2,1,0:T(8,128)} %constant.38.clone.gather_ref) | copy-start | bytes 589828
  26.9 15.4 %collective-permute-start.1 = (bf16[2,8,512]{2,1,0:T(8,128)(2,1)S(1)}, bf16[2,8,512]{2,1,0:T(8,128)(2,1)S(1)}, u32[]{:S(2)}, u32[]{:S(2)}) collective-permute-start(bf16[2,8,512]{2,1,0:T(8,128)(2,1)S(1)} %copy-done.10), channel_id=1, source_target_pairs={{0,32},{1,63},{2,62},{3,61},{4,60},{5,59},{6,58},{7,57},{8,56},{9,... | collective-permute-start | bytes 49160 | tf_op jit(solution)/shard_map/filter_mirror/ppermute | solution.py:309
  47.1 69.5 %all-to-all-start.1 = ((bf16[64,8,256]{2,1,0:T(8,128)(2,1)}), bf16[64,8,256]{2,1,0:T(8,128)(2,1)S(1)}, u32[]{:S(2)}, u32[]{:S(2)}) async-start(bf16[64,8,256]{2,1,0:T(8,128)(2,1)} %bitcast.6), calls=%async_computation.1 | async-start | bytes 524288 | tf_op jit(solution)/shard_map/second_exchange/all_to_all | solution.py:335
  56.8 10.5 %collective-permute-start.2 = (bf16[2,48,512]{2,1,0:T(8,128)(2,1)S(1)}, bf16[2,48,512]{2,1,0:T(8,128)(2,1)S(1)}, u32[]{:S(2)}, u32[]{:S(2)}) collective-permute-start(bf16[2,48,512]{2,1,0:T(8,128)(2,1)S(1)} %get-tuple-element.16), channel_id=1, source_target_pairs={{0,128},{64,192},{128,0},{192,64},{256,384},{320,448},{384,256},{4... | collective-permute-start | bytes 294920 | tf_op jit(solution)/shard_map/grad_sum/ppermute | solution.py:337
  60.3 8.0 %collective-permute-start.3 = (bf16[2,48,512]{2,1,0:T(8,128)(2,1)S(1)}, bf16[2,48,512]{2,1,0:T(8,128)(2,1)S(1)}, u32[]{:S(2)}, u32[]{:S(2)}) collective-permute-start(bf16[2,48,512]{2,1,0:T(8,128)(2,1)S(1)} %get-tuple-element.16), channel_id=1, source_target_pairs={{0,256},{64,320},{128,384},{192,448},{256,0},{320,64},{384,128},{4... | collective-permute-start | bytes 294920 | tf_op jit(solution)/shard_map/grad_sum/ppermute | solution.py:337
  65.1 7.7 %collective-permute-start.4 = (bf16[2,48,512]{2,1,0:T(8,128)(2,1)S(1)}, bf16[2,48,512]{2,1,0:T(8,128)(2,1)S(1)}, u32[]{:S(2)}, u32[]{:S(2)}) collective-permute-start(bf16[2,48,512]{2,1,0:T(8,128)(2,1)S(1)} %get-tuple-element.16), channel_id=1, source_target_pairs={{0,384},{64,448},{128,256},{192,320},{256,128},{320,192},{384,0},{... | collective-permute-start | bytes 294920 | tf_op jit(solution)/shard_map/grad_sum/ppermute | solution.py:337
  72.9 42.2 %copy-start.8 = (bf16[4,64,112]{2,1,0:T(8,128)(2,1)S(1)}, bf16[4,64,112]{2,1,0:T(8,128)(2,1)}, u32[]{:S(2)}) copy-start(bf16[4,64,112]{2,1,0:T(8,128)(2,1)} %constant.36.clone.own_ref) | copy-start | bytes 172036
  72.9 42.2 %copy-start.9 = (bf16[4,64,112]{2,1,0:T(8,128)(2,1)S(1)}, bf16[4,64,112]{2,1,0:T(8,128)(2,1)}, u32[]{:S(2)}) copy-start(bf16[4,64,112]{2,1,0:T(8,128)(2,1)} %constant.37.clone.mirror_ref) | copy-start | bytes 172036
  72.9 42.1 %collective-permute-start.5 = (bf16[2,48,512]{2,1,0:T(8,128)(2,1)S(1)}, bf16[2,48,512]{2,1,0:T(8,128)(2,1)S(1)}, u32[]{:S(2)}, u32[]{:S(2)}) collective-permute-start(bf16[2,48,512]{2,1,0:T(8,128)(2,1)S(1)} %add_convert_fusion.g0_ref), channel_id=1, source_target_pairs={{0,64},{64,0},{128,192},{192,128},{256,320},{320,256},{384,448},{4... | collective-permute-start | bytes 294920 | tf_op jit(solution)/shard_map/grad_mirror/ppermute | solution.py:347
  77.6 37.5 %collective-permute-start.6 = (bf16[2,48,512]{2,1,0:T(8,128)(2,1)S(1)}, bf16[2,48,512]{2,1,0:T(8,128)(2,1)S(1)}, u32[]{:S(2)}, u32[]{:S(2)}) collective-permute-start(bf16[2,48,512]{2,1,0:T(8,128)(2,1)S(1)} %add_convert_fusion.g0_ref), channel_id=1, source_target_pairs={{0,63},{1,62},{2,61},{3,60},{4,59},{5,58},{6,57},{7,56},{8,55},{9,... | collective-permute-start | bytes 294920 | tf_op jit(solution)/shard_map/grad_mirror/ppermute | solution.py:343
  83.4 31.6 %collective-permute-start.7 = (bf16[2,48,512]{2,1,0:T(8,128)(2,1)S(1)}, bf16[2,48,512]{2,1,0:T(8,128)(2,1)S(1)}, u32[]{:S(2)}, u32[]{:S(2)}) collective-permute-start(bf16[2,48,512]{2,1,0:T(8,128)(2,1)S(1)} %add_convert_fusion.g0_ref), channel_id=1, source_target_pairs={{0,127},{1,126},{2,125},{3,124},{4,123},{5,122},{6,121},{7,120},{8... | collective-permute-start | bytes 294920 | tf_op jit(solution)/shard_map/grad_mirror/ppermute | solution.py:344
  90.0 26.6 %copy-start.2 = (bf16[512,512]{1,0:T(8,128)(2,1)S(1)}, bf16[512,512]{1,0:T(8,128)(2,1)}, u32[]{:S(2)}) copy-start(bf16[512,512]{1,0:T(8,128)(2,1)} %constant.28.clone.t_ref) | copy-start | bytes 1572868
  90.0 16.9 %collective-permute-start.8 = (bf16[2,8,512]{2,1,0:T(8,128)(2,1)S(1)}, bf16[2,8,512]{2,1,0:T(8,128)(2,1)S(1)}, u32[]{:S(2)}, u32[]{:S(2)}) collective-permute-start(bf16[2,8,512]{2,1,0:T(8,128)(2,1)S(1)} %slice_select_fusion), channel_id=1, source_target_pairs={{0,32},{1,63},{2,62},{3,61},{4,60},{5,59},{6,58},{7,57},{8,56},{9,... | collective-permute-start | bytes 49160 | tf_op jit(solution)/shard_map/grad_mirror/ppermute | solution.py:345
  98.6 16.5 %collective-permute-start.9 = (bf16[2,8,512]{2,1,0:T(8,128)(2,1)S(1)}, bf16[2,8,512]{2,1,0:T(8,128)(2,1)S(1)}, u32[]{:S(2)}, u32[]{:S(2)}) collective-permute-start(bf16[2,8,512]{2,1,0:T(8,128)(2,1)S(1)} %slice_select_fusion), channel_id=1, source_target_pairs={{0,96},{1,127},{2,126},{3,125},{4,124},{5,123},{6,122},{7,121},{8,... | collective-permute-start | bytes 49160 | tf_op jit(solution)/shard_map/grad_mirror/ppermute | solution.py:346

commit v3 on v2

--- a/solution.py
+++ b/solution.py
@@ -245,32 +245,24 @@
         ref[...] = total.astype(BF)
 
 
-def kernel_g(idx_ref, g0_ref, g1_ref, far0_ref, far1_ref, head0_ref, head1_ref, own_ref,
-             mirror_ref, flip_ref, out_ref, rows):
+def kernel_g(idx_ref, g_ref, far_ref, head_ref, own_ref, mirror_ref, flip_ref, out_ref, rows):
     place = idx_ref[0]
     kind = jnp.where(
         place == 0, 0, jnp.where(place == 32, 3, jnp.where(place < 32, 1, 2))
     )
-    sources = ((g0_ref, far0_ref, head0_ref), (g1_ref, far1_ref, head1_ref))
-    for k, (g_ref, far_ref, head_ref) in enumerate(sources):
-        rows[k, :, :48, :] = g_ref[...]
-        rows[k, :, 48:96, :] = far_ref[...]
-        rows[k, :, 96:, :] = jnp.zeros((2, 16, N), BF)
-        rows[k, :, 96:104, :] = head_ref[...]
+    rows[:, :48, :] = g_ref[...]
+    rows[:, 48:80, :] = far_ref[...]
+    rows[:, 80:96, :] = jnp.zeros((2, 16, N), BF)
+    rows[:, 96:, :] = jnp.zeros((2, 16, N), BF)
+    rows[:, 96:104, :] = head_ref[...]
     row = lax.broadcasted_iota(jnp.int32, (64, N), 0)
     shifted = ((row & 7) == 0) & (place == 0)
     for ri in range(2):
-        near = dot(own_ref[kind], rows[0, ri]) + dot(own_ref[kind], rows[1, ri])
-        far = [
-            dot(dot(mirror_ref[kind], rows[k, ri]).astype(BF), flip_ref[...]) for k in range(2)
-        ]
-        far = far[0] + far[1]
+        near = dot(own_ref[kind], rows[ri])
+        far = dot(mirror_ref[kind], rows[ri]).astype(BF)
+        far = dot(far, flip_ref[...])
         far = jnp.where(shifted, pltpu.roll(far, 1, 1), far)
         out_ref[ri] = (near + far if ri == 0 else near - far).astype(BF)
-
-
-def across(moves):
-    return [(d * SEQ + a, (d ^ 1) * SEQ + b) for d in range(8) for a, b in moves]
 
 
 def body(signal, cotangent, filter_spec):
@@ -286,98 +278,76 @@
     opposite = [(d, SEQ - 1 - d) for d in range(SEQ)]
     heads_to = [(d, {0: 32, 32: 0}.get(d, SEQ - d)) for d in range(SEQ)]
     filt = filter_spec.reshape(2, 64, N)
-    with jax.named_scope("kernel_a"):
-        sent, tails, heads = pl.pallas_call(
-            kernel_a,
-            in_specs=[SMEM] + [VMEM] * 6,
-            out_specs=[VMEM] * 3,
-            out_shape=[
-                jax.ShapeDtypeStruct((N, HALF), BF),
-                jax.ShapeDtypeStruct((2, 32, N), BF),
-                jax.ShapeDtypeStruct((2, 8, N), BF),
-            ],
-            scratch_shapes=[
-                pltpu.VMEM((2, 256, 128), F32),
-                pltpu.VMEM((2, 256, 128), F32),
-                pltpu.VMEM((2, N, 128), F32),
-            ],
-        )(place, signal.reshape(128, N), cotangent.reshape(128, N), table, filt, tail, head)
-    with jax.named_scope("first_exchange"):
-        got = lax.all_to_all(sent.reshape(SEQ, ROWS, HALF), "seq", 0, 0, tiled=True)
-    with jax.named_scope("filter_mirror"):
-        tails = lax.ppermute(tails, "seq", opposite)
-        heads = lax.ppermute(heads, "seq", heads_to)
-    with jax.named_scope("kernel_f"):
-        spread = pl.pallas_call(
-            kernel_f,
-            in_specs=[SMEM] + [VMEM] * 6,
-            out_specs=VMEM,
-            out_shape=jax.ShapeDtypeStruct((N, N), F32),
-            scratch_shapes=[pltpu.VMEM((2, 112, N), BF)],
-            compiler_params=PARAMS,
-            cost_estimate=pl.CostEstimate(
-                flops=400000000, bytes_accessed=2000000, transcendentals=0
-            ),
-        )(place, filt, tails, heads, f_own, f_mirror, flip)
-    with jax.named_scope("kernel_b"):
-        back, grad = pl.pallas_call(
-            kernel_b,
-            in_specs=[SMEM] + [VMEM] * 5,
-            out_specs=[VMEM, VMEM],
-            out_shape=[
-                jax.ShapeDtypeStruct((N, HALF), BF),
-                jax.ShapeDtypeStruct((2, 48, N), BF),
-            ],
-            scratch_shapes=[pltpu.VMEM((N, HALF), BF)],
-            compiler_params=PARAMS,
-        )(place, got.reshape(N, HALF), cos_t, sin_t, spread, gather)
-    with jax.named_scope("second_exchange"):
-        mid = lax.all_to_all(back.reshape(SEQ, ROWS, HALF), "seq", 0, 0, tiled=True)
-    with jax.named_scope("grad_sum"):
-        parts = [lax.ppermute(grad, "dp", [(d, d ^ bit) for d in range(8)]) for bit in (2, 4, 6)]
-        wide = [v.astype(F32) for v in [grad] + parts]
-        grad = ((wide[0] + wide[1]) + (wide[2] + wide[3])).astype(BF)
-    with jax.named_scope("grad_mirror"):
-        slot = jnp.where(place[0] == 0, grad[:, 32:40], grad[:, :8])
-        both = ("dp", "seq")
-        far0 = lax.ppermute(grad, "seq", opposite)
-        far1 = lax.ppermute(grad, both, across(opposite))
-        slot0 = lax.ppermute(slot, "seq", heads_to)
-        slot1 = lax.ppermute(slot, both, across(heads_to))
-        grad1 = lax.ppermute(grad, "dp", [(d, d ^ 1) for d in range(8)])
-    with jax.named_scope("kernel_c"):
-        output, grad_signal = pl.pallas_call(
-            kernel_c,
-            in_specs=[SMEM, VMEM, VMEM],
-            out_specs=[VMEM, VMEM],
-            out_shape=[jax.ShapeDtypeStruct((128, N), BF)] * 2,
-            scratch_shapes=[
-                pltpu.VMEM((2, N, 128), F32),
-                pltpu.VMEM((2, 256, 128), F32),
-                pltpu.VMEM((2, 256, 128), F32),
-            ],
-            compiler_params=PARAMS,
-            cost_estimate=pl.CostEstimate(
-                flops=400000000, bytes_accessed=2000000, transcendentals=0
-            ),
-        )(place, mid.reshape(N, HALF), table)
-    with jax.named_scope("kernel_g"):
-        grad_filter = pl.pallas_call(
-            kernel_g,
-            in_specs=[SMEM] + [VMEM] * 9,
-            out_specs=VMEM,
-            out_shape=jax.ShapeDtypeStruct((2, 64, N), BF),
-            scratch_shapes=[pltpu.VMEM((2, 2, 112, N), BF)],
-            compiler_params=PARAMS,
-            cost_estimate=pl.CostEstimate(
-                flops=100000000, bytes_accessed=1000000, transcendentals=0
-            ),
-        )(place, grad, grad1, far0, far1, slot0, slot1, g_own, g_mirror, flip)
+    sent, tails, heads = pl.pallas_call(
+        kernel_a,
+        in_specs=[SMEM] + [VMEM] * 6,
+        out_specs=[VMEM] * 3,
+        out_shape=[
+            jax.ShapeDtypeStruct((N, HALF), BF),
+            jax.ShapeDtypeStruct((2, 32, N), BF),
+            jax.ShapeDtypeStruct((2, 8, N), BF),
+        ],
+        scratch_shapes=[
+            pltpu.VMEM((2, 256, 128), F32),
+            pltpu.VMEM((2, 256, 128), F32),
+            pltpu.VMEM((2, N, 128), F32),
+        ],
+    )(place, signal.reshape(128, N), cotangent.reshape(128, N), table, filt, tail, head)
+    got = lax.all_to_all(sent.reshape(SEQ, ROWS, HALF), "seq", 0, 0, tiled=True)
+    tails = lax.ppermute(tails, "seq", opposite)
+    heads = lax.ppermute(heads, "seq", heads_to)
+    spread = pl.pallas_call(
+        kernel_f,
+        in_specs=[SMEM] + [VMEM] * 6,
+        out_specs=VMEM,
+        out_shape=jax.ShapeDtypeStruct((N, N), F32),
+        scratch_shapes=[pltpu.VMEM((2, 112, N), BF)],
+        compiler_params=PARAMS,
+        cost_estimate=pl.CostEstimate(flops=400000000, bytes_accessed=2000000, transcendentals=0),
+    )(place, filt, tails, heads, f_own, f_mirror, flip)
+    back, grad = pl.pallas_call(
+        kernel_b,
+        in_specs=[SMEM] + [VMEM] * 5,
+        out_specs=[VMEM, VMEM],
+        out_shape=[
+            jax.ShapeDtypeStruct((N, HALF), BF),
+            jax.ShapeDtypeStruct((2, 48, N), BF),
+        ],
+        scratch_shapes=[pltpu.VMEM((N, HALF), BF)],
+        compiler_params=PARAMS,
+    )(place, got.reshape(N, HALF), cos_t, sin_t, spread, gather)
+    mid = lax.all_to_all(back.reshape(SEQ, ROWS, HALF), "seq", 0, 0, tiled=True)
+    for bit in (1, 2, 4):
+        other = lax.ppermute(grad, "dp", [(d, d ^ bit) for d in range(8)])
+        grad = (grad.astype(F32) + other.astype(F32)).astype(BF)
+    far = lax.ppermute(grad[:, :32], "seq", opposite)
+    slot = jnp.where(place[0] == 0, grad[:, 32:40], grad[:, :8])
+    slot = lax.ppermute(slot, "seq", heads_to)
+    output, grad_signal = pl.pallas_call(
+        kernel_c,
+        in_specs=[SMEM, VMEM, VMEM],
+        out_specs=[VMEM, VMEM],
+        out_shape=[jax.ShapeDtypeStruct((128, N), BF)] * 2,
+        scratch_shapes=[
+            pltpu.VMEM((2, N, 128), F32),
+            pltpu.VMEM((2, 256, 128), F32),
+            pltpu.VMEM((2, 256, 128), F32),
+        ],
+        compiler_params=PARAMS,
+        cost_estimate=pl.CostEstimate(flops=400000000, bytes_accessed=2000000, transcendentals=0),
+    )(place, mid.reshape(N, HALF), table)
+    grad_filter = pl.pallas_call(
+        kernel_g,
+        in_specs=[SMEM] + [VMEM] * 6,
+        out_specs=VMEM,
+        out_shape=jax.ShapeDtypeStruct((2, 64, N), BF),
+        scratch_shapes=[pltpu.VMEM((2, 112, N), BF)],
+        compiler_params=PARAMS,
+        cost_estimate=pl.CostEstimate(flops=100000000, bytes_accessed=1000000, transcendentals=0),
+    )(place, grad, far, slot, g_own, g_mirror, flip)
     return output.reshape(shape), grad_signal.reshape(shape), grad_filter.reshape(2, 8, 8, N)
 
 
 def solution(mesh):
     placed = (P(None, "dp", "seq", None), P(None, "dp", "seq", None), P(None, None, "seq", None))
-    return jax.shard_map(
-        body, mesh=mesh, in_specs=placed, out_specs=placed, check_vma=False
-    )
+    return jax.shard_map(body, mesh=mesh, in_specs=placed, out_specs=placed, check_vma=False)

time: 119 us -> 101 us (0.85)
  the two profiles are of different devices: /device:TPU:128 before, /device:TPU:144 now
where the time goes in v3:
time: 101 us
  starting transfers between devices  59.9 us (59%)
  waiting for transfers between devices  29.9 us (30%)
  Pallas kernels  9.97 us (10%)
    all_to_all x1, starting transfers between devices, body(): got = lax.all_to_all(sent.reshape(SEQ, ROWS, HALF), 'seq', 0, 0, tiled=True)  15.5 us
    ppermute x1, waiting for transfers between devices, body(): slot = lax.ppermute(slot, 'seq', heads_to)  10.3 us
    ppermute x1, waiting for transfers between devices, body(): heads = lax.ppermute(heads, 'seq', heads_to)  10.3 us
    ppermute x3, starting transfers between devices, body(): other = lax.ppermute(grad, 'dp', [(d, d ^ bit) for d in range(8)])  10.1 us
    all_to_all x1, starting transfers between devices, body(): mid = lax.all_to_all(back.reshape(SEQ, ROWS, HALF), 'seq', 0, 0, tiled=True)  9.7 us
    ppermute x3, waiting for transfers between devices, body(): other = lax.ppermute(grad, 'dp', [(d, d ^ bit) for d in range(8)])  9.27 us
    ppermute x1, starting transfers between devices, body(): tails = lax.ppermute(tails, 'seq', opposite)  8.15 us
    ppermute x1, starting transfers between devices, body(): far = lax.ppermute(grad[:, :32], 'seq', opposite)  6.58 us
  transfers between devices with their start and end apart: 9, of which 4 were waited for; matrix products, arithmetic and copies ran while one was open for 0% of the time, Pallas kernels for 2%

profile of v3, /device:TPU:144, one launch (start us, length us, event | category | flops | bytes accessed | tf_op | source)
XLA Modules:
  0.0 100.9 jit_solution(10925838600723057677)
XLA Ops:
  0.6 0.0 copy-start
  0.6 2.6 %shard_map.157 = (bf16[512,256]{1,0:T(8,128)(2,1)}, bf16[2,32,512]{2,1,0:T(8,128)(2,1)}, bf16[2,8,512]{2,1,0:T(8,128)(2,1)}) custom-call(s32[1]{0:T(128)} %bitcast.idx_ref, bf16[128,512]{1,0:T(8,128)(2,1)} %bitcast.16, bf16[128,512]{1,0:T(8,128)(2,1)} %bitcast.17, bf16[512,512]{1,0:T(8,128)(2,1)} %constant.28.clone.t_ref, bf16[2,64,512]{2,1,0:T(8,128)(2,1)} %bitcast.12, ...), custom_call_target="tpu_custom_call" | custom-call | tf_op jit(solution)/shard_map/pallas_call | solution.py:281
  3.3 0.0 copy-start.7
  3.3 15.5 %all-to-all-start = ((bf16[64,8,256]{2,1,0:T(8,128)(2,1)}), bf16[64,8,256]{2,1,0:T(8,128)(2,1)S(1)}, u32[]{:S(2)}, u32[]{:S(2)}) async-start(bf16[64,8,256]{2,1,0:T(8,128)(2,1)} %bitcast.15), calls=%async_computation | async-start | bytes 524288 | tf_op jit(solution)/shard_map/all_to_all | solution.py:296
  18.8 8.2 %collective-permute-start = (bf16[2,32,512]{2,1,0:T(8,128)(2,1)}, bf16[2,32,512]{2,1,0:T(8,128)(2,1)S(1)}, u32[]{:S(2)}, u32[]{:S(2)}) collective-permute-start(bf16[2,32,512]{2,1,0:T(8,128)(2,1)} %get-tuple-element.11), channel_id=1, source_target_pairs={{0,63},{1,62},{2,61},{3,60},{4,59},{5,58},{6,57},{7,56},{8,55},{9,... | collective-permute-start | bytes 196616 | tf_op jit(solution)/shard_map/ppermute | solution.py:297
  26.9 0.0 copy-start.3
  26.9 0.0 copy-start.4
  27.0 0.0 copy-start.5
  27.0 5.0 %collective-permute-start.1 = (bf16[2,8,512]{2,1,0:T(8,128)(2,1)S(1)}, bf16[2,8,512]{2,1,0:T(8,128)(2,1)S(1)}, u32[]{:S(2)}, u32[]{:S(2)}) collective-permute-start(bf16[2,8,512]{2,1,0:T(8,128)(2,1)S(1)} %copy-done.10), channel_id=1, source_target_pairs={{0,32},{1,63},{2,62},{3,61},{4,60},{5,59},{6,58},{7,57},{8,56},{9,... | collective-permute-start | bytes 49160 | tf_op jit(solution)/shard_map/ppermute | solution.py:298
  32.0 10.3 %collective-permute-done.1.head_ref = bf16[2,8,512]{2,1,0:T(8,128)(2,1)S(1)} collective-permute-done((bf16[2,8,512]{2,1,0:T(8,128)(2,1)S(1)}, bf16[2,8,512]{2,1,0:T(8,128)(2,1)S(1)}, u32[]{:S(2)}, u32[]{:S(2)}) %collective-permute-start.1) | collective-permute-done | bytes 16416 | tf_op jit(solution)/shard_map/ppermute | solution.py:298
  42.3 0.0 collective-permute-done.tail_ref
  42.4 1.1 %shard_map.158.h_ref = f32[512,512]{1,0:T(8,128)S(1)} custom-call(s32[1]{0:T(128)} %bitcast.idx_ref, bf16[2,64,512]{2,1,0:T(8,128)(2,1)S(1)} %bitcast.13, bf16[2,32,512]{2,1,0:T(8,128)(2,1)S(1)} %collective-permute-done.tail_ref, bf16[2,8,512]{2,1,0:T(8,128)(2,1)S(1)} %collective-permute-done.1.head_ref, bf16[3,112,256]{2,1,0:T(8,128)(2,1)S(1)} %copy-done.6, ...), custom_call_target="tpu_custom_call" | custom-call | flops 400000000 | bytes 2000000 | tf_op jit(solution)/shard_map/pallas_call | solution.py:299
  43.5 0.0 all-to-all-done
  43.5 0.0 copy-done.3
  43.5 3.6 %shard_map.159 = (bf16[512,256]{1,0:T(8,128)(2,1)}, bf16[2,48,512]{2,1,0:T(8,128)(2,1)S(1)}) custom-call(s32[1]{0:T(128)} %bitcast.idx_ref, bf16[512,256]{1,0:T(8,128)(2,1)S(1)} %bitcast.11, bf16[512,512]{1,0:T(8,128)(2,1)S(1)} %copy-done.3, bf16[512,512]{1,0:T(8,128)(2,1)S(1)} %copy-done.4, f32[512,512]{1,0:T(8,128)S(1)} %shard_map.158.h_ref, ...), custom_call_target="tpu_custom_call" | custom-call | tf_op jit(solution)/shard_map/pallas_call | solution.py:308
  47.2 4.6 %collective-permute-start.2 = (bf16[2,48,512]{2,1,0:T(8,128)(2,1)S(1)}, bf16[2,48,512]{2,1,0:T(8,128)(2,1)S(1)}, u32[]{:S(2)}, u32[]{:S(2)}) collective-permute-start(bf16[2,48,512]{2,1,0:T(8,128)(2,1)S(1)} %get-tuple-element.16), channel_id=1, source_target_pairs={{0,64},{64,0},{128,192},{192,128},{256,320},{320,256},{384,448},{4... | collective-permute-start | bytes 294920 | tf_op jit(solution)/shard_map/ppermute | solution.py:321
  51.8 9.7 %all-to-all-start.1 = ((bf16[64,8,256]{2,1,0:T(8,128)(2,1)}), bf16[64,8,256]{2,1,0:T(8,128)(2,1)S(1)}, u32[]{:S(2)}, u32[]{:S(2)}) async-start(bf16[64,8,256]{2,1,0:T(8,128)(2,1)} %bitcast.6), calls=%async_computation.1 | async-start | bytes 524288 | tf_op jit(solution)/shard_map/all_to_all | solution.py:319
  61.5 0.0 collective-permute-done.2
  61.6 3.2 %collective-permute-start.3 = (bf16[2,48,512]{2,1,0:T(8,128)(2,1)S(1)}, bf16[2,48,512]{2,1,0:T(8,128)(2,1)S(1)}, u32[]{:S(2)}, u32[]{:S(2)}) collective-permute-start(bf16[2,48,512]{2,1,0:T(8,128)(2,1)S(1)} %add_convert_fusion.2), channel_id=1, source_target_pairs={{0,128},{64,192},{128,0},{192,64},{256,384},{320,448},{384,256},{4... | collective-permute-start | bytes 294920 | tf_op jit(solution)/shard_map/ppermute | solution.py:321
  64.8 3.5 %collective-permute-done.3 = bf16[2,48,512]{2,1,0:T(8,128)(2,1)S(1)} collective-permute-done((bf16[2,48,512]{2,1,0:T(8,128)(2,1)S(1)}, bf16[2,48,512]{2,1,0:T(8,128)(2,1)S(1)}, u32[]{:S(2)}, u32[]{:S(2)}) %collective-permute-start.3) | collective-permute-done | bytes 98336 | tf_op jit(solution)/shard_map/ppermute | solution.py:321
  68.3 2.2 %collective-permute-start.4 = (bf16[2,48,512]{2,1,0:T(8,128)(2,1)S(1)}, bf16[2,48,512]{2,1,0:T(8,128)(2,1)S(1)}, u32[]{:S(2)}, u32[]{:S(2)}) collective-permute-start(bf16[2,48,512]{2,1,0:T(8,128)(2,1)S(1)} %add_convert_fusion.1), channel_id=1, source_target_pairs={{0,256},{64,320},{128,384},{192,448},{256,0},{320,64},{384,128},{4... | collective-permute-start | bytes 294920 | tf_op jit(solution)/shard_map/ppermute | solution.py:321
  70.6 5.8 %collective-permute-done.4 = bf16[2,48,512]{2,1,0:T(8,128)(2,1)S(1)} collective-permute-done((bf16[2,48,512]{2,1,0:T(8,128)(2,1)S(1)}, bf16[2,48,512]{2,1,0:T(8,128)(2,1)S(1)}, u32[]{:S(2)}, u32[]{:S(2)}) %collective-permute-start.4) | collective-permute-done | bytes 98336 | tf_op jit(solution)/shard_map/ppermute | solution.py:321
  76.3 0.0 copy-start.8
  76.4 0.0 copy-start.9
  76.4 0.0 copy-start.2
  76.4 6.6 %collective-permute-start.5 = (bf16[2,32,512]{2,1,0:T(8,128)(2,1)S(1)}, bf16[2,32,512]{2,1,0:T(8,128)(2,1)S(1)}, u32[]{:S(2)}, u32[]{:S(2)}) collective-permute-start(bf16[2,32,512]{2,1,0:T(8,128)(2,1)S(1)} %slice.12), channel_id=1, source_target_pairs={{0,63},{1,62},{2,61},{3,60},{4,59},{5,58},{6,57},{7,56},{8,55},{9,... | collective-permute-start | bytes 196616 | tf_op jit(solution)/shard_map/ppermute | solution.py:323
  83.0 4.9 %collective-permute-start.6 = (bf16[2,8,512]{2,1,0:T(8,128)(2,1)S(1)}, bf16[2,8,512]{2,1,0:T(8,128)(2,1)S(1)}, u32[]{:S(2)}, u32[]{:S(2)}) collective-permute-start(bf16[2,8,512]{2,1,0:T(8,128)(2,1)S(1)} %slice_select_fusion), channel_id=1, source_target_pairs={{0,32},{1,63},{2,62},{3,61},{4,60},{5,59},{6,58},{7,57},{8,56},{9,... | collective-permute-start | bytes 49160 | tf_op jit(solution)/shard_map/ppermute | solution.py:325
  87.9 10.3 %collective-permute-done.6.head_ref = bf16[2,8,512]{2,1,0:T(8,128)(2,1)S(1)} collective-permute-done((bf16[2,8,512]{2,1,0:T(8,128)(2,1)S(1)}, bf16[2,8,512]{2,1,0:T(8,128)(2,1)S(1)}, u32[]{:S(2)}, u32[]{:S(2)}) %collective-permute-start.6) | collective-permute-done | bytes 16416 | tf_op jit(solution)/shard_map/ppermute | solution.py:325
  98.2 0.0 collective-permute-done.5.far_ref
  98.2 1.3 %shard_map.161 = bf16[2,64,512]{2,1,0:T(8,128)(2,1)} custom-call(s32[1]{0:T(128)} %bitcast.idx_ref, bf16[2,48,512]{2,1,0:T(8,128)(2,1)S(1)} %add_convert_fusion.g_ref, bf16[2,32,512]{2,1,0:T(8,128)(2,1)S(1)} %collective-permute-done.5.far_ref, bf16[2,8,512]{2,1,0:T(8,128)(2,1)S(1)} %collective-permute-done.6.head_ref, bf16[4,64,112]{2,1,0:T(8,128)(2,1)S(1)} %copy-done.8, ...), custom_call_target="tpu_custom_call" | custom-call | flops 100000000 | bytes 1000000 | tf_op jit(solution)/shard_map/pallas_call | solution.py:339
  99.5 0.0 all-to-all-done.1
  99.5 1.3 %shard_map.160 = (bf16[128,512]{1,0:T(8,128)(2,1)}, bf16[128,512]{1,0:T(8,128)(2,1)}) custom-call(s32[1]{0:T(128)} %bitcast.idx_ref, bf16[512,256]{1,0:T(8,128)(2,1)S(1)} %bitcast.14, bf16[512,512]{1,0:T(8,128)(2,1)S(1)} %copy-done.2), custom_call_target="tpu_custom_call" | custom-call | flops 400000000 | bytes 2000000 | tf_op jit(solution)/shard_map/pallas_call | solution.py:326
  (18 shorter events, 0.1 us)
Async XLA Ops:
  0.6 41.7 %copy-start = (bf16[512,512]{1,0:T(8,128)(2,1)S(1)}, bf16[512,512]{1,0:T(8,128)(2,1)}, u32[]{:S(2)}) copy-start(bf16[512,512]{1,0:T(8,128)(2,1)} %constant.31.clone.flip_ref) | copy-start | bytes 1572868
  3.3 23.7 %copy-start.10 = (bf16[2,8,512]{2,1,0:T(8,128)(2,1)S(1)}, bf16[2,8,512]{2,1,0:T(8,128)(2,1)}, u32[]{:S(2)}) copy-start(bf16[2,8,512]{2,1,0:T(8,128)(2,1)} %get-tuple-element.12) | copy-start | bytes 49156
  3.3 39.1 %copy-start.1 = (bf16[2,8,8,512]{3,2,1,0:T(8,128)(2,1)S(1)}, bf16[2,8,8,512]{3,2,1,0:T(8,128)(2,1)}, u32[]{:S(2)}) copy-start(bf16[2,8,8,512]{3,2,1,0:T(8,128)(2,1)} %param.16) | copy-start | bytes 393220
  3.3 39.1 %copy-start.6 = (bf16[3,112,256]{2,1,0:T(8,128)(2,1)S(1)}, bf16[3,112,256]{2,1,0:T(8,128)(2,1)}, u32[]{:S(2)}) copy-start(bf16[3,112,256]{2,1,0:T(8,128)(2,1)} %constant.34.clone.own_ref) | copy-start | bytes 516100
  3.3 39.1 %copy-start.7 = (bf16[3,112,256]{2,1,0:T(8,128)(2,1)S(1)}, bf16[3,112,256]{2,1,0:T(8,128)(2,1)}, u32[]{:S(2)}) copy-start(bf16[3,112,256]{2,1,0:T(8,128)(2,1)} %constant.35.clone.mirror_ref) | copy-start | bytes 516100
  3.3 40.2 %all-to-all-start = ((bf16[64,8,256]{2,1,0:T(8,128)(2,1)}), bf16[64,8,256]{2,1,0:T(8,128)(2,1)S(1)}, u32[]{:S(2)}, u32[]{:S(2)}) async-start(bf16[64,8,256]{2,1,0:T(8,128)(2,1)} %bitcast.15), calls=%async_computation | async-start | bytes 524288 | tf_op jit(solution)/shard_map/all_to_all | solution.py:296
  18.8 23.6 %collective-permute-start = (bf16[2,32,512]{2,1,0:T(8,128)(2,1)}, bf16[2,32,512]{2,1,0:T(8,128)(2,1)S(1)}, u32[]{:S(2)}, u32[]{:S(2)}) collective-permute-start(bf16[2,32,512]{2,1,0:T(8,128)(2,1)} %get-tuple-element.11), channel_id=1, source_target_pairs={{0,63},{1,62},{2,61},{3,60},{4,59},{5,58},{6,57},{7,56},{8,55},{9,... | collective-permute-start | bytes 196616 | tf_op jit(solution)/shard_map/ppermute | solution.py:297
  26.9 16.6 %copy-start.3 = (bf16[512,512]{1,0:T(8,128)(2,1)S(1)}, bf16[512,512]{1,0:T(8,128)(2,1)}, u32[]{:S(2)}) copy-start(bf16[512,512]{1,0:T(8,128)(2,1)} %constant.29.clone.wc_ref) | copy-start | bytes 1572868
  26.9 16.6 %copy-start.4 = (bf16[512,512]{1,0:T(8,128)(2,1)S(1)}, bf16[512,512]{1,0:T(8,128)(2,1)}, u32[]{:S(2)}) copy-start(bf16[512,512]{1,0:T(8,128)(2,1)} %constant.30.clone.ws_ref) | copy-start | bytes 1572868
  27.0 16.6 %copy-start.5 = (f32[2,2,48,256]{3,2,1,0:T(8,128)S(1)}, f32[2,2,48,256]{3,2,1,0:T(8,128)}, u32[]{:S(2)}) copy-start(f32[2,2,48,256]{3,2,1,0:T(8,128)} %constant.38.clone.gather_ref) | copy-start | bytes 589828
  27.0 15.4 %collective-permute-start.1 = (bf16[2,8,512]{2,1,0:T(8,128)(2,1)S(1)}, bf16[2,8,512]{2,1,0:T(8,128)(2,1)S(1)}, u32[]{:S(2)}, u32[]{:S(2)}) collective-permute-start(bf16[2,8,512]{2,1,0:T(8,128)(2,1)S(1)} %copy-done.10), channel_id=1, source_target_pairs={{0,32},{1,63},{2,62},{3,61},{4,60},{5,59},{6,58},{7,57},{8,56},{9,... | collective-permute-start | bytes 49160 | tf_op jit(solution)/shard_map/ppermute | solution.py:298
  47.2 14.3 %collective-permute-start.2 = (bf16[2,48,512]{2,1,0:T(8,128)(2,1)S(1)}, bf16[2,48,512]{2,1,0:T(8,128)(2,1)S(1)}, u32[]{:S(2)}, u32[]{:S(2)}) collective-permute-start(bf16[2,48,512]{2,1,0:T(8,128)(2,1)S(1)} %get-tuple-element.16), channel_id=1, source_target_pairs={{0,64},{64,0},{128,192},{192,128},{256,320},{320,256},{384,448},{4... | collective-permute-start | bytes 294920 | tf_op jit(solution)/shard_map/ppermute | solution.py:321
  51.8 47.7 %all-to-all-start.1 = ((bf16[64,8,256]{2,1,0:T(8,128)(2,1)}), bf16[64,8,256]{2,1,0:T(8,128)(2,1)S(1)}, u32[]{:S(2)}, u32[]{:S(2)}) async-start(bf16[64,8,256]{2,1,0:T(8,128)(2,1)} %bitcast.6), calls=%async_computation.1 | async-start | bytes 524288 | tf_op jit(solution)/shard_map/all_to_all | solution.py:319
  61.6 6.7 %collective-permute-start.3 = (bf16[2,48,512]{2,1,0:T(8,128)(2,1)S(1)}, bf16[2,48,512]{2,1,0:T(8,128)(2,1)S(1)}, u32[]{:S(2)}, u32[]{:S(2)}) collective-permute-start(bf16[2,48,512]{2,1,0:T(8,128)(2,1)S(1)} %add_convert_fusion.2), channel_id=1, source_target_pairs={{0,128},{64,192},{128,0},{192,64},{256,384},{320,448},{384,256},{4... | collective-permute-start | bytes 294920 | tf_op jit(solution)/shard_map/ppermute | solution.py:321
  68.3 8.0 %collective-permute-start.4 = (bf16[2,48,512]{2,1,0:T(8,128)(2,1)S(1)}, bf16[2,48,512]{2,1,0:T(8,128)(2,1)S(1)}, u32[]{:S(2)}, u32[]{:S(2)}) collective-permute-start(bf16[2,48,512]{2,1,0:T(8,128)(2,1)S(1)} %add_convert_fusion.1), channel_id=1, source_target_pairs={{0,256},{64,320},{128,384},{192,448},{256,0},{320,64},{384,128},{4... | collective-permute-start | bytes 294920 | tf_op jit(solution)/shard_map/ppermute | solution.py:321
  76.3 21.9 %copy-start.8 = (bf16[4,64,112]{2,1,0:T(8,128)(2,1)S(1)}, bf16[4,64,112]{2,1,0:T(8,128)(2,1)}, u32[]{:S(2)}) copy-start(bf16[4,64,112]{2,1,0:T(8,128)(2,1)} %constant.36.clone.own_ref) | copy-start | bytes 172036
  76.4 21.9 %copy-start.9 = (bf16[4,64,112]{2,1,0:T(8,128)(2,1)S(1)}, bf16[4,64,112]{2,1,0:T(8,128)(2,1)}, u32[]{:S(2)}) copy-start(bf16[4,64,112]{2,1,0:T(8,128)(2,1)} %constant.37.clone.mirror_ref) | copy-start | bytes 172036
  76.4 23.2 %copy-start.2 = (bf16[512,512]{1,0:T(8,128)(2,1)S(1)}, bf16[512,512]{1,0:T(8,128)(2,1)}, u32[]{:S(2)}) copy-start(bf16[512,512]{1,0:T(8,128)(2,1)} %constant.28.clone.t_ref) | copy-start | bytes 1572868
  76.4 21.8 %collective-permute-start.5 = (bf16[2,32,512]{2,1,0:T(8,128)(2,1)S(1)}, bf16[2,32,512]{2,1,0:T(8,128)(2,1)S(1)}, u32[]{:S(2)}, u32[]{:S(2)}) collective-permute-start(bf16[2,32,512]{2,1,0:T(8,128)(2,1)S(1)} %slice.12), channel_id=1, source_target_pairs={{0,63},{1,62},{2,61},{3,60},{4,59},{5,58},{6,57},{7,56},{8,55},{9,... | collective-permute-start | bytes 196616 | tf_op jit(solution)/shard_map/ppermute | solution.py:323
  83.0 15.2 %collective-permute-start.6 = (bf16[2,8,512]{2,1,0:T(8,128)(2,1)S(1)}, bf16[2,8,512]{2,1,0:T(8,128)(2,1)S(1)}, u32[]{:S(2)}, u32[]{:S(2)}) collective-permute-start(bf16[2,8,512]{2,1,0:T(8,128)(2,1)S(1)} %slice_select_fusion), channel_id=1, source_target_pairs={{0,32},{1,63},{2,62},{3,61},{4,60},{5,59},{6,58},{7,57},{8,56},{9,... | collective-permute-start | bytes 49160 | tf_op jit(solution)/shard_map/ppermute | solution.py:325

commit v4 on v3

--- a/solution.py
+++ b/solution.py
@@ -78,7 +78,7 @@
                     out[first, ri, slot[lane] * 8 + filt[lane], lane] = sign
                 if extra:
                     out[first, ri, 32 + filt[lane], lane] = sign
-    return out
+    return out.astype(BF)
 
 
 def grad_selectors():
@@ -205,9 +205,11 @@
             pairs.append((pltpu.roll(x, 112, 1) * x, pltpu.roll(x, 48, 1) * x))
         for ri in range(2):
             terms = jnp.concatenate([pairs[0][ri], pairs[1][ri]], axis=1)
-            g_ref[ri, :, at] = dot(
-                gather_ref[first, ri], terms, ((1,), (1,)), lax.Precision.HIGHEST
-            ).astype(BF)
+            high = terms.astype(BF)
+            low = (terms - high.astype(F32)).astype(BF)
+            take = gather_ref[first, ri]
+            total = dot(take, high, ((1,), (1,))) + dot(take, low, ((1,), (1,)))
+            g_ref[ri, :, at] = total.astype(BF)
     for k in range(4):
         at = pl.ds(k * 128, 128)
         q1 = dot(wc_ref[at, :], prod[...])
@@ -316,13 +318,22 @@
         scratch_shapes=[pltpu.VMEM((N, HALF), BF)],
         compiler_params=PARAMS,
     )(place, got.reshape(N, HALF), cos_t, sin_t, spread, gather)
-    mid = lax.all_to_all(back.reshape(SEQ, ROWS, HALF), "seq", 0, 0, tiled=True)
-    for bit in (1, 2, 4):
-        other = lax.ppermute(grad, "dp", [(d, d ^ bit) for d in range(8)])
-        grad = (grad.astype(F32) + other.astype(F32)).astype(BF)
     far = lax.ppermute(grad[:, :32], "seq", opposite)
     slot = jnp.where(place[0] == 0, grad[:, 32:40], grad[:, :8])
     slot = lax.ppermute(slot, "seq", heads_to)
+    mid = lax.all_to_all(back.reshape(SEQ, ROWS, HALF), "seq", 0, 0, tiled=True)
+    grad = pl.pallas_call(
+        kernel_g,
+        in_specs=[SMEM] + [VMEM] * 6,
+        out_specs=VMEM,
+        out_shape=jax.ShapeDtypeStruct((2, 64, N), BF),
+        scratch_shapes=[pltpu.VMEM((2, 112, N), BF)],
+        compiler_params=PARAMS,
+        cost_estimate=pl.CostEstimate(flops=100000000, bytes_accessed=1000000, transcendentals=0),
+    )(place, grad, far, slot, g_own, g_mirror, flip)
+    for bit in (2, 4, 1):
+        other = lax.ppermute(grad, "dp", [(d, d ^ bit) for d in range(8)])
+        grad = (grad.astype(F32) + other.astype(F32)).astype(BF)
     output, grad_signal = pl.pallas_call(
         kernel_c,
         in_specs=[SMEM, VMEM, VMEM],
@@ -336,16 +347,7 @@
         compiler_params=PARAMS,
         cost_estimate=pl.CostEstimate(flops=400000000, bytes_accessed=2000000, transcendentals=0),
     )(place, mid.reshape(N, HALF), table)
-    grad_filter = pl.pallas_call(
-        kernel_g,
-        in_specs=[SMEM] + [VMEM] * 6,
-        out_specs=VMEM,
-        out_shape=jax.ShapeDtypeStruct((2, 64, N), BF),
-        scratch_shapes=[pltpu.VMEM((2, 112, N), BF)],
-        compiler_params=PARAMS,
-        cost_estimate=pl.CostEstimate(flops=100000000, bytes_accessed=1000000, transcendentals=0),
-    )(place, grad, far, slot, g_own, g_mirror, flip)
-    return output.reshape(shape), grad_signal.reshape(shape), grad_filter.reshape(2, 8, 8, N)
+    return output.reshape(shape), grad_signal.reshape(shape), grad.reshape(2, 8, 8, N)
 
 
 def solution(mesh):

time: 101 us -> 105 us (1.040)
  the two profiles are of different devices: /device:TPU:144 before, /device:TPU:1 now
where the time goes in v4:
time: 105 us; the launch traced here: 104 us
  starting transfers between devices  64 us (61%)
  waiting for transfers between devices  30 us (29%)
  Pallas kernels  8.62 us (8%)
    all_to_all x1, starting transfers between devices, body(): mid = lax.all_to_all(back.reshape(SEQ, ROWS, HALF), 'seq', 0, 0, tiled=True)  20.1 us
    all_to_all x1, starting transfers between devices, body(): got = lax.all_to_all(sent.reshape(SEQ, ROWS, HALF), 'seq', 0, 0, tiled=True)  18.2 us
    ppermute x1, waiting for transfers between devices, body(): heads = lax.ppermute(heads, 'seq', heads_to)  14.1 us
    ppermute x3, starting transfers between devices, body(): other = lax.ppermute(grad, 'dp', [(d, d ^ bit) for d in range(8)])  12.2 us
    ppermute x3, waiting for transfers between devices, body(): other = lax.ppermute(grad, 'dp', [(d, d ^ bit) for d in range(8)])  6.8 us
    ppermute x1, starting transfers between devices, body(): tails = lax.ppermute(tails, 'seq', opposite)  5.95 us
    all_to_all x1, waiting for transfers between devices, body(): mid = lax.all_to_all(back.reshape(SEQ, ROWS, HALF), 'seq', 0, 0, tiled=True)  5.61 us
    ppermute x1, starting transfers between devices, body(): slot = lax.ppermute(slot, 'seq', heads_to)  3.56 us
  transfers between devices with their start and end apart: 9, of which 6 were waited for; matrix products, arithmetic and copies ran while one was open for 1% of the time, Pallas kernels for 1%

profile of v4, /device:TPU:1, one launch (start us, length us, event | category | flops | bytes accessed | tf_op | source)
XLA Modules:
  0.0 104.3 jit_solution(17074230335777050562)
XLA Ops:
  0.6 0.0 copy-start
  0.6 2.6 %shard_map.157 = (bf16[512,256]{1,0:T(8,128)(2,1)}, bf16[2,32,512]{2,1,0:T(8,128)(2,1)}, bf16[2,8,512]{2,1,0:T(8,128)(2,1)}) custom-call(s32[1]{0:T(128)} %bitcast.idx_ref, bf16[128,512]{1,0:T(8,128)(2,1)} %bitcast.17, bf16[128,512]{1,0:T(8,128)(2,1)} %bitcast.18, bf16[512,512]{1,0:T(8,128)(2,1)} %constant.28.clone.t_ref, bf16[2,64,512]{2,1,0:T(8,128)(2,1)} %bitcast.13, ...), custom_call_target="tpu_custom_call" | custom-call | tf_op jit(solution)/shard_map/pallas_call | solution.py:283
  3.3 0.0 copy-start.6
  3.3 18.2 %all-to-all-start = ((bf16[64,8,256]{2,1,0:T(8,128)(2,1)}), bf16[64,8,256]{2,1,0:T(8,128)(2,1)S(1)}, u32[]{:S(2)}, u32[]{:S(2)}) async-start(bf16[64,8,256]{2,1,0:T(8,128)(2,1)} %bitcast.16), calls=%async_computation | async-start | bytes 524288 | tf_op jit(solution)/shard_map/all_to_all | solution.py:298
  21.5 6.0 %collective-permute-start = (bf16[2,32,512]{2,1,0:T(8,128)(2,1)}, bf16[2,32,512]{2,1,0:T(8,128)(2,1)S(1)}, u32[]{:S(2)}, u32[]{:S(2)}) collective-permute-start(bf16[2,32,512]{2,1,0:T(8,128)(2,1)} %get-tuple-element.11), channel_id=1, source_target_pairs={{0,63},{1,62},{2,61},{3,60},{4,59},{5,58},{6,57},{7,56},{8,55},{9,... | collective-permute-start | bytes 196616 | tf_op jit(solution)/shard_map/ppermute | solution.py:299
  27.5 0.0 copy-done.10
  27.5 1.9 %collective-permute-start.1 = (bf16[2,8,512]{2,1,0:T(8,128)(2,1)S(1)}, bf16[2,8,512]{2,1,0:T(8,128)(2,1)S(1)}, u32[]{:S(2)}, u32[]{:S(2)}) collective-permute-start(bf16[2,8,512]{2,1,0:T(8,128)(2,1)S(1)} %copy-done.10), channel_id=1, source_target_pairs={{0,32},{1,63},{2,62},{3,61},{4,60},{5,59},{6,58},{7,57},{8,56},{9,... | collective-permute-start | bytes 49160 | tf_op jit(solution)/shard_map/ppermute | solution.py:300
  29.4 0.0 copy-start.3
  29.4 0.0 copy-start.4
  29.4 0.0 copy-start.7
  29.4 14.1 %collective-permute-done.1.head_ref = bf16[2,8,512]{2,1,0:T(8,128)(2,1)S(1)} collective-permute-done((bf16[2,8,512]{2,1,0:T(8,128)(2,1)S(1)}, bf16[2,8,512]{2,1,0:T(8,128)(2,1)S(1)}, u32[]{:S(2)}, u32[]{:S(2)}) %collective-permute-start.1) | collective-permute-done | bytes 16416 | tf_op jit(solution)/shard_map/ppermute | solution.py:300
  43.5 0.4 collective-permute-done.tail_ref
  44.0 1.1 %shard_map.158.h_ref = f32[512,512]{1,0:T(8,128)S(1)} custom-call(s32[1]{0:T(128)} %bitcast.idx_ref, bf16[2,64,512]{2,1,0:T(8,128)(2,1)S(1)} %bitcast.14, bf16[2,32,512]{2,1,0:T(8,128)(2,1)S(1)} %collective-permute-done.tail_ref, bf16[2,8,512]{2,1,0:T(8,128)(2,1)S(1)} %collective-permute-done.1.head_ref, bf16[3,112,256]{2,1,0:T(8,128)(2,1)S(1)} %copy-done.5, ...), custom_call_target="tpu_custom_call" | custom-call | flops 400000000 | bytes 2000000 | tf_op jit(solution)/shard_map/pallas_call | solution.py:301
  45.1 0.0 all-to-all-done
  45.2 2.9 %shard_map.159 = (bf16[512,256]{1,0:T(8,128)(2,1)}, bf16[2,48,512]{2,1,0:T(8,128)(2,1)S(1)}) custom-call(s32[1]{0:T(128)} %bitcast.idx_ref, bf16[512,256]{1,0:T(8,128)(2,1)S(1)} %bitcast.12, bf16[512,512]{1,0:T(8,128)(2,1)S(1)} %copy-done.3, bf16[512,512]{1,0:T(8,128)(2,1)S(1)} %copy-done.4, f32[512,512]{1,0:T(8,128)S(1)} %shard_map.158.h_ref, ...), custom_call_target="tpu_custom_call" | custom-call | tf_op jit(solution)/shard_map/pallas_call | solution.py:310
  48.1 2.1 %collective-permute-start.2 = (bf16[2,32,512]{2,1,0:T(8,128)(2,1)S(1)}, bf16[2,32,512]{2,1,0:T(8,128)(2,1)S(1)}, u32[]{:S(2)}, u32[]{:S(2)}) collective-permute-start(bf16[2,32,512]{2,1,0:T(8,128)(2,1)S(1)} %slice.9), channel_id=1, source_target_pairs={{0,63},{1,62},{2,61},{3,60},{4,59},{5,58},{6,57},{7,56},{8,55},{9,... | collective-permute-start | bytes 196616 | tf_op jit(solution)/shard_map/ppermute | solution.py:321
  50.2 3.6 %collective-permute-start.3 = (bf16[2,8,512]{2,1,0:T(8,128)(2,1)S(1)}, bf16[2,8,512]{2,1,0:T(8,128)(2,1)S(1)}, u32[]{:S(2)}, u32[]{:S(2)}) collective-permute-start(bf16[2,8,512]{2,1,0:T(8,128)(2,1)S(1)} %slice_select_fusion), channel_id=1, source_target_pairs={{0,32},{1,63},{2,62},{3,61},{4,60},{5,59},{6,58},{7,57},{8,56},{9,... | collective-permute-start | bytes 49160 | tf_op jit(solution)/shard_map/ppermute | solution.py:323
  53.8 3.0 %collective-permute-done.3.head_ref = bf16[2,8,512]{2,1,0:T(8,128)(2,1)S(1)} collective-permute-done((bf16[2,8,512]{2,1,0:T(8,128)(2,1)S(1)}, bf16[2,8,512]{2,1,0:T(8,128)(2,1)S(1)}, u32[]{:S(2)}, u32[]{:S(2)}) %collective-permute-start.3) | collective-permute-done | bytes 16416 | tf_op jit(solution)/shard_map/ppermute | solution.py:323
  56.8 0.0 collective-permute-done.2.far_ref
  56.8 0.0 copy-done.8
  56.8 0.6 shard_map.161
  57.5 3.2 %collective-permute-start.4 = (bf16[2,64,512]{2,1,0:T(8,128)(2,1)S(1)}, bf16[2,64,512]{2,1,0:T(8,128)(2,1)S(1)}, u32[]{:S(2)}, u32[]{:S(2)}) collective-permute-start(bf16[2,64,512]{2,1,0:T(8,128)(2,1)S(1)} %shard_map.161), channel_id=1, source_target_pairs={{0,128},{64,192},{128,0},{192,64},{256,384},{320,448},{384,256},{4... | collective-permute-start | bytes 393224 | tf_op jit(solution)/shard_map/ppermute | solution.py:335
  60.7 20.1 %all-to-all-start.1 = ((bf16[64,8,256]{2,1,0:T(8,128)(2,1)}), bf16[64,8,256]{2,1,0:T(8,128)(2,1)S(1)}, u32[]{:S(2)}, u32[]{:S(2)}) async-start(bf16[64,8,256]{2,1,0:T(8,128)(2,1)} %bitcast.6), calls=%async_computation.1 | async-start | bytes 524288 | tf_op jit(solution)/shard_map/all_to_all | solution.py:324
  80.7 0.0 copy-start.2
  80.8 0.0 collective-permute-done.4
  80.8 4.7 %collective-permute-start.5 = (bf16[2,64,512]{2,1,0:T(8,128)(2,1)S(1)}, bf16[2,64,512]{2,1,0:T(8,128)(2,1)S(1)}, u32[]{:S(2)}, u32[]{:S(2)}) collective-permute-start(bf16[2,64,512]{2,1,0:T(8,128)(2,1)S(1)} %add_convert_fusion.2), channel_id=1, source_target_pairs={{0,256},{64,320},{128,384},{192,448},{256,0},{320,64},{384,128},{4... | collective-permute-start | bytes 393224 | tf_op jit(solution)/shard_map/ppermute | solution.py:335
  85.5 3.5 %collective-permute-done.5 = bf16[2,64,512]{2,1,0:T(8,128)(2,1)S(1)} collective-permute-done((bf16[2,64,512]{2,1,0:T(8,128)(2,1)S(1)}, bf16[2,64,512]{2,1,0:T(8,128)(2,1)S(1)}, u32[]{:S(2)}, u32[]{:S(2)}) %collective-permute-start.5) | collective-permute-done | bytes 131104 | tf_op jit(solution)/shard_map/ppermute | solution.py:335
  89.0 4.4 %collective-permute-start.6 = (bf16[2,64,512]{2,1,0:T(8,128)(2,1)S(1)}, bf16[2,64,512]{2,1,0:T(8,128)(2,1)S(1)}, u32[]{:S(2)}, u32[]{:S(2)}) collective-permute-start(bf16[2,64,512]{2,1,0:T(8,128)(2,1)S(1)} %add_convert_fusion.1), channel_id=1, source_target_pairs={{0,64},{64,0},{128,192},{192,128},{256,320},{320,256},{384,448},{4... | collective-permute-start | bytes 393224 | tf_op jit(solution)/shard_map/ppermute | solution.py:335
  93.3 3.3 %collective-permute-done.6 = bf16[2,64,512]{2,1,0:T(8,128)(2,1)S(1)} collective-permute-done((bf16[2,64,512]{2,1,0:T(8,128)(2,1)S(1)}, bf16[2,64,512]{2,1,0:T(8,128)(2,1)S(1)}, u32[]{:S(2)}, u32[]{:S(2)}) %collective-permute-start.6) | collective-permute-done | bytes 131104 | tf_op jit(solution)/shard_map/ppermute | solution.py:335
  96.7 0.7 fusion
  97.4 5.6 %all-to-all-done.1 = bf16[64,8,256]{2,1,0:T(8,128)(2,1)S(1)} async-done(((bf16[64,8,256]{2,1,0:T(8,128)(2,1)}), bf16[64,8,256]{2,1,0:T(8,128)(2,1)S(1)}, u32[]{:S(2)}, u32[]{:S(2)}) %all-to-all-start.1) | async-done | bytes 262176 | tf_op jit(solution)/shard_map/all_to_all | solution.py:324
  103.0 1.3 %shard_map.160 = (bf16[128,512]{1,0:T(8,128)(2,1)}, bf16[128,512]{1,0:T(8,128)(2,1)}) custom-call(s32[1]{0:T(128)} %bitcast.idx_ref, bf16[512,256]{1,0:T(8,128)(2,1)S(1)} %bitcast.15, bf16[512,512]{1,0:T(8,128)(2,1)S(1)} %copy-done.2), custom_call_target="tpu_custom_call" | custom-call | flops 400000000 | bytes 2000000 | tf_op jit(solution)/shard_map/pallas_call | solution.py:337
  (18 shorter events, 0.1 us)
Async XLA Ops:
  0.6 43.3 %copy-start = (bf16[512,512]{1,0:T(8,128)(2,1)S(1)}, bf16[512,512]{1,0:T(8,128)(2,1)}, u32[]{:S(2)}) copy-start(bf16[512,512]{1,0:T(8,128)(2,1)} %constant.31.clone.flip_ref) | copy-start | bytes 1572868
  3.3 24.2 %copy-start.10 = (bf16[2,8,512]{2,1,0:T(8,128)(2,1)S(1)}, bf16[2,8,512]{2,1,0:T(8,128)(2,1)}, u32[]{:S(2)}) copy-start(bf16[2,8,512]{2,1,0:T(8,128)(2,1)} %get-tuple-element.12) | copy-start | bytes 49156
  3.3 40.7 %copy-start.1 = (bf16[2,8,8,512]{3,2,1,0:T(8,128)(2,1)S(1)}, bf16[2,8,8,512]{3,2,1,0:T(8,128)(2,1)}, u32[]{:S(2)}) copy-start(bf16[2,8,8,512]{3,2,1,0:T(8,128)(2,1)} %param.16) | copy-start | bytes 393220
  3.3 40.7 %copy-start.5 = (bf16[3,112,256]{2,1,0:T(8,128)(2,1)S(1)}, bf16[3,112,256]{2,1,0:T(8,128)(2,1)}, u32[]{:S(2)}) copy-start(bf16[3,112,256]{2,1,0:T(8,128)(2,1)} %constant.34.clone.own_ref) | copy-start | bytes 516100
  3.3 40.7 %copy-start.6 = (bf16[3,112,256]{2,1,0:T(8,128)(2,1)S(1)}, bf16[3,112,256]{2,1,0:T(8,128)(2,1)}, u32[]{:S(2)}) copy-start(bf16[3,112,256]{2,1,0:T(8,128)(2,1)} %constant.35.clone.mirror_ref) | copy-start | bytes 516100
  3.3 41.8 %all-to-all-start = ((bf16[64,8,256]{2,1,0:T(8,128)(2,1)}), bf16[64,8,256]{2,1,0:T(8,128)(2,1)S(1)}, u32[]{:S(2)}, u32[]{:S(2)}) async-start(bf16[64,8,256]{2,1,0:T(8,128)(2,1)} %bitcast.16), calls=%async_computation | async-start | bytes 524288 | tf_op jit(solution)/shard_map/all_to_all | solution.py:298
  21.5 22.5 %collective-permute-start = (bf16[2,32,512]{2,1,0:T(8,128)(2,1)}, bf16[2,32,512]{2,1,0:T(8,128)(2,1)S(1)}, u32[]{:S(2)}, u32[]{:S(2)}) collective-permute-start(bf16[2,32,512]{2,1,0:T(8,128)(2,1)} %get-tuple-element.11), channel_id=1, source_target_pairs={{0,63},{1,62},{2,61},{3,60},{4,59},{5,58},{6,57},{7,56},{8,55},{9,... | collective-permute-start | bytes 196616 | tf_op jit(solution)/shard_map/ppermute | solution.py:299
  27.5 16.1 %collective-permute-start.1 = (bf16[2,8,512]{2,1,0:T(8,128)(2,1)S(1)}, bf16[2,8,512]{2,1,0:T(8,128)(2,1)S(1)}, u32[]{:S(2)}, u32[]{:S(2)}) collective-permute-start(bf16[2,8,512]{2,1,0:T(8,128)(2,1)S(1)} %copy-done.10), channel_id=1, source_target_pairs={{0,32},{1,63},{2,62},{3,61},{4,60},{5,59},{6,58},{7,57},{8,56},{9,... | collective-permute-start | bytes 49160 | tf_op jit(solution)/shard_map/ppermute | solution.py:300
  29.4 15.7 %copy-start.3 = (bf16[512,512]{1,0:T(8,128)(2,1)S(1)}, bf16[512,512]{1,0:T(8,128)(2,1)}, u32[]{:S(2)}) copy-start(bf16[512,512]{1,0:T(8,128)(2,1)} %constant.29.clone.wc_ref) | copy-start | bytes 1572868
  29.4 15.7 %copy-start.4 = (bf16[512,512]{1,0:T(8,128)(2,1)S(1)}, bf16[512,512]{1,0:T(8,128)(2,1)}, u32[]{:S(2)}) copy-start(bf16[512,512]{1,0:T(8,128)(2,1)} %constant.30.clone.ws_ref) | copy-start | bytes 1572868
  29.4 15.7 %copy-start.7 = (bf16[2,2,48,256]{3,2,1,0:T(8,128)(2,1)S(1)}, bf16[2,2,48,256]{3,2,1,0:T(8,128)(2,1)}, u32[]{:S(2)}) copy-start(bf16[2,2,48,256]{3,2,1,0:T(8,128)(2,1)} %constant.38.clone.gather_ref) | copy-start | bytes 294916
  48.1 8.7 %copy-start.8 = (bf16[4,64,112]{2,1,0:T(8,128)(2,1)S(1)}, bf16[4,64,112]{2,1,0:T(8,128)(2,1)}, u32[]{:S(2)}) copy-start(bf16[4,64,112]{2,1,0:T(8,128)(2,1)} %constant.36.clone.own_ref) | copy-start | bytes 172036
  48.1 8.7 %copy-start.9 = (bf16[4,64,112]{2,1,0:T(8,128)(2,1)S(1)}, bf16[4,64,112]{2,1,0:T(8,128)(2,1)}, u32[]{:S(2)}) copy-start(bf16[4,64,112]{2,1,0:T(8,128)(2,1)} %constant.37.clone.mirror_ref) | copy-start | bytes 172036
  48.1 8.7 %collective-permute-start.2 = (bf16[2,32,512]{2,1,0:T(8,128)(2,1)S(1)}, bf16[2,32,512]{2,1,0:T(8,128)(2,1)S(1)}, u32[]{:S(2)}, u32[]{:S(2)}) collective-permute-start(bf16[2,32,512]{2,1,0:T(8,128)(2,1)S(1)} %slice.9), channel_id=1, source_target_pairs={{0,63},{1,62},{2,61},{3,60},{4,59},{5,58},{6,57},{7,56},{8,55},{9,... | collective-permute-start | bytes 196616 | tf_op jit(solution)/shard_map/ppermute | solution.py:321
  50.2 6.6 %collective-permute-start.3 = (bf16[2,8,512]{2,1,0:T(8,128)(2,1)S(1)}, bf16[2,8,512]{2,1,0:T(8,128)(2,1)S(1)}, u32[]{:S(2)}, u32[]{:S(2)}) collective-permute-start(bf16[2,8,512]{2,1,0:T(8,128)(2,1)S(1)} %slice_select_fusion), channel_id=1, source_target_pairs={{0,32},{1,63},{2,62},{3,61},{4,60},{5,59},{6,58},{7,57},{8,56},{9,... | collective-permute-start | bytes 49160 | tf_op jit(solution)/shard_map/ppermute | solution.py:323
  57.5 23.3 %collective-permute-start.4 = (bf16[2,64,512]{2,1,0:T(8,128)(2,1)S(1)}, bf16[2,64,512]{2,1,0:T(8,128)(2,1)S(1)}, u32[]{:S(2)}, u32[]{:S(2)}) collective-permute-start(bf16[2,64,512]{2,1,0:T(8,128)(2,1)S(1)} %shard_map.161), channel_id=1, source_target_pairs={{0,128},{64,192},{128,0},{192,64},{256,384},{320,448},{384,256},{4... | collective-permute-start | bytes 393224 | tf_op jit(solution)/shard_map/ppermute | solution.py:335
  60.7 42.3 %all-to-all-start.1 = ((bf16[64,8,256]{2,1,0:T(8,128)(2,1)}), bf16[64,8,256]{2,1,0:T(8,128)(2,1)S(1)}, u32[]{:S(2)}, u32[]{:S(2)}) async-start(bf16[64,8,256]{2,1,0:T(8,128)(2,1)} %bitcast.6), calls=%async_computation.1 | async-start | bytes 524288 | tf_op jit(solution)/shard_map/all_to_all | solution.py:324
  80.7 22.2 %copy-start.2 = (bf16[512,512]{1,0:T(8,128)(2,1)S(1)}, bf16[512,512]{1,0:T(8,128)(2,1)}, u32[]{:S(2)}) copy-start(bf16[512,512]{1,0:T(8,128)(2,1)} %constant.28.clone.t_ref) | copy-start | bytes 1572868
  80.8 8.1 %collective-permute-start.5 = (bf16[2,64,512]{2,1,0:T(8,128)(2,1)S(1)}, bf16[2,64,512]{2,1,0:T(8,128)(2,1)S(1)}, u32[]{:S(2)}, u32[]{:S(2)}) collective-permute-start(bf16[2,64,512]{2,1,0:T(8,128)(2,1)S(1)} %add_convert_fusion.2), channel_id=1, source_target_pairs={{0,256},{64,320},{128,384},{192,448},{256,0},{320,64},{384,128},{4... | collective-permute-start | bytes 393224 | tf_op jit(solution)/shard_map/ppermute | solution.py:335
  89.0 7.7 %collective-permute-start.6 = (bf16[2,64,512]{2,1,0:T(8,128)(2,1)S(1)}, bf16[2,64,512]{2,1,0:T(8,128)(2,1)S(1)}, u32[]{:S(2)}, u32[]{:S(2)}) collective-permute-start(bf16[2,64,512]{2,1,0:T(8,128)(2,1)S(1)} %add_convert_fusion.1), channel_id=1, source_target_pairs={{0,64},{64,0},{128,192},{192,128},{256,320},{320,256},{384,448},{4... | collective-permute-start | bytes 393224 | tf_op jit(solution)/shard_map/ppermute | solution.py:335

commit v5 on v4

--- a/solution.py
+++ b/solution.py
@@ -44,21 +44,29 @@
     return slot, lane // 64 % 2, lane // 16 % 2, lane // 2 % 8, lane % 2
 
 
+def tail_row(f, row):
+    return 64 + 16 * (f // 2) + 4 * (f % 2) + row - 4
+
+
+def head_row(f):
+    return 72 + 16 * (f // 2) + f % 2
+
+
 def filter_selectors():
     slot, _, _, filt, chan = lanes()
-    own = np.zeros((3, 112, HALF), np.float32)
-    mirror = np.zeros((3, 112, HALF), np.float32)
+    own = np.zeros((3, 128, HALF), np.float32)
+    mirror = np.zeros((3, 128, HALF), np.float32)
     for lane in range(HALF):
         k, f = slot[lane], filt[lane]
         for kind in (0, 1):
             own[kind, f * 8 + k, lane] = 0.5
-            mirror[kind, 96 + f if k == 0 else 64 + f * 4 + 4 - k, lane] = 0.5
+            mirror[kind, head_row(f) if k == 0 else tail_row(f, 8 - k), lane] = 0.5
         own[2, f * 8 + k + 1, lane] = 0.5
-        mirror[2, 64 + f * 4 + 3 - k, lane] = 0.5
+        mirror[2, tail_row(f, 7 - k), lane] = 0.5
         if k == 0:
             own[0, :, lane] = 0
             mirror[0, :, lane] = 0
-            source = 96 + f if chan[lane] else f * 8
+            source = head_row(f) if chan[lane] else f * 8
             own[0, source, lane] = 0.5
             mirror[0, source, lane] = 0.5
     return own.astype(BF), mirror.astype(BF)
@@ -107,13 +115,12 @@
 
 
 def payload_selectors():
-    tail = np.zeros((32, 64), np.float32)
-    head = np.zeros((8, 64), np.float32)
+    out = np.zeros((2, 4, 8, 64), np.float32)
     for f in range(8):
-        head[f, f * 8] = 1
+        out[1, f // 2, f % 2, f * 8] = 1
         for row in range(4):
-            tail[f * 4 + row, f * 8 + 4 + row] = 1
-    return tail.astype(BF), head.astype(BF)
+            out[0, f // 2, 4 * (f % 2) + row, f * 8 + 4 + row] = 1
+    return out.astype(BF)
 
 
 def dot(a, b, dims=((1,), (0,)), precision=None):
@@ -137,11 +144,12 @@
     return (re[0], jnp.where(first, im[0], re[1])), (jnp.where(first, re[1], im[0]), im[1])
 
 
-def kernel_a(idx_ref, sig_ref, cot_ref, t_ref, f_ref, tail_ref, head_ref, out_ref, tails_ref,
-             heads_ref, yre, yim, z):
+def kernel_a(idx_ref, rank_ref, sig_ref, cot_ref, t_ref, f_ref, pick_ref, out_ref, tails_ref, heads_ref,
+             yre, yim, z):
+    pair = rank_ref[0] >> 1
     for ri in range(2):
-        tails_ref[ri] = dot(tail_ref[...], f_ref[ri]).astype(BF)
-        heads_ref[ri] = dot(head_ref[...], f_ref[ri]).astype(BF)
+        tails_ref[ri] = dot(pick_ref[0, pair], f_ref[ri]).astype(BF)
+        heads_ref[ri] = dot(pick_ref[1, pair], f_ref[ri]).astype(BF)
     turns = [turn(idx_ref, chan) for chan in range(2)]
     for half, ref in enumerate((sig_ref, cot_ref)):
         x = ref[...]
@@ -164,13 +172,13 @@
         out_ref[:, p * 128 : (p + 1) * 128] = z[p].astype(BF)
 
 
-def kernel_f(idx_ref, f_ref, tail_ref, head_ref, own_ref, mirror_ref, flip_ref, h_ref, rows):
+def kernel_f(idx_ref, rank_ref, f_ref, s0_ref, s1_ref, s2_ref, s3_ref, own_ref, mirror_ref, flip_ref, h_ref, rows):
     place = idx_ref[0]
     kind = jnp.where(place == 0, 0, jnp.where(place < 32, 1, 2))
     rows[:, :64, :] = f_ref[...]
-    rows[:, 64:96, :] = tail_ref[...]
-    rows[:, 96:, :] = jnp.zeros((2, 16, N), BF)
-    rows[:, 96:104, :] = head_ref[...]
+    for k, share_ref in enumerate((s0_ref, s1_ref, s2_ref, s3_ref)):
+        at = pl.multiple_of(64 + 16 * ((rank_ref[0] >> 1) ^ k), 16)
+        rows[:, pl.ds(at, 16), :] = share_ref[...]
     lane = lax.broadcasted_iota(jnp.int32, (N, HALF), 1)
     shifted = ((lane & ~30) == 0) | ((lane & ~30) == 64)
     shifted = shifted & (place == 0)
@@ -187,9 +195,13 @@
             h_ref[:, HALF:] = jnp.where(negative, -value, value)
 
 
-def kernel_b(idx_ref, r_ref, wc_ref, ws_ref, h_ref, gather_ref, v_ref, g_ref, prod):
+def signs():
+    return jnp.where(lax.broadcasted_iota(jnp.int32, (128, 128), 1) < 64, -1.0, 1.0)
+
+
+def kernel_b(idx_ref, r_ref, wc_ref, ws_ref, gather_ref, x_ref, g_ref):
     first = jnp.where(idx_ref[0] == 0, 1, 0)
-    sign = jnp.where(lax.broadcasted_iota(jnp.int32, (128, 128), 1) < 64, -1.0, 1.0)
+    sign = signs()
     for k in range(4):
         at = pl.ds(k * 128, 128)
         p1 = dot(wc_ref[at, :], r_ref[...])
@@ -198,10 +210,7 @@
         for p in range(2):
             cols = slice(p * 128, (p + 1) * 128)
             x = p1[:, cols] + sign * pltpu.roll(p2[:, cols], 64, 1)
-            swapped = pltpu.roll(x, 64, 1)
-            h1 = h_ref[at, p * 128 : (p + 1) * 128]
-            h2 = h_ref[at, HALF + p * 128 : HALF + (p + 1) * 128]
-            prod[at, cols] = (h1 * x + h2 * swapped).astype(BF)
+            x_ref[at, cols] = x
             pairs.append((pltpu.roll(x, 112, 1) * x, pltpu.roll(x, 48, 1) * x))
         for ri in range(2):
             terms = jnp.concatenate([pairs[0][ri], pairs[1][ri]], axis=1)
@@ -210,6 +219,18 @@
             take = gather_ref[first, ri]
             total = dot(take, high, ((1,), (1,))) + dot(take, low, ((1,), (1,)))
             g_ref[ri, :, at] = total.astype(BF)
+
+
+def kernel_d(x_ref, wc_ref, ws_ref, h_ref, v_ref, prod):
+    sign = signs()
+    for k in range(4):
+        at = pl.ds(k * 128, 128)
+        for p in range(2):
+            cols = slice(p * 128, (p + 1) * 128)
+            x = x_ref[at, cols]
+            h1 = h_ref[at, cols]
+            h2 = h_ref[at, HALF + p * 128 : HALF + (p + 1) * 128]
+            prod[at, cols] = (h1 * x + h2 * pltpu.roll(x, 64, 1)).astype(BF)
     for k in range(4):
         at = pl.ds(k * 128, 128)
         q1 = dot(wc_ref[at, :], prod[...])
@@ -270,10 +291,11 @@
 def body(signal, cotangent, filter_spec):
     shape = signal.shape
     place = lax.axis_index("seq").astype(jnp.int32).reshape(1)
+    rank = lax.axis_index("dp").astype(jnp.int32).reshape(1)
     table = jnp.asarray(first_table())
     cos_t, sin_t = (jnp.asarray(t) for t in unit_tables())
     flip = jnp.asarray(np.eye(N, dtype=np.float32)[::-1].astype(BF))
-    tail, head = (jnp.asarray(t) for t in payload_selectors())
+    pick = jnp.asarray(payload_selectors())
     f_own, f_mirror = (jnp.asarray(t) for t in filter_selectors())
     g_own, g_mirror = (jnp.asarray(t) for t in grad_selectors())
     gather = jnp.asarray(gather_tables())
@@ -282,11 +304,11 @@
     filt = filter_spec.reshape(2, 64, N)
     sent, tails, heads = pl.pallas_call(
         kernel_a,
-        in_specs=[SMEM] + [VMEM] * 6,
+        in_specs=[SMEM] * 2 + [VMEM] * 5,
         out_specs=[VMEM] * 3,
         out_shape=[
             jax.ShapeDtypeStruct((N, HALF), BF),
-            jax.ShapeDtypeStruct((2, 32, N), BF),
+            jax.ShapeDtypeStruct((2, 8, N), BF),
             jax.ShapeDtypeStruct((2, 8, N), BF),
         ],
         scratch_shapes=[
@@ -294,30 +316,41 @@
             pltpu.VMEM((2, 256, 128), F32),
             pltpu.VMEM((2, N, 128), F32),
         ],
-    )(place, signal.reshape(128, N), cotangent.reshape(128, N), table, filt, tail, head)
+    )(place, rank, signal.reshape(128, N), cotangent.reshape(128, N), table, filt, pick)
     got = lax.all_to_all(sent.reshape(SEQ, ROWS, HALF), "seq", 0, 0, tiled=True)
     tails = lax.ppermute(tails, "seq", opposite)
     heads = lax.ppermute(heads, "seq", heads_to)
+    share = jnp.concatenate([tails, heads], axis=1)
+    shares = [share] + [
+        lax.ppermute(share, "dp", [(d, d ^ bit) for d in range(8)]) for bit in (2, 4, 6)
+    ]
+    spec, grad = pl.pallas_call(
+        kernel_b,
+        in_specs=[SMEM] + [VMEM] * 4,
+        out_specs=[VMEM, VMEM],
+        out_shape=[
+            jax.ShapeDtypeStruct((N, HALF), F32),
+            jax.ShapeDtypeStruct((2, 48, N), BF),
+        ],
+        compiler_params=PARAMS,
+    )(place, got.reshape(N, HALF), cos_t, sin_t, gather)
     spread = pl.pallas_call(
         kernel_f,
-        in_specs=[SMEM] + [VMEM] * 6,
+        in_specs=[SMEM] * 2 + [VMEM] * 8,
         out_specs=VMEM,
         out_shape=jax.ShapeDtypeStruct((N, N), F32),
-        scratch_shapes=[pltpu.VMEM((2, 112, N), BF)],
+        scratch_shapes=[pltpu.VMEM((2, 128, N), BF)],
         compiler_params=PARAMS,
         cost_estimate=pl.CostEstimate(flops=400000000, bytes_accessed=2000000, transcendentals=0),
-    )(place, filt, tails, heads, f_own, f_mirror, flip)
-    back, grad = pl.pallas_call(
-        kernel_b,
-        in_specs=[SMEM] + [VMEM] * 5,
-        out_specs=[VMEM, VMEM],
-        out_shape=[
-            jax.ShapeDtypeStruct((N, HALF), BF),
-            jax.ShapeDtypeStruct((2, 48, N), BF),
-        ],
+    )(place, rank, filt, *shares, f_own, f_mirror, flip)
+    back = pl.pallas_call(
+        kernel_d,
+        in_specs=[VMEM] * 4,
+        out_specs=VMEM,
+        out_shape=jax.ShapeDtypeStruct((N, HALF), BF),
         scratch_shapes=[pltpu.VMEM((N, HALF), BF)],
         compiler_params=PARAMS,
-    )(place, got.reshape(N, HALF), cos_t, sin_t, spread, gather)
+    )(spec, cos_t, sin_t, spread)
     far = lax.ppermute(grad[:, :32], "seq", opposite)
     slot = jnp.where(place[0] == 0, grad[:, 32:40], grad[:, :8])
     slot = lax.ppermute(slot, "seq", heads_to)

time: 105 us -> 107 us (1.019)
  starting transfers between devices: 64 us -> 67.4 us
  waiting for transfers between devices: 30 us -> 28.7 us
    ppermute x1, waiting for transfers between devices: 14.1 us -> 0.01 us  [body(): heads = lax.ppermute(heads, 'seq', heads_to)]
    ppermute x0 -> x3, starting transfers between devices: none -> 9.79 us  [body(): lax.ppermute(share, 'dp', [(d, d ^ bit) for d in range(8)])]
    ppermute x1, waiting for transfers between devices: 0.44 us -> 8.77 us  [body(): tails = lax.ppermute(tails, 'seq', opposite)]
    all_to_all x1, starting transfers between devices: 20.1 us -> 14.1 us  [body(): mid = lax.all_to_all(back.reshape(SEQ, ROWS, HALF), 'seq', 0, 0, tiled=True)]
    all_to_all x1, waiting for transfers between devices: 0.01 us -> 5.49 us  [body(): got = lax.all_to_all(sent.reshape(SEQ, ROWS, HALF), 'seq', 0, 0, tiled=True)]
    ppermute x1, waiting for transfers between devices: 3.02 us -> 0.01 us  [body(): slot = lax.ppermute(slot, 'seq', heads_to)]
    ppermute x3, starting transfers between devices: 12.2 us -> 10.3 us  [body(): other = lax.ppermute(grad, 'dp', [(d, d ^ bit) for d in range(8)])]
    ppermute x1, starting transfers between devices: 3.56 us -> 5.06 us  [body(): slot = lax.ppermute(slot, 'seq', heads_to)]
  transfers between devices with their start and end apart: 9 -> 12, of which waited for: 6 -> 6; matrix products, arithmetic and copies ran while one was open for 1% -> 1% of each run, Pallas kernels for 1% -> 5%
where the time goes in v5:
time: 107 us
  starting transfers between devices  67.4 us (63%)
  waiting for transfers between devices  28.7 us (27%)
  Pallas kernels  8.98 us (8%)
    all_to_all x1, starting transfers between devices, body(): got = lax.all_to_all(sent.reshape(SEQ, ROWS, HALF), 'seq', 0, 0, tiled=True)  18.2 us
    all_to_all x1, starting transfers between devices, body(): mid = lax.all_to_all(back.reshape(SEQ, ROWS, HALF), 'seq', 0, 0, tiled=True)  14.1 us
    ppermute x3, starting transfers between devices, body(): other = lax.ppermute(grad, 'dp', [(d, d ^ bit) for d in range(8)])  10.3 us
    ppermute x3, starting transfers between devices, body(): lax.ppermute(share, 'dp', [(d, d ^ bit) for d in range(8)])  9.79 us
    ppermute x1, waiting for transfers between devices, body(): tails = lax.ppermute(tails, 'seq', opposite)  8.77 us
    ppermute x3, waiting for transfers between devices, body(): other = lax.ppermute(grad, 'dp', [(d, d ^ bit) for d in range(8)])  7.49 us
    ppermute x1, starting transfers between devices, body(): tails = lax.ppermute(tails, 'seq', opposite)  5.95 us
    all_to_all x1, waiting for transfers between devices, body(): mid = lax.all_to_all(back.reshape(SEQ, ROWS, HALF), 'seq', 0, 0, tiled=True)  5.59 us
  transfers between devices with their start and end apart: 12, of which 6 were waited for; matrix products, arithmetic and copies ran while one was open for 1% of the time, Pallas kernels for 5%

profile of v5, /device:TPU:1, one launch (start us, length us, event | category | flops | bytes accessed | tf_op | source)
XLA Modules:
  0.0 106.9 jit_solution(17991735952698776451)
XLA Ops:
  0.6 0.0 copy-start.1
  0.7 2.6 %shard_map.148 = (bf16[512,256]{1,0:T(8,128)(2,1)}, bf16[2,8,512]{2,1,0:T(8,128)(2,1)}, bf16[2,8,512]{2,1,0:T(8,128)(2,1)}) custom-call(s32[1]{0:T(128)} %bitcast.idx_ref, s32[1]{0:T(128)} %bitcast.1.rank_ref, bf16[128,512]{1,0:T(8,128)(2,1)} %bitcast.18, bf16[128,512]{1,0:T(8,128)(2,1)} %bitcast.19, bf16[512,512]{1,0:T(8,128)(2,1)} %constant.31.clone.t_ref, ...), custom_call_target="tpu_custom_call" | custom-call | tf_op jit(solution)/shard_map/pallas_call | solution.py:305
  3.3 18.2 %all-to-all-start = ((bf16[64,8,256]{2,1,0:T(8,128)(2,1)}), bf16[64,8,256]{2,1,0:T(8,128)(2,1)S(1)}, u32[]{:S(2)}, u32[]{:S(2)}) async-start(bf16[64,8,256]{2,1,0:T(8,128)(2,1)} %bitcast.17), calls=%async_computation | async-start | bytes 524288 | tf_op jit(solution)/shard_map/all_to_all | solution.py:320
  21.5 6.0 %collective-permute-start = (bf16[2,8,512]{2,1,0:T(8,128)(2,1)S(1)}, bf16[2,8,512]{2,1,0:T(8,128)(2,1)S(1)}, u32[]{:S(2)}, u32[]{:S(2)}) collective-permute-start(bf16[2,8,512]{2,1,0:T(8,128)(2,1)S(1)} %copy-done.11), channel_id=1, source_target_pairs={{0,63},{1,62},{2,61},{3,60},{4,59},{5,58},{6,57},{7,56},{8,55},{9,... | collective-permute-start | bytes 49160 | tf_op jit(solution)/shard_map/ppermute | solution.py:321
  27.5 1.9 %collective-permute-start.1 = (bf16[2,8,512]{2,1,0:T(8,128)(2,1)S(1)}, bf16[2,8,512]{2,1,0:T(8,128)(2,1)S(1)}, u32[]{:S(2)}, u32[]{:S(2)}) collective-permute-start(bf16[2,8,512]{2,1,0:T(8,128)(2,1)S(1)} %copy-done.10), channel_id=1, source_target_pairs={{0,32},{1,63},{2,62},{3,61},{4,60},{5,59},{6,58},{7,57},{8,56},{9,... | collective-permute-start | bytes 49160 | tf_op jit(solution)/shard_map/ppermute | solution.py:322
  29.4 8.8 %collective-permute-done = bf16[2,8,512]{2,1,0:T(8,128)(2,1)S(1)} collective-permute-done((bf16[2,8,512]{2,1,0:T(8,128)(2,1)S(1)}, bf16[2,8,512]{2,1,0:T(8,128)(2,1)S(1)}, u32[]{:S(2)}, u32[]{:S(2)}) %collective-permute-start) | collective-permute-done | bytes 16416 | tf_op jit(solution)/shard_map/ppermute | solution.py:321
  38.2 5.5 %all-to-all-done = bf16[64,8,256]{2,1,0:T(8,128)(2,1)S(1)} async-done(((bf16[64,8,256]{2,1,0:T(8,128)(2,1)}), bf16[64,8,256]{2,1,0:T(8,128)(2,1)S(1)}, u32[]{:S(2)}, u32[]{:S(2)}) %all-to-all-start) | async-done | bytes 262176 | tf_op jit(solution)/shard_map/all_to_all | solution.py:320
  43.7 0.0 copy-start.2
  43.7 1.8 %shard_map.149 = (f32[512,256]{1,0:T(8,128)S(1)}, bf16[2,48,512]{2,1,0:T(8,128)(2,1)S(1)}) custom-call(s32[1]{0:T(128)} %bitcast.idx_ref, bf16[512,256]{1,0:T(8,128)(2,1)S(1)} %bitcast.13, bf16[512,512]{1,0:T(8,128)(2,1)S(1)} %copy-done, bf16[512,512]{1,0:T(8,128)(2,1)S(1)} %copy-done.1, bf16[2,2,48,256]{3,2,1,0:T(8,128)(2,1)S(1)} %copy-done.7), custom_call_target="tpu_custom_call" | custom-call | tf_op jit(solution)/shard_map/pallas_call | solution.py:327
  45.6 0.0 copy-start.9
  45.6 0.0 copy-start.8
  45.6 2.1 %collective-permute-start.5 = (bf16[2,32,512]{2,1,0:T(8,128)(2,1)S(1)}, bf16[2,32,512]{2,1,0:T(8,128)(2,1)S(1)}, u32[]{:S(2)}, u32[]{:S(2)}) collective-permute-start(bf16[2,32,512]{2,1,0:T(8,128)(2,1)S(1)} %slice.9), channel_id=1, source_target_pairs={{0,63},{1,62},{2,61},{3,60},{4,59},{5,58},{6,57},{7,56},{8,55},{9,... | collective-permute-start | bytes 196616 | tf_op jit(solution)/shard_map/ppermute | solution.py:354
  47.7 5.1 %collective-permute-start.6 = (bf16[2,8,512]{2,1,0:T(8,128)(2,1)S(1)}, bf16[2,8,512]{2,1,0:T(8,128)(2,1)S(1)}, u32[]{:S(2)}, u32[]{:S(2)}) collective-permute-start(bf16[2,8,512]{2,1,0:T(8,128)(2,1)S(1)} %slice_select_fusion), channel_id=1, source_target_pairs={{0,32},{1,63},{2,62},{3,61},{4,60},{5,59},{6,58},{7,57},{8,56},{9,... | collective-permute-start | bytes 49160 | tf_op jit(solution)/shard_map/ppermute | solution.py:356
  52.8 0.0 copy-start.5
  52.8 0.0 copy-start.6
  52.8 3.3 %collective-permute-start.2 = (bf16[2,16,512]{2,1,0:T(8,128)(2,1)S(1)}, bf16[2,16,512]{2,1,0:T(8,128)(2,1)S(1)}, u32[]{:S(2)}, u32[]{:S(2)}) collective-permute-start(bf16[2,16,512]{2,1,0:T(8,128)(2,1)S(1)} %constant_dynamic-update-slice_fusion.s0_ref), channel_id=1, source_target_pairs={{0,128},{64,192},{128,0},{192,64},{256,384},{320,448},{384,256},{4... | collective-permute-start | bytes 98312 | tf_op jit(solution)/shard_map/ppermute | solution.py:325
  56.1 4.5 %collective-permute-start.3 = (bf16[2,16,512]{2,1,0:T(8,128)(2,1)S(1)}, bf16[2,16,512]{2,1,0:T(8,128)(2,1)S(1)}, u32[]{:S(2)}, u32[]{:S(2)}) collective-permute-start(bf16[2,16,512]{2,1,0:T(8,128)(2,1)S(1)} %constant_dynamic-update-slice_fusion.s0_ref), channel_id=1, source_target_pairs={{0,256},{64,320},{128,384},{192,448},{256,0},{320,64},{384,128},{4... | collective-permute-start | bytes 98312 | tf_op jit(solution)/shard_map/ppermute | solution.py:325
  60.7 1.9 %collective-permute-start.4 = (bf16[2,16,512]{2,1,0:T(8,128)(2,1)S(1)}, bf16[2,16,512]{2,1,0:T(8,128)(2,1)S(1)}, u32[]{:S(2)}, u32[]{:S(2)}) collective-permute-start(bf16[2,16,512]{2,1,0:T(8,128)(2,1)S(1)} %constant_dynamic-update-slice_fusion.s0_ref), channel_id=1, source_target_pairs={{0,384},{64,448},{128,256},{192,320},{256,128},{320,192},{384,0},{... | collective-permute-start | bytes 98312 | tf_op jit(solution)/shard_map/ppermute | solution.py:325
  62.7 0.6 shard_map.153
  63.3 1.9 %collective-permute-start.7 = (bf16[2,64,512]{2,1,0:T(8,128)(2,1)S(1)}, bf16[2,64,512]{2,1,0:T(8,128)(2,1)S(1)}, u32[]{:S(2)}, u32[]{:S(2)}) collective-permute-start(bf16[2,64,512]{2,1,0:T(8,128)(2,1)S(1)} %shard_map.153), channel_id=1, source_target_pairs={{0,128},{64,192},{128,0},{192,64},{256,384},{320,448},{384,256},{4... | collective-permute-start | bytes 393224 | tf_op jit(solution)/shard_map/ppermute | solution.py:368
  65.2 1.3 %collective-permute-done.4.s3_ref = bf16[2,16,512]{2,1,0:T(8,128)(2,1)S(1)} collective-permute-done((bf16[2,16,512]{2,1,0:T(8,128)(2,1)S(1)}, bf16[2,16,512]{2,1,0:T(8,128)(2,1)S(1)}, u32[]{:S(2)}, u32[]{:S(2)}) %collective-permute-start.4) | collective-permute-done | bytes 32800 | tf_op jit(solution)/shard_map/ppermute | solution.py:325
  66.6 1.1 %shard_map.150.h_ref = f32[512,512]{1,0:T(8,128)S(1)} custom-call(s32[1]{0:T(128)} %bitcast.idx_ref, s32[1]{0:T(128)} %bitcast.1.rank_ref, bf16[2,64,512]{2,1,0:T(8,128)(2,1)S(1)} %bitcast.15, bf16[2,16,512]{2,1,0:T(8,128)(2,1)S(1)} %constant_dynamic-update-slice_fusion.s0_ref, bf16[2,16,512]{2,1,0:T(8,128)(2,1)S(1)} %collective-permute-done.2.s1_ref, ...), custom_call_target="tpu_custom_call" | custom-call | flops 400000000 | bytes 2000000 | tf_op jit(solution)/shard_map/pallas_call | solution.py:337
  67.7 1.4 %shard_map.151 = bf16[512,256]{1,0:T(8,128)(2,1)} custom-call(f32[512,256]{1,0:T(8,128)S(1)} %get-tuple-element.11.x_ref, bf16[512,512]{1,0:T(8,128)(2,1)S(1)} %copy-done, bf16[512,512]{1,0:T(8,128)(2,1)S(1)} %copy-done.1, f32[512,512]{1,0:T(8,128)S(1)} %shard_map.150.h_ref), custom_call_target="tpu_custom_call" | custom-call | tf_op jit(solution)/shard_map/pallas_call | solution.py:346
  69.1 14.1 %all-to-all-start.1 = ((bf16[64,8,256]{2,1,0:T(8,128)(2,1)}), bf16[64,8,256]{2,1,0:T(8,128)(2,1)S(1)}, u32[]{:S(2)}, u32[]{:S(2)}) async-start(bf16[64,8,256]{2,1,0:T(8,128)(2,1)} %bitcast.7), calls=%async_computation.1 | async-start | bytes 524288 | tf_op jit(solution)/shard_map/all_to_all | solution.py:357
  83.3 0.0 copy-start.3
  83.4 4.0 %collective-permute-start.8 = (bf16[2,64,512]{2,1,0:T(8,128)(2,1)S(1)}, bf16[2,64,512]{2,1,0:T(8,128)(2,1)S(1)}, u32[]{:S(2)}, u32[]{:S(2)}) collective-permute-start(bf16[2,64,512]{2,1,0:T(8,128)(2,1)S(1)} %add_convert_fusion.2), channel_id=1, source_target_pairs={{0,256},{64,320},{128,384},{192,448},{256,0},{320,64},{384,128},{4... | collective-permute-start | bytes 393224 | tf_op jit(solution)/shard_map/ppermute | solution.py:368
  87.4 4.1 %collective-permute-done.8 = bf16[2,64,512]{2,1,0:T(8,128)(2,1)S(1)} collective-permute-done((bf16[2,64,512]{2,1,0:T(8,128)(2,1)S(1)}, bf16[2,64,512]{2,1,0:T(8,128)(2,1)S(1)}, u32[]{:S(2)}, u32[]{:S(2)}) %collective-permute-start.8) | collective-permute-done | bytes 131104 | tf_op jit(solution)/shard_map/ppermute | solution.py:368
  91.5 4.3 %collective-permute-start.9 = (bf16[2,64,512]{2,1,0:T(8,128)(2,1)S(1)}, bf16[2,64,512]{2,1,0:T(8,128)(2,1)S(1)}, u32[]{:S(2)}, u32[]{:S(2)}) collective-permute-start(bf16[2,64,512]{2,1,0:T(8,128)(2,1)S(1)} %add_convert_fusion.1), channel_id=1, source_target_pairs={{0,64},{64,0},{128,192},{192,128},{256,320},{320,256},{384,448},{4... | collective-permute-start | bytes 393224 | tf_op jit(solution)/shard_map/ppermute | solution.py:368
  95.9 3.4 %collective-permute-done.9 = bf16[2,64,512]{2,1,0:T(8,128)(2,1)S(1)} collective-permute-done((bf16[2,64,512]{2,1,0:T(8,128)(2,1)S(1)}, bf16[2,64,512]{2,1,0:T(8,128)(2,1)S(1)}, u32[]{:S(2)}, u32[]{:S(2)}) %collective-permute-start.9) | collective-permute-done | bytes 131104 | tf_op jit(solution)/shard_map/ppermute | solution.py:368
  99.3 0.7 fusion
  99.9 5.6 %all-to-all-done.1 = bf16[64,8,256]{2,1,0:T(8,128)(2,1)S(1)} async-done(((bf16[64,8,256]{2,1,0:T(8,128)(2,1)}), bf16[64,8,256]{2,1,0:T(8,128)(2,1)S(1)}, u32[]{:S(2)}, u32[]{:S(2)}) %all-to-all-start.1) | async-done | bytes 262176 | tf_op jit(solution)/shard_map/all_to_all | solution.py:357
  105.5 1.3 %shard_map.152 = (bf16[128,512]{1,0:T(8,128)(2,1)}, bf16[128,512]{1,0:T(8,128)(2,1)}) custom-call(s32[1]{0:T(128)} %bitcast.idx_ref, bf16[512,256]{1,0:T(8,128)(2,1)S(1)} %bitcast.16, bf16[512,512]{1,0:T(8,128)(2,1)S(1)} %copy-done.3), custom_call_target="tpu_custom_call" | custom-call | flops 400000000 | bytes 2000000 | tf_op jit(solution)/shard_map/pallas_call | solution.py:370
  (29 shorter events, 0.1 us)
Async XLA Ops:
  0.6 43.1 %copy-start = (bf16[512,512]{1,0:T(8,128)(2,1)S(1)}, bf16[512,512]{1,0:T(8,128)(2,1)}, u32[]{:S(2)}) copy-start(bf16[512,512]{1,0:T(8,128)(2,1)} %constant.32.clone.wc_ref) | copy-start | bytes 1572868
  0.6 43.1 %copy-start.1 = (bf16[512,512]{1,0:T(8,128)(2,1)S(1)}, bf16[512,512]{1,0:T(8,128)(2,1)}, u32[]{:S(2)}) copy-start(bf16[512,512]{1,0:T(8,128)(2,1)} %constant.33.clone.ws_ref) | copy-start | bytes 1572868
  3.3 18.2 %copy-start.11 = (bf16[2,8,512]{2,1,0:T(8,128)(2,1)S(1)}, bf16[2,8,512]{2,1,0:T(8,128)(2,1)}, u32[]{:S(2)}) copy-start(bf16[2,8,512]{2,1,0:T(8,128)(2,1)} %get-tuple-element.12) | copy-start | bytes 49156
  3.3 24.2 %copy-start.10 = (bf16[2,8,512]{2,1,0:T(8,128)(2,1)S(1)}, bf16[2,8,512]{2,1,0:T(8,128)(2,1)}, u32[]{:S(2)}) copy-start(bf16[2,8,512]{2,1,0:T(8,128)(2,1)} %get-tuple-element.13) | copy-start | bytes 49156
  3.3 40.4 %copy-start.7 = (bf16[2,2,48,256]{3,2,1,0:T(8,128)(2,1)S(1)}, bf16[2,2,48,256]{3,2,1,0:T(8,128)(2,1)}, u32[]{:S(2)}) copy-start(bf16[2,2,48,256]{3,2,1,0:T(8,128)(2,1)} %constant.40.clone.gather_ref) | copy-start | bytes 294916
  3.3 40.4 %all-to-all-start = ((bf16[64,8,256]{2,1,0:T(8,128)(2,1)}), bf16[64,8,256]{2,1,0:T(8,128)(2,1)S(1)}, u32[]{:S(2)}, u32[]{:S(2)}) async-start(bf16[64,8,256]{2,1,0:T(8,128)(2,1)} %bitcast.17), calls=%async_computation | async-start | bytes 524288 | tf_op jit(solution)/shard_map/all_to_all | solution.py:320
  21.5 16.7 %collective-permute-start = (bf16[2,8,512]{2,1,0:T(8,128)(2,1)S(1)}, bf16[2,8,512]{2,1,0:T(8,128)(2,1)S(1)}, u32[]{:S(2)}, u32[]{:S(2)}) collective-permute-start(bf16[2,8,512]{2,1,0:T(8,128)(2,1)S(1)} %copy-done.11), channel_id=1, source_target_pairs={{0,63},{1,62},{2,61},{3,60},{4,59},{5,58},{6,57},{7,56},{8,55},{9,... | collective-permute-start | bytes 49160 | tf_op jit(solution)/shard_map/ppermute | solution.py:321
  27.5 25.2 %collective-permute-start.1 = (bf16[2,8,512]{2,1,0:T(8,128)(2,1)S(1)}, bf16[2,8,512]{2,1,0:T(8,128)(2,1)S(1)}, u32[]{:S(2)}, u32[]{:S(2)}) collective-permute-start(bf16[2,8,512]{2,1,0:T(8,128)(2,1)S(1)} %copy-done.10), channel_id=1, source_target_pairs={{0,32},{1,63},{2,62},{3,61},{4,60},{5,59},{6,58},{7,57},{8,56},{9,... | collective-permute-start | bytes 49160 | tf_op jit(solution)/shard_map/ppermute | solution.py:322
  43.7 18.9 %copy-start.2 = (bf16[512,512]{1,0:T(8,128)(2,1)S(1)}, bf16[512,512]{1,0:T(8,128)(2,1)}, u32[]{:S(2)}) copy-start(bf16[512,512]{1,0:T(8,128)(2,1)} %constant.34.clone.flip_ref) | copy-start | bytes 1572868
  45.6 17.1 %copy-start.9 = (bf16[4,64,112]{2,1,0:T(8,128)(2,1)S(1)}, bf16[4,64,112]{2,1,0:T(8,128)(2,1)}, u32[]{:S(2)}) copy-start(bf16[4,64,112]{2,1,0:T(8,128)(2,1)} %constant.39.clone.mirror_ref) | copy-start | bytes 172036
  45.6 17.1 %copy-start.8 = (bf16[4,64,112]{2,1,0:T(8,128)(2,1)S(1)}, bf16[4,64,112]{2,1,0:T(8,128)(2,1)}, u32[]{:S(2)}) copy-start(bf16[4,64,112]{2,1,0:T(8,128)(2,1)} %constant.38.clone.own_ref) | copy-start | bytes 172036
  45.6 17.0 %collective-permute-start.5 = (bf16[2,32,512]{2,1,0:T(8,128)(2,1)S(1)}, bf16[2,32,512]{2,1,0:T(8,128)(2,1)S(1)}, u32[]{:S(2)}, u32[]{:S(2)}) collective-permute-start(bf16[2,32,512]{2,1,0:T(8,128)(2,1)S(1)} %slice.9), channel_id=1, source_target_pairs={{0,63},{1,62},{2,61},{3,60},{4,59},{5,58},{6,57},{7,56},{8,55},{9,... | collective-permute-start | bytes 196616 | tf_op jit(solution)/shard_map/ppermute | solution.py:354
  47.7 14.9 %collective-permute-start.6 = (bf16[2,8,512]{2,1,0:T(8,128)(2,1)S(1)}, bf16[2,8,512]{2,1,0:T(8,128)(2,1)S(1)}, u32[]{:S(2)}, u32[]{:S(2)}) collective-permute-start(bf16[2,8,512]{2,1,0:T(8,128)(2,1)S(1)} %slice_select_fusion), channel_id=1, source_target_pairs={{0,32},{1,63},{2,62},{3,61},{4,60},{5,59},{6,58},{7,57},{8,56},{9,... | collective-permute-start | bytes 49160 | tf_op jit(solution)/shard_map/ppermute | solution.py:356
  52.8 13.8 %copy-start.4 = (bf16[2,8,8,512]{3,2,1,0:T(8,128)(2,1)S(1)}, bf16[2,8,8,512]{3,2,1,0:T(8,128)(2,1)}, u32[]{:S(2)}) copy-start(bf16[2,8,8,512]{3,2,1,0:T(8,128)(2,1)} %param.15) | copy-start | bytes 393220
  52.8 13.8 %copy-start.5 = (bf16[3,128,256]{2,1,0:T(8,128)(2,1)S(1)}, bf16[3,128,256]{2,1,0:T(8,128)(2,1)}, u32[]{:S(2)}) copy-start(bf16[3,128,256]{2,1,0:T(8,128)(2,1)} %constant.36.clone.own_ref) | copy-start | bytes 589828
  52.8 13.8 %copy-start.6 = (bf16[3,128,256]{2,1,0:T(8,128)(2,1)S(1)}, bf16[3,128,256]{2,1,0:T(8,128)(2,1)}, u32[]{:S(2)}) copy-start(bf16[3,128,256]{2,1,0:T(8,128)(2,1)} %constant.37.clone.mirror_ref) | copy-start | bytes 589828
  52.8 12.4 %collective-permute-start.2 = (bf16[2,16,512]{2,1,0:T(8,128)(2,1)S(1)}, bf16[2,16,512]{2,1,0:T(8,128)(2,1)S(1)}, u32[]{:S(2)}, u32[]{:S(2)}) collective-permute-start(bf16[2,16,512]{2,1,0:T(8,128)(2,1)S(1)} %constant_dynamic-update-slice_fusion.s0_ref), channel_id=1, source_target_pairs={{0,128},{64,192},{128,0},{192,64},{256,384},{320,448},{384,256},{4... | collective-permute-start | bytes 98312 | tf_op jit(solution)/shard_map/ppermute | solution.py:325
  56.1 9.1 %collective-permute-start.3 = (bf16[2,16,512]{2,1,0:T(8,128)(2,1)S(1)}, bf16[2,16,512]{2,1,0:T(8,128)(2,1)S(1)}, u32[]{:S(2)}, u32[]{:S(2)}) collective-permute-start(bf16[2,16,512]{2,1,0:T(8,128)(2,1)S(1)} %constant_dynamic-update-slice_fusion.s0_ref), channel_id=1, source_target_pairs={{0,256},{64,320},{128,384},{192,448},{256,0},{320,64},{384,128},{4... | collective-permute-start | bytes 98312 | tf_op jit(solution)/shard_map/ppermute | solution.py:325
  60.7 5.9 %collective-permute-start.4 = (bf16[2,16,512]{2,1,0:T(8,128)(2,1)S(1)}, bf16[2,16,512]{2,1,0:T(8,128)(2,1)S(1)}, u32[]{:S(2)}, u32[]{:S(2)}) collective-permute-start(bf16[2,16,512]{2,1,0:T(8,128)(2,1)S(1)} %constant_dynamic-update-slice_fusion.s0_ref), channel_id=1, source_target_pairs={{0,384},{64,448},{128,256},{192,320},{256,128},{320,192},{384,0},{... | collective-permute-start | bytes 98312 | tf_op jit(solution)/shard_map/ppermute | solution.py:325
  63.3 20.0 %collective-permute-start.7 = (bf16[2,64,512]{2,1,0:T(8,128)(2,1)S(1)}, bf16[2,64,512]{2,1,0:T(8,128)(2,1)S(1)}, u32[]{:S(2)}, u32[]{:S(2)}) collective-permute-start(bf16[2,64,512]{2,1,0:T(8,128)(2,1)S(1)} %shard_map.153), channel_id=1, source_target_pairs={{0,128},{64,192},{128,0},{192,64},{256,384},{320,448},{384,256},{4... | collective-permute-start | bytes 393224 | tf_op jit(solution)/shard_map/ppermute | solution.py:368
  69.1 36.4 %all-to-all-start.1 = ((bf16[64,8,256]{2,1,0:T(8,128)(2,1)}), bf16[64,8,256]{2,1,0:T(8,128)(2,1)S(1)}, u32[]{:S(2)}, u32[]{:S(2)}) async-start(bf16[64,8,256]{2,1,0:T(8,128)(2,1)} %bitcast.7), calls=%async_computation.1 | async-start | bytes 524288 | tf_op jit(solution)/shard_map/all_to_all | solution.py:357
  83.3 22.2 %copy-start.3 = (bf16[512,512]{1,0:T(8,128)(2,1)S(1)}, bf16[512,512]{1,0:T(8,128)(2,1)}, u32[]{:S(2)}) copy-start(bf16[512,512]{1,0:T(8,128)(2,1)} %constant.31.clone.t_ref) | copy-start | bytes 1572868
  83.4 8.1 %collective-permute-start.8 = (bf16[2,64,512]{2,1,0:T(8,128)(2,1)S(1)}, bf16[2,64,512]{2,1,0:T(8,128)(2,1)S(1)}, u32[]{:S(2)}, u32[]{:S(2)}) collective-permute-start(bf16[2,64,512]{2,1,0:T(8,128)(2,1)S(1)} %add_convert_fusion.2), channel_id=1, source_target_pairs={{0,256},{64,320},{128,384},{192,448},{256,0},{320,64},{384,128},{4... | collective-permute-start | bytes 393224 | tf_op jit(solution)/shard_map/ppermute | solution.py:368
  91.5 7.7 %collective-permute-start.9 = (bf16[2,64,512]{2,1,0:T(8,128)(2,1)S(1)}, bf16[2,64,512]{2,1,0:T(8,128)(2,1)S(1)}, u32[]{:S(2)}, u32[]{:S(2)}) collective-permute-start(bf16[2,64,512]{2,1,0:T(8,128)(2,1)S(1)} %add_convert_fusion.1), channel_id=1, source_target_pairs={{0,64},{64,0},{128,192},{192,128},{256,320},{320,256},{384,448},{4... | collective-permute-start | bytes 393224 | tf_op jit(solution)/shard_map/ppermute | solution.py:368

commit v6 on v4

--- a/solution.py
+++ b/solution.py
@@ -18,6 +18,8 @@
 SMEM = pl.BlockSpec(memory_space=pltpu.SMEM)
 PARAMS = pltpu.CompilerParams(vmem_limit_bytes=20 * 2**20)
 
+LAST = 31
+
 
 def unit_tables():
     steps = np.arange(N, dtype=np.int32)
@@ -32,9 +34,10 @@
     cos_t, sin_t = unit_tables()
     col = np.arange(HALF)
     place = col % 64
-    row = 8 * place + 2 * (col // 128) + col // 64 % 2 + (place >= 32)
+    slot = 2 * (col // 128) + col // 64 % 2
+    row = 8 * place + slot + np.where(place >= 32, 1, 8 * (slot == 0))
     re, im = cos_t[:, row], sin_t[:, row]
-    im[:, 0] = cos_t[:, HALF]
+    im[:, LAST] = cos_t[:, 0]
     return np.concatenate([re, im], axis=1)
 
 
@@ -51,14 +54,14 @@
     for lane in range(HALF):
         k, f = slot[lane], filt[lane]
         for kind in (0, 1):
-            own[kind, f * 8 + k, lane] = 0.5
-            mirror[kind, 96 + f if k == 0 else 64 + f * 4 + 4 - k, lane] = 0.5
+            own[kind, f * 8 + k if k else 96 + f, lane] = 0.5
+            mirror[kind, 64 + f * 4 + (4 - k) % 4, lane] = 0.5
         own[2, f * 8 + k + 1, lane] = 0.5
         mirror[2, 64 + f * 4 + 3 - k, lane] = 0.5
         if k == 0:
             own[0, :, lane] = 0
             mirror[0, :, lane] = 0
-            source = 96 + f if chan[lane] else f * 8
+            source = 96 + f if chan[lane] else 64 + f * 4
             own[0, source, lane] = 0.5
             mirror[0, source, lane] = 0.5
     return own.astype(BF), mirror.astype(BF)
@@ -89,30 +92,29 @@
             at = f * 8 + row
             for kind in (0, 1):
                 if row < 4:
-                    own[kind, at, row * 8 + f] = 1
+                    own[kind, at, row * 8 + f if row else 96 + f] = 1
                 else:
                     mirror[kind, at, 48 + (7 - row) * 8 + f] = 1
             for kind in (2, 3):
-                if row == 0:
-                    mirror[kind, at, 96 + f] = 1
-                elif row < 5:
+                if 0 < row < 5:
                     own[kind, at, (row - 1) * 8 + f] = 1
                 else:
-                    mirror[kind, at, 48 + (8 - row) * 8 + f] = 1
-        own[0, f * 8, f] = 0.5
-        mirror[0, f * 8, f] = 0.5
-        own[3, f * 8, 96 + f] = 0.5
-        mirror[3, f * 8, 96 + f] = 0.5
+                    mirror[kind, at, 48 + (8 - row) % 8 * 8 + f] = 1
+        own[0, f * 8, 96 + f] = 0.5
+        mirror[0, f * 8, 96 + f] = 0.5
+        own[3, f * 8, 48 + f] = 0.5
+        mirror[3, f * 8, 48 + f] = 0.5
     return own.astype(BF), mirror.astype(BF)
 
 
 def payload_selectors():
-    tail = np.zeros((32, 64), np.float32)
+    tail = np.zeros((2, 32, 64), np.float32)
     head = np.zeros((8, 64), np.float32)
     for f in range(8):
         head[f, f * 8] = 1
         for row in range(4):
-            tail[f * 4 + row, f * 8 + 4 + row] = 1
+            tail[0, f * 4 + row, f * 8 + 4 + row] = 1
+            tail[1, f * 4 + row, f * 8 + (4 + row if row else 0)] = 1
     return tail.astype(BF), head.astype(BF)
 
 
@@ -125,22 +127,24 @@
     lane = lax.broadcasted_iota(jnp.int32, shape, 1)
     row = idx_ref[0] * ROWS + lax.broadcasted_iota(jnp.int32, shape, 0)
     place = lane & 63
-    col = 8 * place + 2 * (lane >> 7) + ((lane >> 6) & 1) + (place >> 5)
+    slot = 2 * (lane >> 7) + ((lane >> 6) & 1)
+    col = 8 * place + slot + jnp.where(place >= 32, 1, jnp.where(slot == 0, 8, 0))
     if chan:
-        col = jnp.where(lane == 0, HALF, col)
+        col = jnp.where(lane == LAST, 0, col)
     phases = (row * col).astype(F32) * (-2.0 * math.pi / (N * N))
     return jnp.cos(phases), jnp.sin(phases)
 
 
 def swap_first(re, im):
-    first = lax.broadcasted_iota(jnp.int32, re[0].shape, 2) == 0
+    first = lax.broadcasted_iota(jnp.int32, re[0].shape, 2) == LAST
     return (re[0], jnp.where(first, im[0], re[1])), (jnp.where(first, re[1], im[0]), im[1])
 
 
 def kernel_a(idx_ref, sig_ref, cot_ref, t_ref, f_ref, tail_ref, head_ref, out_ref, tails_ref,
              heads_ref, yre, yim, z):
+    upper = idx_ref[0] >> 5
     for ri in range(2):
-        tails_ref[ri] = dot(tail_ref[...], f_ref[ri]).astype(BF)
+        tails_ref[ri] = dot(tail_ref[upper], f_ref[ri]).astype(BF)
         heads_ref[ri] = dot(head_ref[...], f_ref[ri]).astype(BF)
     turns = [turn(idx_ref, chan) for chan in range(2)]
     for half, ref in enumerate((sig_ref, cot_ref)):
@@ -166,14 +170,14 @@
 
 def kernel_f(idx_ref, f_ref, tail_ref, head_ref, own_ref, mirror_ref, flip_ref, h_ref, rows):
     place = idx_ref[0]
-    kind = jnp.where(place == 0, 0, jnp.where(place < 32, 1, 2))
+    kind = jnp.where(place == LAST, 0, jnp.where(place < 32, 1, 2))
     rows[:, :64, :] = f_ref[...]
     rows[:, 64:96, :] = tail_ref[...]
     rows[:, 96:, :] = jnp.zeros((2, 16, N), BF)
     rows[:, 96:104, :] = head_ref[...]
     lane = lax.broadcasted_iota(jnp.int32, (N, HALF), 1)
-    shifted = ((lane & ~30) == 0) | ((lane & ~30) == 64)
-    shifted = shifted & (place == 0)
+    shifted = ((lane & ~30) == 1) | ((lane & ~30) == 65)
+    shifted = shifted & (place == LAST)
     negative = ((lane >> 6) & 1) == ((lane >> 4) & 1)
     for ri in range(2):
         near = dot(rows[ri], own_ref[kind], ((0,), (0,)))
@@ -188,7 +192,7 @@
 
 
 def kernel_b(idx_ref, r_ref, wc_ref, ws_ref, h_ref, gather_ref, v_ref, g_ref, prod):
-    first = jnp.where(idx_ref[0] == 0, 1, 0)
+    first = jnp.where(idx_ref[0] == LAST, 1, 0)
     sign = jnp.where(lax.broadcasted_iota(jnp.int32, (128, 128), 1) < 64, -1.0, 1.0)
     for k in range(4):
         at = pl.ds(k * 128, 128)
@@ -229,7 +233,7 @@
             for s in range(2):
                 at = ri * 64 + s * 32
                 y[s, pl.ds(r, 32, stride=ROWS), :] = block[at : at + 32]
-    double = jnp.where(lax.broadcasted_iota(jnp.int32, (ROWS, HALF), 1) == 0, 1.0, 2.0)
+    double = jnp.where(lax.broadcasted_iota(jnp.int32, (ROWS, HALF), 1) == LAST, 1.0, 2.0)
     turns = [[t * double for t in turn(idx_ref, chan)] for chan in range(2)]
     for half, ref in enumerate((out_ref, grad_ref)):
         at = pl.ds(half * 128, 128)
@@ -278,7 +282,8 @@
     g_own, g_mirror = (jnp.asarray(t) for t in grad_selectors())
     gather = jnp.asarray(gather_tables())
     opposite = [(d, SEQ - 1 - d) for d in range(SEQ)]
-    heads_to = [(d, {0: 32, 32: 0}.get(d, SEQ - d)) for d in range(SEQ)]
+    down = [(d, d // 32 * 32 + (d - 1) % 32) for d in range(SEQ)]
+    up = [(b, a) for a, b in down]
     filt = filter_spec.reshape(2, 64, N)
     sent, tails, heads = pl.pallas_call(
         kernel_a,
@@ -297,7 +302,7 @@
     )(place, signal.reshape(128, N), cotangent.reshape(128, N), table, filt, tail, head)
     got = lax.all_to_all(sent.reshape(SEQ, ROWS, HALF), "seq", 0, 0, tiled=True)
     tails = lax.ppermute(tails, "seq", opposite)
-    heads = lax.ppermute(heads, "seq", heads_to)
+    heads = lax.ppermute(heads, "seq", down)
     spread = pl.pallas_call(
         kernel_f,
         in_specs=[SMEM] + [VMEM] * 6,
@@ -319,8 +324,8 @@
         compiler_params=PARAMS,
     )(place, got.reshape(N, HALF), cos_t, sin_t, spread, gather)
     far = lax.ppermute(grad[:, :32], "seq", opposite)
-    slot = jnp.where(place[0] == 0, grad[:, 32:40], grad[:, :8])
-    slot = lax.ppermute(slot, "seq", heads_to)
+    slot = jnp.where(place[0] == LAST, grad[:, 32:40], grad[:, :8])
+    slot = lax.ppermute(slot, "seq", up)
     mid = lax.all_to_all(back.reshape(SEQ, ROWS, HALF), "seq", 0, 0, tiled=True)
     grad = pl.pallas_call(
         kernel_g,

time: 105 us -> 98.3 us (0.936)
  starting transfers between devices: 64 us -> 55.2 us
  waiting for transfers between devices: 30 us -> 32.4 us
    all_to_all x1, starting transfers between devices: 20.1 us -> 14.8 us  [body(): mid = lax.all_to_all(back.reshape(SEQ, ROWS, HALF), 'seq', 0, 0, tiled=True)]
    ppermute x2, waiting for transfers between devices: 17.1 us -> 12.8 us  [the longest x1 12 us: body(): heads = lax.ppermute(heads, 'seq', down)]
    ppermute x1, waiting for transfers between devices: 0.01 us -> 3.79 us  [body(): far = lax.ppermute(grad[:, :32], 'seq', opposite)]
    ppermute x2, starting transfers between devices: 5.48 us -> 1.94 us  [the longest x1 1.81 us: body(): slot = lax.ppermute(slot, 'seq', up)]
    ppermute x1, waiting for transfers between devices: 0.44 us -> 3.42 us  [body(): tails = lax.ppermute(tails, 'seq', opposite)]
  transfers between devices with their start and end apart: 9 -> 9, of which waited for: 6 -> 7; matrix products, arithmetic and copies ran while one was open for 1% -> 1% of each run, Pallas kernels for 1% -> 1%
where the time goes in v6:
time: 98.3 us; the launch traced here: 97.9 us
  starting transfers between devices  55.2 us (56%)
  waiting for transfers between devices  32.4 us (33%)
  Pallas kernels  8.6 us (9%)
    all_to_all x1, starting transfers between devices, body(): got = lax.all_to_all(sent.reshape(SEQ, ROWS, HALF), 'seq', 0, 0, tiled=True)  18.2 us
    all_to_all x1, starting transfers between devices, body(): mid = lax.all_to_all(back.reshape(SEQ, ROWS, HALF), 'seq', 0, 0, tiled=True)  14.8 us
    ppermute x3, starting transfers between devices, body(): other = lax.ppermute(grad, 'dp', [(d, d ^ bit) for d in range(8)])  12.2 us
    ppermute x1, waiting for transfers between devices, body(): heads = lax.ppermute(heads, 'seq', down)  12 us
    ppermute x3, waiting for transfers between devices, body(): other = lax.ppermute(grad, 'dp', [(d, d ^ bit) for d in range(8)])  6.78 us
    ppermute x1, starting transfers between devices, body(): tails = lax.ppermute(tails, 'seq', opposite)  5.95 us
    all_to_all x1, waiting for transfers between devices, body(): mid = lax.all_to_all(back.reshape(SEQ, ROWS, HALF), 'seq', 0, 0, tiled=True)  5.62 us
    ppermute x1, waiting for transfers between devices, body(): far = lax.ppermute(grad[:, :32], 'seq', opposite)  3.79 us
  transfers between devices with their start and end apart: 9, of which 7 were waited for; matrix products, arithmetic and copies ran while one was open for 1% of the time, Pallas kernels for 1%

profile of v6, /device:TPU:1, one launch (start us, length us, event | category | flops | bytes accessed | tf_op | source)
XLA Modules:
  0.0 97.9 jit_solution(7379005192048259125)
XLA Ops:
  0.6 0.0 copy-start
  0.6 2.6 %shard_map.157 = (bf16[512,256]{1,0:T(8,128)(2,1)}, bf16[2,32,512]{2,1,0:T(8,128)(2,1)}, bf16[2,8,512]{2,1,0:T(8,128)(2,1)}) custom-call(s32[1]{0:T(128)} %bitcast.idx_ref, bf16[128,512]{1,0:T(8,128)(2,1)} %bitcast.17, bf16[128,512]{1,0:T(8,128)(2,1)} %bitcast.18, bf16[512,512]{1,0:T(8,128)(2,1)} %constant.28.clone.t_ref, bf16[2,64,512]{2,1,0:T(8,128)(2,1)} %bitcast.13, ...), custom_call_target="tpu_custom_call" | custom-call | tf_op jit(solution)/shard_map/pallas_call | solution.py:288
  3.3 0.0 copy-start.6
  3.3 18.2 %all-to-all-start = ((bf16[64,8,256]{2,1,0:T(8,128)(2,1)}), bf16[64,8,256]{2,1,0:T(8,128)(2,1)S(1)}, u32[]{:S(2)}, u32[]{:S(2)}) async-start(bf16[64,8,256]{2,1,0:T(8,128)(2,1)} %bitcast.16), calls=%async_computation | async-start | bytes 524288 | tf_op jit(solution)/shard_map/all_to_all | solution.py:303
  21.5 6.0 %collective-permute-start = (bf16[2,32,512]{2,1,0:T(8,128)(2,1)}, bf16[2,32,512]{2,1,0:T(8,128)(2,1)S(1)}, u32[]{:S(2)}, u32[]{:S(2)}) collective-permute-start(bf16[2,32,512]{2,1,0:T(8,128)(2,1)} %get-tuple-element.11), channel_id=1, source_target_pairs={{0,63},{1,62},{2,61},{3,60},{4,59},{5,58},{6,57},{7,56},{8,55},{9,... | collective-permute-start | bytes 196616 | tf_op jit(solution)/shard_map/ppermute | solution.py:304
  27.5 0.0 copy-done.10
  27.5 0.1 collective-permute-start.1
  27.6 12.0 %collective-permute-done.1.head_ref = bf16[2,8,512]{2,1,0:T(8,128)(2,1)S(1)} collective-permute-done((bf16[2,8,512]{2,1,0:T(8,128)(2,1)S(1)}, bf16[2,8,512]{2,1,0:T(8,128)(2,1)S(1)}, u32[]{:S(2)}, u32[]{:S(2)}) %collective-permute-start.1) | collective-permute-done | bytes 16416 | tf_op jit(solution)/shard_map/ppermute | solution.py:305
  39.6 3.4 %collective-permute-done.tail_ref = bf16[2,32,512]{2,1,0:T(8,128)(2,1)S(1)} collective-permute-done((bf16[2,32,512]{2,1,0:T(8,128)(2,1)}, bf16[2,32,512]{2,1,0:T(8,128)(2,1)S(1)}, u32[]{:S(2)}, u32[]{:S(2)}) %collective-permute-start) | collective-permute-done | bytes 65568 | tf_op jit(solution)/shard_map/ppermute | solution.py:304
  43.0 0.0 copy-done
  43.0 1.1 %shard_map.158.h_ref = f32[512,512]{1,0:T(8,128)S(1)} custom-call(s32[1]{0:T(128)} %bitcast.idx_ref, bf16[2,64,512]{2,1,0:T(8,128)(2,1)S(1)} %bitcast.14, bf16[2,32,512]{2,1,0:T(8,128)(2,1)S(1)} %collective-permute-done.tail_ref, bf16[2,8,512]{2,1,0:T(8,128)(2,1)S(1)} %collective-permute-done.1.head_ref, bf16[3,112,256]{2,1,0:T(8,128)(2,1)S(1)} %copy-done.5, ...), custom_call_target="tpu_custom_call" | custom-call | flops 400000000 | bytes 2000000 | tf_op jit(solution)/shard_map/pallas_call | solution.py:306
  44.1 0.0 all-to-all-done
  44.1 0.0 copy-done.3
  44.1 0.0 copy-done.4
  44.2 0.0 copy-done.7
  44.2 2.9 %shard_map.159 = (bf16[512,256]{1,0:T(8,128)(2,1)}, bf16[2,48,512]{2,1,0:T(8,128)(2,1)S(1)}) custom-call(s32[1]{0:T(128)} %bitcast.idx_ref, bf16[512,256]{1,0:T(8,128)(2,1)S(1)} %bitcast.12, bf16[512,512]{1,0:T(8,128)(2,1)S(1)} %copy-done.3, bf16[512,512]{1,0:T(8,128)(2,1)S(1)} %copy-done.4, f32[512,512]{1,0:T(8,128)S(1)} %shard_map.158.h_ref, ...), custom_call_target="tpu_custom_call" | custom-call | tf_op jit(solution)/shard_map/pallas_call | solution.py:315
  47.1 2.1 %collective-permute-start.2 = (bf16[2,32,512]{2,1,0:T(8,128)(2,1)S(1)}, bf16[2,32,512]{2,1,0:T(8,128)(2,1)S(1)}, u32[]{:S(2)}, u32[]{:S(2)}) collective-permute-start(bf16[2,32,512]{2,1,0:T(8,128)(2,1)S(1)} %slice.9), channel_id=1, source_target_pairs={{0,63},{1,62},{2,61},{3,60},{4,59},{5,58},{6,57},{7,56},{8,55},{9,... | collective-permute-start | bytes 196616 | tf_op jit(solution)/shard_map/ppermute | solution.py:326
  49.2 1.8 %collective-permute-start.3 = (bf16[2,8,512]{2,1,0:T(8,128)(2,1)S(1)}, bf16[2,8,512]{2,1,0:T(8,128)(2,1)S(1)}, u32[]{:S(2)}, u32[]{:S(2)}) collective-permute-start(bf16[2,8,512]{2,1,0:T(8,128)(2,1)S(1)} %slice_select_fusion), channel_id=1, source_target_pairs={{31,0},{0,1},{1,2},{2,3},{3,4},{4,5},{5,6},{6,7},{7,8},{8,9},{9,10... | collective-permute-start | bytes 49160 | tf_op jit(solution)/shard_map/ppermute | solution.py:328
  51.0 0.9 collective-permute-done.3.head_ref
  51.9 3.8 %collective-permute-done.2.far_ref = bf16[2,32,512]{2,1,0:T(8,128)(2,1)S(1)} collective-permute-done((bf16[2,32,512]{2,1,0:T(8,128)(2,1)S(1)}, bf16[2,32,512]{2,1,0:T(8,128)(2,1)S(1)}, u32[]{:S(2)}, u32[]{:S(2)}) %collective-permute-start.2) | collective-permute-done | bytes 65568 | tf_op jit(solution)/shard_map/ppermute | solution.py:326
  55.7 0.6 shard_map.161
  56.3 3.2 %collective-permute-start.4 = (bf16[2,64,512]{2,1,0:T(8,128)(2,1)S(1)}, bf16[2,64,512]{2,1,0:T(8,128)(2,1)S(1)}, u32[]{:S(2)}, u32[]{:S(2)}) collective-permute-start(bf16[2,64,512]{2,1,0:T(8,128)(2,1)S(1)} %shard_map.161), channel_id=1, source_target_pairs={{0,128},{64,192},{128,0},{192,64},{256,384},{320,448},{384,256},{4... | collective-permute-start | bytes 393224 | tf_op jit(solution)/shard_map/ppermute | solution.py:340
  59.5 14.8 %all-to-all-start.1 = ((bf16[64,8,256]{2,1,0:T(8,128)(2,1)}), bf16[64,8,256]{2,1,0:T(8,128)(2,1)S(1)}, u32[]{:S(2)}, u32[]{:S(2)}) async-start(bf16[64,8,256]{2,1,0:T(8,128)(2,1)} %bitcast.6), calls=%async_computation.1 | async-start | bytes 524288 | tf_op jit(solution)/shard_map/all_to_all | solution.py:329
  74.3 0.0 copy-start.2
  74.3 0.0 collective-permute-done.4
  74.4 4.7 %collective-permute-start.5 = (bf16[2,64,512]{2,1,0:T(8,128)(2,1)S(1)}, bf16[2,64,512]{2,1,0:T(8,128)(2,1)S(1)}, u32[]{:S(2)}, u32[]{:S(2)}) collective-permute-start(bf16[2,64,512]{2,1,0:T(8,128)(2,1)S(1)} %add_convert_fusion.2), channel_id=1, source_target_pairs={{0,256},{64,320},{128,384},{192,448},{256,0},{320,64},{384,128},{4... | collective-permute-start | bytes 393224 | tf_op jit(solution)/shard_map/ppermute | solution.py:340
  79.1 3.5 %collective-permute-done.5 = bf16[2,64,512]{2,1,0:T(8,128)(2,1)S(1)} collective-permute-done((bf16[2,64,512]{2,1,0:T(8,128)(2,1)S(1)}, bf16[2,64,512]{2,1,0:T(8,128)(2,1)S(1)}, u32[]{:S(2)}, u32[]{:S(2)}) %collective-permute-start.5) | collective-permute-done | bytes 131104 | tf_op jit(solution)/shard_map/ppermute | solution.py:340
  82.6 4.4 %collective-permute-start.6 = (bf16[2,64,512]{2,1,0:T(8,128)(2,1)S(1)}, bf16[2,64,512]{2,1,0:T(8,128)(2,1)S(1)}, u32[]{:S(2)}, u32[]{:S(2)}) collective-permute-start(bf16[2,64,512]{2,1,0:T(8,128)(2,1)S(1)} %add_convert_fusion.1), channel_id=1, source_target_pairs={{0,64},{64,0},{128,192},{192,128},{256,320},{320,256},{384,448},{4... | collective-permute-start | bytes 393224 | tf_op jit(solution)/shard_map/ppermute | solution.py:340
  86.9 3.3 %collective-permute-done.6 = bf16[2,64,512]{2,1,0:T(8,128)(2,1)S(1)} collective-permute-done((bf16[2,64,512]{2,1,0:T(8,128)(2,1)S(1)}, bf16[2,64,512]{2,1,0:T(8,128)(2,1)S(1)}, u32[]{:S(2)}, u32[]{:S(2)}) %collective-permute-start.6) | collective-permute-done | bytes 131104 | tf_op jit(solution)/shard_map/ppermute | solution.py:340
  90.3 0.7 fusion
  90.9 5.6 %all-to-all-done.1 = bf16[64,8,256]{2,1,0:T(8,128)(2,1)S(1)} async-done(((bf16[64,8,256]{2,1,0:T(8,128)(2,1)}), bf16[64,8,256]{2,1,0:T(8,128)(2,1)S(1)}, u32[]{:S(2)}, u32[]{:S(2)}) %all-to-all-start.1) | async-done | bytes 262176 | tf_op jit(solution)/shard_map/all_to_all | solution.py:329
  96.6 1.3 %shard_map.160 = (bf16[128,512]{1,0:T(8,128)(2,1)}, bf16[128,512]{1,0:T(8,128)(2,1)}) custom-call(s32[1]{0:T(128)} %bitcast.idx_ref, bf16[512,256]{1,0:T(8,128)(2,1)S(1)} %bitcast.15, bf16[512,512]{1,0:T(8,128)(2,1)S(1)} %copy-done.2), custom_call_target="tpu_custom_call" | custom-call | flops 400000000 | bytes 2000000 | tf_op jit(solution)/shard_map/pallas_call | solution.py:342
  (18 shorter events, 0.1 us)
Async XLA Ops:
  0.6 42.4 %copy-start = (bf16[512,512]{1,0:T(8,128)(2,1)S(1)}, bf16[512,512]{1,0:T(8,128)(2,1)}, u32[]{:S(2)}) copy-start(bf16[512,512]{1,0:T(8,128)(2,1)} %constant.31.clone.flip_ref) | copy-start | bytes 1572868
  3.3 24.2 %copy-start.10 = (bf16[2,8,512]{2,1,0:T(8,128)(2,1)S(1)}, bf16[2,8,512]{2,1,0:T(8,128)(2,1)}, u32[]{:S(2)}) copy-start(bf16[2,8,512]{2,1,0:T(8,128)(2,1)} %get-tuple-element.12) | copy-start | bytes 49156
  3.3 39.7 %copy-start.1 = (bf16[2,8,8,512]{3,2,1,0:T(8,128)(2,1)S(1)}, bf16[2,8,8,512]{3,2,1,0:T(8,128)(2,1)}, u32[]{:S(2)}) copy-start(bf16[2,8,8,512]{3,2,1,0:T(8,128)(2,1)} %param.16) | copy-start | bytes 393220
  3.3 39.7 %copy-start.5 = (bf16[3,112,256]{2,1,0:T(8,128)(2,1)S(1)}, bf16[3,112,256]{2,1,0:T(8,128)(2,1)}, u32[]{:S(2)}) copy-start(bf16[3,112,256]{2,1,0:T(8,128)(2,1)} %constant.34.clone.own_ref) | copy-start | bytes 516100
  3.3 39.7 %copy-start.6 = (bf16[3,112,256]{2,1,0:T(8,128)(2,1)S(1)}, bf16[3,112,256]{2,1,0:T(8,128)(2,1)}, u32[]{:S(2)}) copy-start(bf16[3,112,256]{2,1,0:T(8,128)(2,1)} %constant.35.clone.mirror_ref) | copy-start | bytes 516100
  3.3 40.8 %all-to-all-start = ((bf16[64,8,256]{2,1,0:T(8,128)(2,1)}), bf16[64,8,256]{2,1,0:T(8,128)(2,1)S(1)}, u32[]{:S(2)}, u32[]{:S(2)}) async-start(bf16[64,8,256]{2,1,0:T(8,128)(2,1)} %bitcast.16), calls=%async_computation | async-start | bytes 524288 | tf_op jit(solution)/shard_map/all_to_all | solution.py:303
  21.5 21.5 %collective-permute-start = (bf16[2,32,512]{2,1,0:T(8,128)(2,1)}, bf16[2,32,512]{2,1,0:T(8,128)(2,1)S(1)}, u32[]{:S(2)}, u32[]{:S(2)}) collective-permute-start(bf16[2,32,512]{2,1,0:T(8,128)(2,1)} %get-tuple-element.11), channel_id=1, source_target_pairs={{0,63},{1,62},{2,61},{3,60},{4,59},{5,58},{6,57},{7,56},{8,55},{9,... | collective-permute-start | bytes 196616 | tf_op jit(solution)/shard_map/ppermute | solution.py:304
  27.5 12.1 %collective-permute-start.1 = (bf16[2,8,512]{2,1,0:T(8,128)(2,1)S(1)}, bf16[2,8,512]{2,1,0:T(8,128)(2,1)S(1)}, u32[]{:S(2)}, u32[]{:S(2)}) collective-permute-start(bf16[2,8,512]{2,1,0:T(8,128)(2,1)S(1)} %copy-done.10), channel_id=1, source_target_pairs={{0,31},{1,0},{2,1},{3,2},{4,3},{5,4},{6,5},{7,6},{8,7},{9,8},{10,9... | collective-permute-start | bytes 49160 | tf_op jit(solution)/shard_map/ppermute | solution.py:305
  27.6 16.5 %copy-start.3 = (bf16[512,512]{1,0:T(8,128)(2,1)S(1)}, bf16[512,512]{1,0:T(8,128)(2,1)}, u32[]{:S(2)}) copy-start(bf16[512,512]{1,0:T(8,128)(2,1)} %constant.29.clone.wc_ref) | copy-start | bytes 1572868
  27.6 16.5 %copy-start.4 = (bf16[512,512]{1,0:T(8,128)(2,1)S(1)}, bf16[512,512]{1,0:T(8,128)(2,1)}, u32[]{:S(2)}) copy-start(bf16[512,512]{1,0:T(8,128)(2,1)} %constant.30.clone.ws_ref) | copy-start | bytes 1572868
  27.6 16.5 %copy-start.7 = (bf16[2,2,48,256]{3,2,1,0:T(8,128)(2,1)S(1)}, bf16[2,2,48,256]{3,2,1,0:T(8,128)(2,1)}, u32[]{:S(2)}) copy-start(bf16[2,2,48,256]{3,2,1,0:T(8,128)(2,1)} %constant.38.clone.gather_ref) | copy-start | bytes 294916
  47.1 8.6 %copy-start.8 = (bf16[4,64,112]{2,1,0:T(8,128)(2,1)S(1)}, bf16[4,64,112]{2,1,0:T(8,128)(2,1)}, u32[]{:S(2)}) copy-start(bf16[4,64,112]{2,1,0:T(8,128)(2,1)} %constant.36.clone.own_ref) | copy-start | bytes 172036
  47.1 8.6 %copy-start.9 = (bf16[4,64,112]{2,1,0:T(8,128)(2,1)S(1)}, bf16[4,64,112]{2,1,0:T(8,128)(2,1)}, u32[]{:S(2)}) copy-start(bf16[4,64,112]{2,1,0:T(8,128)(2,1)} %constant.37.clone.mirror_ref) | copy-start | bytes 172036
  47.1 8.5 %collective-permute-start.2 = (bf16[2,32,512]{2,1,0:T(8,128)(2,1)S(1)}, bf16[2,32,512]{2,1,0:T(8,128)(2,1)S(1)}, u32[]{:S(2)}, u32[]{:S(2)}) collective-permute-start(bf16[2,32,512]{2,1,0:T(8,128)(2,1)S(1)} %slice.9), channel_id=1, source_target_pairs={{0,63},{1,62},{2,61},{3,60},{4,59},{5,58},{6,57},{7,56},{8,55},{9,... | collective-permute-start | bytes 196616 | tf_op jit(solution)/shard_map/ppermute | solution.py:326
  49.2 2.7 %collective-permute-start.3 = (bf16[2,8,512]{2,1,0:T(8,128)(2,1)S(1)}, bf16[2,8,512]{2,1,0:T(8,128)(2,1)S(1)}, u32[]{:S(2)}, u32[]{:S(2)}) collective-permute-start(bf16[2,8,512]{2,1,0:T(8,128)(2,1)S(1)} %slice_select_fusion), channel_id=1, source_target_pairs={{31,0},{0,1},{1,2},{2,3},{3,4},{4,5},{5,6},{6,7},{7,8},{8,9},{9,10... | collective-permute-start | bytes 49160 | tf_op jit(solution)/shard_map/ppermute | solution.py:328
  56.3 18.0 %collective-permute-start.4 = (bf16[2,64,512]{2,1,0:T(8,128)(2,1)S(1)}, bf16[2,64,512]{2,1,0:T(8,128)(2,1)S(1)}, u32[]{:S(2)}, u32[]{:S(2)}) collective-permute-start(bf16[2,64,512]{2,1,0:T(8,128)(2,1)S(1)} %shard_map.161), channel_id=1, source_target_pairs={{0,128},{64,192},{128,0},{192,64},{256,384},{320,448},{384,256},{4... | collective-permute-start | bytes 393224 | tf_op jit(solution)/shard_map/ppermute | solution.py:340
  59.5 37.1 %all-to-all-start.1 = ((bf16[64,8,256]{2,1,0:T(8,128)(2,1)}), bf16[64,8,256]{2,1,0:T(8,128)(2,1)S(1)}, u32[]{:S(2)}, u32[]{:S(2)}) async-start(bf16[64,8,256]{2,1,0:T(8,128)(2,1)} %bitcast.6), calls=%async_computation.1 | async-start | bytes 524288 | tf_op jit(solution)/shard_map/all_to_all | solution.py:329
  74.3 22.2 %copy-start.2 = (bf16[512,512]{1,0:T(8,128)(2,1)S(1)}, bf16[512,512]{1,0:T(8,128)(2,1)}, u32[]{:S(2)}) copy-start(bf16[512,512]{1,0:T(8,128)(2,1)} %constant.28.clone.t_ref) | copy-start | bytes 1572868
  74.4 8.1 %collective-permute-start.5 = (bf16[2,64,512]{2,1,0:T(8,128)(2,1)S(1)}, bf16[2,64,512]{2,1,0:T(8,128)(2,1)S(1)}, u32[]{:S(2)}, u32[]{:S(2)}) collective-permute-start(bf16[2,64,512]{2,1,0:T(8,128)(2,1)S(1)} %add_convert_fusion.2), channel_id=1, source_target_pairs={{0,256},{64,320},{128,384},{192,448},{256,0},{320,64},{384,128},{4... | collective-permute-start | bytes 393224 | tf_op jit(solution)/shard_map/ppermute | solution.py:340
  82.6 7.7 %collective-permute-start.6 = (bf16[2,64,512]{2,1,0:T(8,128)(2,1)S(1)}, bf16[2,64,512]{2,1,0:T(8,128)(2,1)S(1)}, u32[]{:S(2)}, u32[]{:S(2)}) collective-permute-start(bf16[2,64,512]{2,1,0:T(8,128)(2,1)S(1)} %add_convert_fusion.1), channel_id=1, source_target_pairs={{0,64},{64,0},{128,192},{192,128},{256,320},{320,256},{384,448},{4... | collective-permute-start | bytes 393224 | tf_op jit(solution)/shard_map/ppermute | solution.py:340

commit v7 on v6

--- a/solution.py
+++ b/solution.py
@@ -147,10 +147,11 @@
         tails_ref[ri] = dot(tail_ref[upper], f_ref[ri]).astype(BF)
         heads_ref[ri] = dot(head_ref[...], f_ref[ri]).astype(BF)
     turns = [turn(idx_ref, chan) for chan in range(2)]
-    for half, ref in enumerate((sig_ref, cot_ref)):
-        x = ref[...]
-        re = dot(x, t_ref[:, :HALF]).reshape(8, 2, ROWS, HALF)
-        im = dot(x, t_ref[:, HALF:]).reshape(8, 2, ROWS, HALF)
+    both = dot(jnp.concatenate([sig_ref[...], cot_ref[...]], axis=0), t_ref[...])
+    for half in range(2):
+        part = both[half * 128 : (half + 1) * 128]
+        re = part[:, :HALF].reshape(8, 2, ROWS, HALF)
+        im = part[:, HALF:].reshape(8, 2, ROWS, HALF)
         re, im = swap_first((re[:, 0], re[:, 1]), (im[:, 0], im[:, 1]))
         at = pl.ds(half * 128, 128)
         out_re = [re[c] * turns[c][0] - im[c] * turns[c][1] for c in range(2)]
@@ -193,34 +194,30 @@
 
 def kernel_b(idx_ref, r_ref, wc_ref, ws_ref, h_ref, gather_ref, v_ref, g_ref, prod):
     first = jnp.where(idx_ref[0] == LAST, 1, 0)
-    sign = jnp.where(lax.broadcasted_iota(jnp.int32, (128, 128), 1) < 64, -1.0, 1.0)
-    for k in range(4):
-        at = pl.ds(k * 128, 128)
-        p1 = dot(wc_ref[at, :], r_ref[...])
-        p2 = dot(ws_ref[at, :], r_ref[...])
-        pairs = []
-        for p in range(2):
-            cols = slice(p * 128, (p + 1) * 128)
-            x = p1[:, cols] + sign * pltpu.roll(p2[:, cols], 64, 1)
-            swapped = pltpu.roll(x, 64, 1)
-            h1 = h_ref[at, p * 128 : (p + 1) * 128]
-            h2 = h_ref[at, HALF + p * 128 : HALF + (p + 1) * 128]
-            prod[at, cols] = (h1 * x + h2 * swapped).astype(BF)
-            pairs.append((pltpu.roll(x, 112, 1) * x, pltpu.roll(x, 48, 1) * x))
-        for ri in range(2):
-            terms = jnp.concatenate([pairs[0][ri], pairs[1][ri]], axis=1)
-            high = terms.astype(BF)
-            low = (terms - high.astype(F32)).astype(BF)
-            take = gather_ref[first, ri]
-            total = dot(take, high, ((1,), (1,))) + dot(take, low, ((1,), (1,)))
-            g_ref[ri, :, at] = total.astype(BF)
-    for k in range(4):
-        at = pl.ds(k * 128, 128)
-        q1 = dot(wc_ref[at, :], prod[...])
-        q2 = dot(ws_ref[at, :], prod[...])
-        for p in range(2):
-            cols = slice(p * 128, (p + 1) * 128)
-            v_ref[at, cols] = (q1[:, cols] - sign * pltpu.roll(q2[:, cols], 64, 1)).astype(BF)
+    sign = jnp.where(lax.broadcasted_iota(jnp.int32, (N, 128), 1) < 64, -1.0, 1.0)
+    p1 = dot(wc_ref[...], r_ref[...])
+    p2 = dot(ws_ref[...], r_ref[...])
+    pairs = []
+    for p in range(2):
+        cols = slice(p * 128, (p + 1) * 128)
+        x = p1[:, cols] + sign * pltpu.roll(p2[:, cols], 64, 1)
+        swapped = pltpu.roll(x, 64, 1)
+        h1 = h_ref[:, p * 128 : (p + 1) * 128]
+        h2 = h_ref[:, HALF + p * 128 : HALF + (p + 1) * 128]
+        prod[:, cols] = (h1 * x + h2 * swapped).astype(BF)
+        pairs.append((pltpu.roll(x, 112, 1) * x, pltpu.roll(x, 48, 1) * x))
+    for ri in range(2):
+        terms = jnp.concatenate([pairs[0][ri], pairs[1][ri]], axis=1)
+        high = terms.astype(BF)
+        low = (terms - high.astype(F32)).astype(BF)
+        take = gather_ref[first, ri]
+        total = dot(take, high, ((1,), (1,))) + dot(take, low, ((1,), (1,)))
+        g_ref[ri] = total.astype(BF)
+    q1 = dot(wc_ref[...], prod[...])
+    q2 = dot(ws_ref[...], prod[...])
+    for p in range(2):
+        cols = slice(p * 128, (p + 1) * 128)
+        v_ref[:, cols] = (q1[:, cols] - sign * pltpu.roll(q2[:, cols], 64, 1)).astype(BF)
 
 
 def kernel_c(idx_ref, v_ref, t_ref, out_ref, grad_ref, z, yre, yim):

time: 98.3 us -> 97.4 us (level)
  no operation moved by 1% of the time
where the time goes in v7:
time: 97.4 us; the launch traced here: 97 us
  starting transfers between devices  55.2 us (57%)
  waiting for transfers between devices  32.4 us (33%)
  Pallas kernels  7.73 us (8%)
    all_to_all x1, starting transfers between devices, body(): got = lax.all_to_all(sent.reshape(SEQ, ROWS, HALF), 'seq', 0, 0, tiled=True)  18.2 us
    all_to_all x1, starting transfers between devices, body(): mid = lax.all_to_all(back.reshape(SEQ, ROWS, HALF), 'seq', 0, 0, tiled=True)  14.8 us
    ppermute x3, starting transfers between devices, body(): other = lax.ppermute(grad, 'dp', [(d, d ^ bit) for d in range(8)])  12.2 us
    ppermute x1, waiting for transfers between devices, body(): heads = lax.ppermute(heads, 'seq', down)  12 us
    ppermute x3, waiting for transfers between devices, body(): other = lax.ppermute(grad, 'dp', [(d, d ^ bit) for d in range(8)])  6.77 us
    ppermute x1, starting transfers between devices, body(): tails = lax.ppermute(tails, 'seq', opposite)  5.95 us
    all_to_all x1, waiting for transfers between devices, body(): mid = lax.all_to_all(back.reshape(SEQ, ROWS, HALF), 'seq', 0, 0, tiled=True)  5.63 us
    ppermute x1, waiting for transfers between devices, body(): far = lax.ppermute(grad[:, :32], 'seq', opposite)  3.78 us
  transfers between devices with their start and end apart: 9, of which 7 were waited for; matrix products, arithmetic and copies ran while one was open for 1% of the time, Pallas kernels for 1%

profile of v7, /device:TPU:1, one launch (start us, length us, event | category | flops | bytes accessed | tf_op | source)
XLA Modules:
  0.0 97.0 jit_solution(3934811045240595928)
XLA Ops:
  0.6 0.0 copy-start
  0.6 2.6 %shard_map.157 = (bf16[512,256]{1,0:T(8,128)(2,1)}, bf16[2,32,512]{2,1,0:T(8,128)(2,1)}, bf16[2,8,512]{2,1,0:T(8,128)(2,1)}) custom-call(s32[1]{0:T(128)} %bitcast.idx_ref, bf16[128,512]{1,0:T(8,128)(2,1)} %bitcast.17, bf16[128,512]{1,0:T(8,128)(2,1)} %bitcast.18, bf16[512,512]{1,0:T(8,128)(2,1)} %constant.28.clone.t_ref, bf16[2,64,512]{2,1,0:T(8,128)(2,1)} %bitcast.13, ...), custom_call_target="tpu_custom_call" | custom-call | tf_op jit(solution)/shard_map/pallas_call | solution.py:285
  3.3 0.0 copy-start.6
  3.3 18.2 %all-to-all-start = ((bf16[64,8,256]{2,1,0:T(8,128)(2,1)}), bf16[64,8,256]{2,1,0:T(8,128)(2,1)S(1)}, u32[]{:S(2)}, u32[]{:S(2)}) async-start(bf16[64,8,256]{2,1,0:T(8,128)(2,1)} %bitcast.16), calls=%async_computation | async-start | bytes 524288 | tf_op jit(solution)/shard_map/all_to_all | solution.py:300
  21.5 6.0 %collective-permute-start = (bf16[2,32,512]{2,1,0:T(8,128)(2,1)}, bf16[2,32,512]{2,1,0:T(8,128)(2,1)S(1)}, u32[]{:S(2)}, u32[]{:S(2)}) collective-permute-start(bf16[2,32,512]{2,1,0:T(8,128)(2,1)} %get-tuple-element.11), channel_id=1, source_target_pairs={{0,63},{1,62},{2,61},{3,60},{4,59},{5,58},{6,57},{7,56},{8,55},{9,... | collective-permute-start | bytes 196616 | tf_op jit(solution)/shard_map/ppermute | solution.py:301
  27.5 0.0 copy-done.10
  27.5 0.1 collective-permute-start.1
  27.6 12.0 %collective-permute-done.1.head_ref = bf16[2,8,512]{2,1,0:T(8,128)(2,1)S(1)} collective-permute-done((bf16[2,8,512]{2,1,0:T(8,128)(2,1)S(1)}, bf16[2,8,512]{2,1,0:T(8,128)(2,1)S(1)}, u32[]{:S(2)}, u32[]{:S(2)}) %collective-permute-start.1) | collective-permute-done | bytes 16416 | tf_op jit(solution)/shard_map/ppermute | solution.py:302
  39.6 3.4 %collective-permute-done.tail_ref = bf16[2,32,512]{2,1,0:T(8,128)(2,1)S(1)} collective-permute-done((bf16[2,32,512]{2,1,0:T(8,128)(2,1)}, bf16[2,32,512]{2,1,0:T(8,128)(2,1)S(1)}, u32[]{:S(2)}, u32[]{:S(2)}) %collective-permute-start) | collective-permute-done | bytes 65568 | tf_op jit(solution)/shard_map/ppermute | solution.py:301
  43.0 0.0 copy-done
  43.0 0.0 copy-done.5
  43.0 1.1 %shard_map.158.h_ref = f32[512,512]{1,0:T(8,128)S(1)} custom-call(s32[1]{0:T(128)} %bitcast.idx_ref, bf16[2,64,512]{2,1,0:T(8,128)(2,1)S(1)} %bitcast.14, bf16[2,32,512]{2,1,0:T(8,128)(2,1)S(1)} %collective-permute-done.tail_ref, bf16[2,8,512]{2,1,0:T(8,128)(2,1)S(1)} %collective-permute-done.1.head_ref, bf16[3,112,256]{2,1,0:T(8,128)(2,1)S(1)} %copy-done.5, ...), custom_call_target="tpu_custom_call" | custom-call | flops 400000000 | bytes 2000000 | tf_op jit(solution)/shard_map/pallas_call | solution.py:303
  44.1 0.0 all-to-all-done
  44.1 0.0 copy-done.3
  44.1 0.0 copy-done.4
  44.2 2.1 %shard_map.159 = (bf16[512,256]{1,0:T(8,128)(2,1)}, bf16[2,48,512]{2,1,0:T(8,128)(2,1)S(1)}) custom-call(s32[1]{0:T(128)} %bitcast.idx_ref, bf16[512,256]{1,0:T(8,128)(2,1)S(1)} %bitcast.12, bf16[512,512]{1,0:T(8,128)(2,1)S(1)} %copy-done.3, bf16[512,512]{1,0:T(8,128)(2,1)S(1)} %copy-done.4, f32[512,512]{1,0:T(8,128)S(1)} %shard_map.158.h_ref, ...), custom_call_target="tpu_custom_call" | custom-call | tf_op jit(solution)/shard_map/pallas_call | solution.py:312
  46.2 2.1 %collective-permute-start.2 = (bf16[2,32,512]{2,1,0:T(8,128)(2,1)S(1)}, bf16[2,32,512]{2,1,0:T(8,128)(2,1)S(1)}, u32[]{:S(2)}, u32[]{:S(2)}) collective-permute-start(bf16[2,32,512]{2,1,0:T(8,128)(2,1)S(1)} %slice.9), channel_id=1, source_target_pairs={{0,63},{1,62},{2,61},{3,60},{4,59},{5,58},{6,57},{7,56},{8,55},{9,... | collective-permute-start | bytes 196616 | tf_op jit(solution)/shard_map/ppermute | solution.py:323
  48.3 1.8 %collective-permute-start.3 = (bf16[2,8,512]{2,1,0:T(8,128)(2,1)S(1)}, bf16[2,8,512]{2,1,0:T(8,128)(2,1)S(1)}, u32[]{:S(2)}, u32[]{:S(2)}) collective-permute-start(bf16[2,8,512]{2,1,0:T(8,128)(2,1)S(1)} %slice_select_fusion), channel_id=1, source_target_pairs={{31,0},{0,1},{1,2},{2,3},{3,4},{4,5},{5,6},{6,7},{7,8},{8,9},{9,10... | collective-permute-start | bytes 49160 | tf_op jit(solution)/shard_map/ppermute | solution.py:325
  50.1 0.9 collective-permute-done.3.head_ref
  51.0 3.8 %collective-permute-done.2.far_ref = bf16[2,32,512]{2,1,0:T(8,128)(2,1)S(1)} collective-permute-done((bf16[2,32,512]{2,1,0:T(8,128)(2,1)S(1)}, bf16[2,32,512]{2,1,0:T(8,128)(2,1)S(1)}, u32[]{:S(2)}, u32[]{:S(2)}) %collective-permute-start.2) | collective-permute-done | bytes 65568 | tf_op jit(solution)/shard_map/ppermute | solution.py:323
  54.8 0.6 shard_map.161
  55.4 3.2 %collective-permute-start.4 = (bf16[2,64,512]{2,1,0:T(8,128)(2,1)S(1)}, bf16[2,64,512]{2,1,0:T(8,128)(2,1)S(1)}, u32[]{:S(2)}, u32[]{:S(2)}) collective-permute-start(bf16[2,64,512]{2,1,0:T(8,128)(2,1)S(1)} %shard_map.161), channel_id=1, source_target_pairs={{0,128},{64,192},{128,0},{192,64},{256,384},{320,448},{384,256},{4... | collective-permute-start | bytes 393224 | tf_op jit(solution)/shard_map/ppermute | solution.py:337
  58.6 14.8 %all-to-all-start.1 = ((bf16[64,8,256]{2,1,0:T(8,128)(2,1)}), bf16[64,8,256]{2,1,0:T(8,128)(2,1)S(1)}, u32[]{:S(2)}, u32[]{:S(2)}) async-start(bf16[64,8,256]{2,1,0:T(8,128)(2,1)} %bitcast.6), calls=%async_computation.1 | async-start | bytes 524288 | tf_op jit(solution)/shard_map/all_to_all | solution.py:326
  73.5 0.0 copy-start.2
  73.5 0.0 collective-permute-done.4
  73.5 4.7 %collective-permute-start.5 = (bf16[2,64,512]{2,1,0:T(8,128)(2,1)S(1)}, bf16[2,64,512]{2,1,0:T(8,128)(2,1)S(1)}, u32[]{:S(2)}, u32[]{:S(2)}) collective-permute-start(bf16[2,64,512]{2,1,0:T(8,128)(2,1)S(1)} %add_convert_fusion.2), channel_id=1, source_target_pairs={{0,256},{64,320},{128,384},{192,448},{256,0},{320,64},{384,128},{4... | collective-permute-start | bytes 393224 | tf_op jit(solution)/shard_map/ppermute | solution.py:337
  78.2 3.5 %collective-permute-done.5 = bf16[2,64,512]{2,1,0:T(8,128)(2,1)S(1)} collective-permute-done((bf16[2,64,512]{2,1,0:T(8,128)(2,1)S(1)}, bf16[2,64,512]{2,1,0:T(8,128)(2,1)S(1)}, u32[]{:S(2)}, u32[]{:S(2)}) %collective-permute-start.5) | collective-permute-done | bytes 131104 | tf_op jit(solution)/shard_map/ppermute | solution.py:337
  81.7 4.4 %collective-permute-start.6 = (bf16[2,64,512]{2,1,0:T(8,128)(2,1)S(1)}, bf16[2,64,512]{2,1,0:T(8,128)(2,1)S(1)}, u32[]{:S(2)}, u32[]{:S(2)}) collective-permute-start(bf16[2,64,512]{2,1,0:T(8,128)(2,1)S(1)} %add_convert_fusion.1), channel_id=1, source_target_pairs={{0,64},{64,0},{128,192},{192,128},{256,320},{320,256},{384,448},{4... | collective-permute-start | bytes 393224 | tf_op jit(solution)/shard_map/ppermute | solution.py:337
  86.1 3.3 %collective-permute-done.6 = bf16[2,64,512]{2,1,0:T(8,128)(2,1)S(1)} collective-permute-done((bf16[2,64,512]{2,1,0:T(8,128)(2,1)S(1)}, bf16[2,64,512]{2,1,0:T(8,128)(2,1)S(1)}, u32[]{:S(2)}, u32[]{:S(2)}) %collective-permute-start.6) | collective-permute-done | bytes 131104 | tf_op jit(solution)/shard_map/ppermute | solution.py:337
  89.4 0.7 fusion
  90.1 5.6 %all-to-all-done.1 = bf16[64,8,256]{2,1,0:T(8,128)(2,1)S(1)} async-done(((bf16[64,8,256]{2,1,0:T(8,128)(2,1)}), bf16[64,8,256]{2,1,0:T(8,128)(2,1)S(1)}, u32[]{:S(2)}, u32[]{:S(2)}) %all-to-all-start.1) | async-done | bytes 262176 | tf_op jit(solution)/shard_map/all_to_all | solution.py:326
  95.7 1.3 %shard_map.160 = (bf16[128,512]{1,0:T(8,128)(2,1)}, bf16[128,512]{1,0:T(8,128)(2,1)}) custom-call(s32[1]{0:T(128)} %bitcast.idx_ref, bf16[512,256]{1,0:T(8,128)(2,1)S(1)} %bitcast.15, bf16[512,512]{1,0:T(8,128)(2,1)S(1)} %copy-done.2), custom_call_target="tpu_custom_call" | custom-call | flops 400000000 | bytes 2000000 | tf_op jit(solution)/shard_map/pallas_call | solution.py:339
  (18 shorter events, 0.1 us)
Async XLA Ops:
  0.6 42.4 %copy-start = (bf16[512,512]{1,0:T(8,128)(2,1)S(1)}, bf16[512,512]{1,0:T(8,128)(2,1)}, u32[]{:S(2)}) copy-start(bf16[512,512]{1,0:T(8,128)(2,1)} %constant.31.clone.flip_ref) | copy-start | bytes 1572868
  3.3 24.2 %copy-start.10 = (bf16[2,8,512]{2,1,0:T(8,128)(2,1)S(1)}, bf16[2,8,512]{2,1,0:T(8,128)(2,1)}, u32[]{:S(2)}) copy-start(bf16[2,8,512]{2,1,0:T(8,128)(2,1)} %get-tuple-element.12) | copy-start | bytes 49156
  3.3 39.7 %copy-start.1 = (bf16[2,8,8,512]{3,2,1,0:T(8,128)(2,1)S(1)}, bf16[2,8,8,512]{3,2,1,0:T(8,128)(2,1)}, u32[]{:S(2)}) copy-start(bf16[2,8,8,512]{3,2,1,0:T(8,128)(2,1)} %param.16) | copy-start | bytes 393220
  3.3 39.7 %copy-start.5 = (bf16[3,112,256]{2,1,0:T(8,128)(2,1)S(1)}, bf16[3,112,256]{2,1,0:T(8,128)(2,1)}, u32[]{:S(2)}) copy-start(bf16[3,112,256]{2,1,0:T(8,128)(2,1)} %constant.34.clone.own_ref) | copy-start | bytes 516100
  3.3 39.7 %copy-start.6 = (bf16[3,112,256]{2,1,0:T(8,128)(2,1)S(1)}, bf16[3,112,256]{2,1,0:T(8,128)(2,1)}, u32[]{:S(2)}) copy-start(bf16[3,112,256]{2,1,0:T(8,128)(2,1)} %constant.35.clone.mirror_ref) | copy-start | bytes 516100
  3.3 40.8 %all-to-all-start = ((bf16[64,8,256]{2,1,0:T(8,128)(2,1)}), bf16[64,8,256]{2,1,0:T(8,128)(2,1)S(1)}, u32[]{:S(2)}, u32[]{:S(2)}) async-start(bf16[64,8,256]{2,1,0:T(8,128)(2,1)} %bitcast.16), calls=%async_computation | async-start | bytes 524288 | tf_op jit(solution)/shard_map/all_to_all | solution.py:300
  21.5 21.5 %collective-permute-start = (bf16[2,32,512]{2,1,0:T(8,128)(2,1)}, bf16[2,32,512]{2,1,0:T(8,128)(2,1)S(1)}, u32[]{:S(2)}, u32[]{:S(2)}) collective-permute-start(bf16[2,32,512]{2,1,0:T(8,128)(2,1)} %get-tuple-element.11), channel_id=1, source_target_pairs={{0,63},{1,62},{2,61},{3,60},{4,59},{5,58},{6,57},{7,56},{8,55},{9,... | collective-permute-start | bytes 196616 | tf_op jit(solution)/shard_map/ppermute | solution.py:301
  27.5 12.1 %collective-permute-start.1 = (bf16[2,8,512]{2,1,0:T(8,128)(2,1)S(1)}, bf16[2,8,512]{2,1,0:T(8,128)(2,1)S(1)}, u32[]{:S(2)}, u32[]{:S(2)}) collective-permute-start(bf16[2,8,512]{2,1,0:T(8,128)(2,1)S(1)} %copy-done.10), channel_id=1, source_target_pairs={{0,31},{1,0},{2,1},{3,2},{4,3},{5,4},{6,5},{7,6},{8,7},{9,8},{10,9... | collective-permute-start | bytes 49160 | tf_op jit(solution)/shard_map/ppermute | solution.py:302
  27.6 16.5 %copy-start.3 = (bf16[512,512]{1,0:T(8,128)(2,1)S(1)}, bf16[512,512]{1,0:T(8,128)(2,1)}, u32[]{:S(2)}) copy-start(bf16[512,512]{1,0:T(8,128)(2,1)} %constant.29.clone.wc_ref) | copy-start | bytes 1572868
  27.6 16.5 %copy-start.4 = (bf16[512,512]{1,0:T(8,128)(2,1)S(1)}, bf16[512,512]{1,0:T(8,128)(2,1)}, u32[]{:S(2)}) copy-start(bf16[512,512]{1,0:T(8,128)(2,1)} %constant.30.clone.ws_ref) | copy-start | bytes 1572868
  27.6 16.5 %copy-start.7 = (bf16[2,2,48,256]{3,2,1,0:T(8,128)(2,1)S(1)}, bf16[2,2,48,256]{3,2,1,0:T(8,128)(2,1)}, u32[]{:S(2)}) copy-start(bf16[2,2,48,256]{3,2,1,0:T(8,128)(2,1)} %constant.38.clone.gather_ref) | copy-start | bytes 294916
  46.2 8.6 %copy-start.8 = (bf16[4,64,112]{2,1,0:T(8,128)(2,1)S(1)}, bf16[4,64,112]{2,1,0:T(8,128)(2,1)}, u32[]{:S(2)}) copy-start(bf16[4,64,112]{2,1,0:T(8,128)(2,1)} %constant.36.clone.own_ref) | copy-start | bytes 172036
  46.2 8.6 %copy-start.9 = (bf16[4,64,112]{2,1,0:T(8,128)(2,1)S(1)}, bf16[4,64,112]{2,1,0:T(8,128)(2,1)}, u32[]{:S(2)}) copy-start(bf16[4,64,112]{2,1,0:T(8,128)(2,1)} %constant.37.clone.mirror_ref) | copy-start | bytes 172036
  46.2 8.5 %collective-permute-start.2 = (bf16[2,32,512]{2,1,0:T(8,128)(2,1)S(1)}, bf16[2,32,512]{2,1,0:T(8,128)(2,1)S(1)}, u32[]{:S(2)}, u32[]{:S(2)}) collective-permute-start(bf16[2,32,512]{2,1,0:T(8,128)(2,1)S(1)} %slice.9), channel_id=1, source_target_pairs={{0,63},{1,62},{2,61},{3,60},{4,59},{5,58},{6,57},{7,56},{8,55},{9,... | collective-permute-start | bytes 196616 | tf_op jit(solution)/shard_map/ppermute | solution.py:323
  48.3 2.7 %collective-permute-start.3 = (bf16[2,8,512]{2,1,0:T(8,128)(2,1)S(1)}, bf16[2,8,512]{2,1,0:T(8,128)(2,1)S(1)}, u32[]{:S(2)}, u32[]{:S(2)}) collective-permute-start(bf16[2,8,512]{2,1,0:T(8,128)(2,1)S(1)} %slice_select_fusion), channel_id=1, source_target_pairs={{31,0},{0,1},{1,2},{2,3},{3,4},{4,5},{5,6},{6,7},{7,8},{8,9},{9,10... | collective-permute-start | bytes 49160 | tf_op jit(solution)/shard_map/ppermute | solution.py:325
  55.4 18.0 %collective-permute-start.4 = (bf16[2,64,512]{2,1,0:T(8,128)(2,1)S(1)}, bf16[2,64,512]{2,1,0:T(8,128)(2,1)S(1)}, u32[]{:S(2)}, u32[]{:S(2)}) collective-permute-start(bf16[2,64,512]{2,1,0:T(8,128)(2,1)S(1)} %shard_map.161), channel_id=1, source_target_pairs={{0,128},{64,192},{128,0},{192,64},{256,384},{320,448},{384,256},{4... | collective-permute-start | bytes 393224 | tf_op jit(solution)/shard_map/ppermute | solution.py:337
  58.6 37.1 %all-to-all-start.1 = ((bf16[64,8,256]{2,1,0:T(8,128)(2,1)}), bf16[64,8,256]{2,1,0:T(8,128)(2,1)S(1)}, u32[]{:S(2)}, u32[]{:S(2)}) async-start(bf16[64,8,256]{2,1,0:T(8,128)(2,1)} %bitcast.6), calls=%async_computation.1 | async-start | bytes 524288 | tf_op jit(solution)/shard_map/all_to_all | solution.py:326
  73.5 22.2 %copy-start.2 = (bf16[512,512]{1,0:T(8,128)(2,1)S(1)}, bf16[512,512]{1,0:T(8,128)(2,1)}, u32[]{:S(2)}) copy-start(bf16[512,512]{1,0:T(8,128)(2,1)} %constant.28.clone.t_ref) | copy-start | bytes 1572868
  73.5 8.1 %collective-permute-start.5 = (bf16[2,64,512]{2,1,0:T(8,128)(2,1)S(1)}, bf16[2,64,512]{2,1,0:T(8,128)(2,1)S(1)}, u32[]{:S(2)}, u32[]{:S(2)}) collective-permute-start(bf16[2,64,512]{2,1,0:T(8,128)(2,1)S(1)} %add_convert_fusion.2), channel_id=1, source_target_pairs={{0,256},{64,320},{128,384},{192,448},{256,0},{320,64},{384,128},{4... | collective-permute-start | bytes 393224 | tf_op jit(solution)/shard_map/ppermute | solution.py:337
  81.7 7.7 %collective-permute-start.6 = (bf16[2,64,512]{2,1,0:T(8,128)(2,1)S(1)}, bf16[2,64,512]{2,1,0:T(8,128)(2,1)S(1)}, u32[]{:S(2)}, u32[]{:S(2)}) collective-permute-start(bf16[2,64,512]{2,1,0:T(8,128)(2,1)S(1)} %add_convert_fusion.1), channel_id=1, source_target_pairs={{0,64},{64,0},{128,192},{192,128},{256,320},{320,256},{384,448},{4... | collective-permute-start | bytes 393224 | tf_op jit(solution)/shard_map/ppermute | solution.py:337

commit v8 on v7

--- a/solution.py
+++ b/solution.py
@@ -108,13 +108,13 @@
 
 
 def payload_selectors():
-    tail = np.zeros((2, 32, 64), np.float32)
+    tail = np.zeros((2, 2, 16, 64), np.float32)
     head = np.zeros((8, 64), np.float32)
     for f in range(8):
         head[f, f * 8] = 1
         for row in range(4):
-            tail[0, f * 4 + row, f * 8 + 4 + row] = 1
-            tail[1, f * 4 + row, f * 8 + (4 + row if row else 0)] = 1
+            tail[0, f // 4, f % 4 * 4 + row, f * 8 + 4 + row] = 1
+            tail[1, f // 4, f % 4 * 4 + row, f * 8 + (4 + row if row else 0)] = 1
     return tail.astype(BF), head.astype(BF)
 
 
@@ -140,11 +140,11 @@
     return (re[0], jnp.where(first, im[0], re[1])), (jnp.where(first, re[1], im[0]), im[1])
 
 
-def kernel_a(idx_ref, sig_ref, cot_ref, t_ref, f_ref, tail_ref, head_ref, out_ref, tails_ref,
+def kernel_a(idx_ref, rank_ref, sig_ref, cot_ref, t_ref, f_ref, tail_ref, head_ref, out_ref, tails_ref,
              heads_ref, yre, yim, z):
     upper = idx_ref[0] >> 5
     for ri in range(2):
-        tails_ref[ri] = dot(tail_ref[upper], f_ref[ri]).astype(BF)
+        tails_ref[ri] = dot(tail_ref[upper, rank_ref[0] & 1], f_ref[ri]).astype(BF)
         heads_ref[ri] = dot(head_ref[...], f_ref[ri]).astype(BF)
     turns = [turn(idx_ref, chan) for chan in range(2)]
     both = dot(jnp.concatenate([sig_ref[...], cot_ref[...]], axis=0), t_ref[...])
@@ -169,11 +169,13 @@
         out_ref[:, p * 128 : (p + 1) * 128] = z[p].astype(BF)
 
 
-def kernel_f(idx_ref, f_ref, tail_ref, head_ref, own_ref, mirror_ref, flip_ref, h_ref, rows):
+def kernel_f(idx_ref, rank_ref, f_ref, tail_ref, share_ref, head_ref, own_ref, mirror_ref, flip_ref, h_ref, rows):
     place = idx_ref[0]
     kind = jnp.where(place == LAST, 0, jnp.where(place < 32, 1, 2))
     rows[:, :64, :] = f_ref[...]
-    rows[:, 64:96, :] = tail_ref[...]
+    half = rank_ref[0] & 1
+    rows[:, pl.ds(pl.multiple_of(64 + 16 * half, 16), 16), :] = tail_ref[...]
+    rows[:, pl.ds(pl.multiple_of(80 - 16 * half, 16), 16), :] = share_ref[...]
     rows[:, 96:, :] = jnp.zeros((2, 16, N), BF)
     rows[:, 96:104, :] = head_ref[...]
     lane = lax.broadcasted_iota(jnp.int32, (N, HALF), 1)
@@ -271,6 +273,7 @@
 def body(signal, cotangent, filter_spec):
     shape = signal.shape
     place = lax.axis_index("seq").astype(jnp.int32).reshape(1)
+    rank = lax.axis_index("dp").astype(jnp.int32).reshape(1)
     table = jnp.asarray(first_table())
     cos_t, sin_t = (jnp.asarray(t) for t in unit_tables())
     flip = jnp.asarray(np.eye(N, dtype=np.float32)[::-1].astype(BF))
@@ -284,11 +287,11 @@
     filt = filter_spec.reshape(2, 64, N)
     sent, tails, heads = pl.pallas_call(
         kernel_a,
-        in_specs=[SMEM] + [VMEM] * 6,
+        in_specs=[SMEM] * 2 + [VMEM] * 6,
         out_specs=[VMEM] * 3,
         out_shape=[
             jax.ShapeDtypeStruct((N, HALF), BF),
-            jax.ShapeDtypeStruct((2, 32, N), BF),
+            jax.ShapeDtypeStruct((2, 16, N), BF),
             jax.ShapeDtypeStruct((2, 8, N), BF),
         ],
         scratch_shapes=[
@@ -296,19 +299,20 @@
             pltpu.VMEM((2, 256, 128), F32),
             pltpu.VMEM((2, N, 128), F32),
         ],
-    )(place, signal.reshape(128, N), cotangent.reshape(128, N), table, filt, tail, head)
+    )(place, rank, signal.reshape(128, N), cotangent.reshape(128, N), table, filt, tail, head)
     got = lax.all_to_all(sent.reshape(SEQ, ROWS, HALF), "seq", 0, 0, tiled=True)
     tails = lax.ppermute(tails, "seq", opposite)
     heads = lax.ppermute(heads, "seq", down)
+    share = lax.ppermute(tails, "dp", [(d, d ^ 1) for d in range(8)])
     spread = pl.pallas_call(
         kernel_f,
-        in_specs=[SMEM] + [VMEM] * 6,
+        in_specs=[SMEM] * 2 + [VMEM] * 7,
         out_specs=VMEM,
         out_shape=jax.ShapeDtypeStruct((N, N), F32),
         scratch_shapes=[pltpu.VMEM((2, 112, N), BF)],
         compiler_params=PARAMS,
         cost_estimate=pl.CostEstimate(flops=400000000, bytes_accessed=2000000, transcendentals=0),
-    )(place, filt, tails, heads, f_own, f_mirror, flip)
+    )(place, rank, filt, tails, share, heads, f_own, f_mirror, flip)
     back, grad = pl.pallas_call(
         kernel_b,
         in_specs=[SMEM] + [VMEM] * 5,

time: 97.4 us -> 103 us (1.057)
  starting transfers between devices: 55.2 us -> 59.2 us
  waiting for transfers between devices: 32.4 us -> 33.5 us
    ppermute x1, waiting for transfers between devices: 3.42 us -> 12.7 us  [body(): tails = lax.ppermute(tails, 'seq', opposite)]
    ppermute x1, waiting for transfers between devices: 12 us -> 3.11 us  [body(): heads = lax.ppermute(heads, 'seq', down)]
    ppermute x0 -> x1, starting transfers between devices: none -> 4.35 us  [body(): share = lax.ppermute(tails, 'dp', [(d, d ^ 1) for d in range(8)])]
  transfers between devices with their start and end apart: 9 -> 10, of which waited for: 7 -> 7; matrix products, arithmetic and copies ran while one was open for 1% -> 1% of each run, Pallas kernels for 1% -> 1%
where the time goes in v8:
time: 103 us; the launch traced here: 102 us
  starting transfers between devices  59.2 us (57%)
  waiting for transfers between devices  33.5 us (33%)
  Pallas kernels  7.7 us (7%)
    all_to_all x1, starting transfers between devices, body(): got = lax.all_to_all(sent.reshape(SEQ, ROWS, HALF), 'seq', 0, 0, tiled=True)  18.2 us
    all_to_all x1, starting transfers between devices, body(): mid = lax.all_to_all(back.reshape(SEQ, ROWS, HALF), 'seq', 0, 0, tiled=True)  15.1 us
    ppermute x1, waiting for transfers between devices, body(): tails = lax.ppermute(tails, 'seq', opposite)  12.7 us
    ppermute x3, starting transfers between devices, body(): other = lax.ppermute(grad, 'dp', [(d, d ^ bit) for d in range(8)])  11.5 us
    ppermute x3, waiting for transfers between devices, body(): other = lax.ppermute(grad, 'dp', [(d, d ^ bit) for d in range(8)])  7.58 us
    ppermute x1, starting transfers between devices, body(): tails = lax.ppermute(tails, 'seq', opposite)  5.95 us
    all_to_all x1, waiting for transfers between devices, body(): mid = lax.all_to_all(back.reshape(SEQ, ROWS, HALF), 'seq', 0, 0, tiled=True)  5.54 us
    ppermute x1, starting transfers between devices, body(): share = lax.ppermute(tails, 'dp', [(d, d ^ 1) for d in range(8)])  4.35 us
  transfers between devices with their start and end apart: 10, of which 7 were waited for; matrix products, arithmetic and copies ran while one was open for 1% of the time, Pallas kernels for 1%

profile of v8, /device:TPU:1, one launch (start us, length us, event | category | flops | bytes accessed | tf_op | source)
XLA Modules:
  0.0 102.2 jit_solution(1465739504573436635)
XLA Ops:
  0.6 0.0 copy-start
  0.6 2.6 %shard_map.157 = (bf16[512,256]{1,0:T(8,128)(2,1)}, bf16[2,16,512]{2,1,0:T(8,128)(2,1)}, bf16[2,8,512]{2,1,0:T(8,128)(2,1)}) custom-call(s32[1]{0:T(128)} %bitcast.idx_ref, s32[1]{0:T(128)} %bitcast.1.rank_ref, bf16[128,512]{1,0:T(8,128)(2,1)} %bitcast.18, bf16[128,512]{1,0:T(8,128)(2,1)} %bitcast.19, bf16[512,512]{1,0:T(8,128)(2,1)} %constant.33.clone.t_ref, ...), custom_call_target="tpu_custom_call" | custom-call | tf_op jit(solution)/shard_map/pallas_call | solution.py:288
  3.2 0.0 copy-start.5
  3.3 0.0 copy-start.6
  3.3 18.2 %all-to-all-start = ((bf16[64,8,256]{2,1,0:T(8,128)(2,1)}), bf16[64,8,256]{2,1,0:T(8,128)(2,1)S(1)}, u32[]{:S(2)}, u32[]{:S(2)}) async-start(bf16[64,8,256]{2,1,0:T(8,128)(2,1)} %bitcast.17), calls=%async_computation | async-start | bytes 524288 | tf_op jit(solution)/shard_map/all_to_all | solution.py:303
  21.5 6.0 %collective-permute-start = (bf16[2,16,512]{2,1,0:T(8,128)(2,1)S(1)}, bf16[2,16,512]{2,1,0:T(8,128)(2,1)S(1)}, u32[]{:S(2)}, u32[]{:S(2)}) collective-permute-start(bf16[2,16,512]{2,1,0:T(8,128)(2,1)S(1)} %copy-done.10), channel_id=1, source_target_pairs={{0,63},{1,62},{2,61},{3,60},{4,59},{5,58},{6,57},{7,56},{8,55},{9,... | collective-permute-start | bytes 98312 | tf_op jit(solution)/shard_map/ppermute | solution.py:304
  27.5 12.7 %collective-permute-done.tail_ref = bf16[2,16,512]{2,1,0:T(8,128)(2,1)S(1)} collective-permute-done((bf16[2,16,512]{2,1,0:T(8,128)(2,1)S(1)}, bf16[2,16,512]{2,1,0:T(8,128)(2,1)S(1)}, u32[]{:S(2)}, u32[]{:S(2)}) %collective-permute-start) | collective-permute-done | bytes 32800 | tf_op jit(solution)/shard_map/ppermute | solution.py:304
  40.1 4.3 %collective-permute-start.1 = (bf16[2,16,512]{2,1,0:T(8,128)(2,1)S(1)}, bf16[2,16,512]{2,1,0:T(8,128)(2,1)S(1)}, u32[]{:S(2)}, u32[]{:S(2)}) collective-permute-start(bf16[2,16,512]{2,1,0:T(8,128)(2,1)S(1)} %collective-permute-done.tail_ref), channel_id=1, source_target_pairs={{0,64},{64,0},{128,192},{192,128},{256,320},{320,256},{384,448},{4... | collective-permute-start | bytes 98312 | tf_op jit(solution)/shard_map/ppermute | solution.py:306
  44.5 0.0 collective-permute-start.2
  44.5 0.0 copy-start.2
  44.5 0.0 copy-start.3
  44.6 0.0 copy-start.7
  44.6 3.1 %collective-permute-done.2.head_ref = bf16[2,8,512]{2,1,0:T(8,128)(2,1)S(1)} collective-permute-done((bf16[2,8,512]{2,1,0:T(8,128)(2,1)S(1)}, bf16[2,8,512]{2,1,0:T(8,128)(2,1)S(1)}, u32[]{:S(2)}, u32[]{:S(2)}) %collective-permute-start.2) | collective-permute-done | bytes 16416 | tf_op jit(solution)/shard_map/ppermute | solution.py:305
  47.7 0.0 collective-permute-done.1.share_ref
  47.7 1.1 %shard_map.158.h_ref = f32[512,512]{1,0:T(8,128)S(1)} custom-call(s32[1]{0:T(128)} %bitcast.idx_ref, s32[1]{0:T(128)} %bitcast.1.rank_ref, bf16[2,64,512]{2,1,0:T(8,128)(2,1)S(1)} %bitcast.15, bf16[2,16,512]{2,1,0:T(8,128)(2,1)S(1)} %collective-permute-done.tail_ref, bf16[2,16,512]{2,1,0:T(8,128)(2,1)S(1)} %collective-permute-done.1.share_ref, ...), custom_call_target="tpu_custom_call" | custom-call | flops 400000000 | bytes 2000000 | tf_op jit(solution)/shard_map/pallas_call | solution.py:307
  48.8 0.0 all-to-all-done
  48.9 2.1 %shard_map.159 = (bf16[512,256]{1,0:T(8,128)(2,1)}, bf16[2,48,512]{2,1,0:T(8,128)(2,1)S(1)}) custom-call(s32[1]{0:T(128)} %bitcast.idx_ref, bf16[512,256]{1,0:T(8,128)(2,1)S(1)} %bitcast.13, bf16[512,512]{1,0:T(8,128)(2,1)S(1)} %copy-done.2, bf16[512,512]{1,0:T(8,128)(2,1)S(1)} %copy-done.3, f32[512,512]{1,0:T(8,128)S(1)} %shard_map.158.h_ref, ...), custom_call_target="tpu_custom_call" | custom-call | tf_op jit(solution)/shard_map/pallas_call | solution.py:316
  50.9 2.1 %collective-permute-start.3 = (bf16[2,32,512]{2,1,0:T(8,128)(2,1)S(1)}, bf16[2,32,512]{2,1,0:T(8,128)(2,1)S(1)}, u32[]{:S(2)}, u32[]{:S(2)}) collective-permute-start(bf16[2,32,512]{2,1,0:T(8,128)(2,1)S(1)} %slice.9), channel_id=1, source_target_pairs={{0,63},{1,62},{2,61},{3,60},{4,59},{5,58},{6,57},{7,56},{8,55},{9,... | collective-permute-start | bytes 196616 | tf_op jit(solution)/shard_map/ppermute | solution.py:327
  53.0 2.0 %collective-permute-start.4 = (bf16[2,8,512]{2,1,0:T(8,128)(2,1)S(1)}, bf16[2,8,512]{2,1,0:T(8,128)(2,1)S(1)}, u32[]{:S(2)}, u32[]{:S(2)}) collective-permute-start(bf16[2,8,512]{2,1,0:T(8,128)(2,1)S(1)} %slice_select_fusion), channel_id=1, source_target_pairs={{31,0},{0,1},{1,2},{2,3},{3,4},{4,5},{5,6},{6,7},{7,8},{8,9},{9,10... | collective-permute-start | bytes 49160 | tf_op jit(solution)/shard_map/ppermute | solution.py:329
  55.0 0.9 collective-permute-done.4.head_ref
  55.9 3.8 %collective-permute-done.3.far_ref = bf16[2,32,512]{2,1,0:T(8,128)(2,1)S(1)} collective-permute-done((bf16[2,32,512]{2,1,0:T(8,128)(2,1)S(1)}, bf16[2,32,512]{2,1,0:T(8,128)(2,1)S(1)}, u32[]{:S(2)}, u32[]{:S(2)}) %collective-permute-start.3) | collective-permute-done | bytes 65568 | tf_op jit(solution)/shard_map/ppermute | solution.py:327
  59.6 0.6 shard_map.161
  60.3 3.2 %collective-permute-start.5 = (bf16[2,64,512]{2,1,0:T(8,128)(2,1)S(1)}, bf16[2,64,512]{2,1,0:T(8,128)(2,1)S(1)}, u32[]{:S(2)}, u32[]{:S(2)}) collective-permute-start(bf16[2,64,512]{2,1,0:T(8,128)(2,1)S(1)} %shard_map.161), channel_id=1, source_target_pairs={{0,128},{64,192},{128,0},{192,64},{256,384},{320,448},{384,256},{4... | collective-permute-start | bytes 393224 | tf_op jit(solution)/shard_map/ppermute | solution.py:341
  63.5 15.1 %all-to-all-start.1 = ((bf16[64,8,256]{2,1,0:T(8,128)(2,1)}), bf16[64,8,256]{2,1,0:T(8,128)(2,1)S(1)}, u32[]{:S(2)}, u32[]{:S(2)}) async-start(bf16[64,8,256]{2,1,0:T(8,128)(2,1)} %bitcast.7), calls=%async_computation.1 | async-start | bytes 524288 | tf_op jit(solution)/shard_map/all_to_all | solution.py:330
  78.6 0.0 copy-start.1
  78.7 4.7 %collective-permute-start.6 = (bf16[2,64,512]{2,1,0:T(8,128)(2,1)S(1)}, bf16[2,64,512]{2,1,0:T(8,128)(2,1)S(1)}, u32[]{:S(2)}, u32[]{:S(2)}) collective-permute-start(bf16[2,64,512]{2,1,0:T(8,128)(2,1)S(1)} %add_convert_fusion.2), channel_id=1, source_target_pairs={{0,256},{64,320},{128,384},{192,448},{256,0},{320,64},{384,128},{4... | collective-permute-start | bytes 393224 | tf_op jit(solution)/shard_map/ppermute | solution.py:341
  83.3 3.5 %collective-permute-done.6 = bf16[2,64,512]{2,1,0:T(8,128)(2,1)S(1)} collective-permute-done((bf16[2,64,512]{2,1,0:T(8,128)(2,1)S(1)}, bf16[2,64,512]{2,1,0:T(8,128)(2,1)S(1)}, u32[]{:S(2)}, u32[]{:S(2)}) %collective-permute-start.6) | collective-permute-done | bytes 131104 | tf_op jit(solution)/shard_map/ppermute | solution.py:341
  86.8 3.7 %collective-permute-start.7 = (bf16[2,64,512]{2,1,0:T(8,128)(2,1)S(1)}, bf16[2,64,512]{2,1,0:T(8,128)(2,1)S(1)}, u32[]{:S(2)}, u32[]{:S(2)}) collective-permute-start(bf16[2,64,512]{2,1,0:T(8,128)(2,1)S(1)} %add_convert_fusion.1), channel_id=1, source_target_pairs={{0,64},{64,0},{128,192},{192,128},{256,320},{320,256},{384,448},{4... | collective-permute-start | bytes 393224 | tf_op jit(solution)/shard_map/ppermute | solution.py:341
  90.5 4.1 %collective-permute-done.7 = bf16[2,64,512]{2,1,0:T(8,128)(2,1)S(1)} collective-permute-done((bf16[2,64,512]{2,1,0:T(8,128)(2,1)S(1)}, bf16[2,64,512]{2,1,0:T(8,128)(2,1)S(1)}, u32[]{:S(2)}, u32[]{:S(2)}) %collective-permute-start.7) | collective-permute-done | bytes 131104 | tf_op jit(solution)/shard_map/ppermute | solution.py:341
  94.6 0.7 fusion
  95.3 5.5 %all-to-all-done.1 = bf16[64,8,256]{2,1,0:T(8,128)(2,1)S(1)} async-done(((bf16[64,8,256]{2,1,0:T(8,128)(2,1)}), bf16[64,8,256]{2,1,0:T(8,128)(2,1)S(1)}, u32[]{:S(2)}, u32[]{:S(2)}) %all-to-all-start.1) | async-done | bytes 262176 | tf_op jit(solution)/shard_map/all_to_all | solution.py:330
  100.8 1.3 %shard_map.160 = (bf16[128,512]{1,0:T(8,128)(2,1)}, bf16[128,512]{1,0:T(8,128)(2,1)}) custom-call(s32[1]{0:T(128)} %bitcast.idx_ref, bf16[512,256]{1,0:T(8,128)(2,1)S(1)} %bitcast.16, bf16[512,512]{1,0:T(8,128)(2,1)S(1)} %copy-done.1), custom_call_target="tpu_custom_call" | custom-call | flops 400000000 | bytes 2000000 | tf_op jit(solution)/shard_map/pallas_call | solution.py:343
  (22 shorter events, 0.1 us)
Async XLA Ops:
  0.6 47.0 %copy-start = (bf16[512,512]{1,0:T(8,128)(2,1)S(1)}, bf16[512,512]{1,0:T(8,128)(2,1)}, u32[]{:S(2)}) copy-start(bf16[512,512]{1,0:T(8,128)(2,1)} %constant.36.clone.flip_ref) | copy-start | bytes 1572868
  3.2 18.3 %copy-start.10 = (bf16[2,16,512]{2,1,0:T(8,128)(2,1)S(1)}, bf16[2,16,512]{2,1,0:T(8,128)(2,1)}, u32[]{:S(2)}) copy-start(bf16[2,16,512]{2,1,0:T(8,128)(2,1)} %get-tuple-element.11) | copy-start | bytes 98308
  3.2 41.2 %copy-start.11 = (bf16[2,8,512]{2,1,0:T(8,128)(2,1)S(1)}, bf16[2,8,512]{2,1,0:T(8,128)(2,1)}, u32[]{:S(2)}) copy-start(bf16[2,8,512]{2,1,0:T(8,128)(2,1)} %get-tuple-element.12) | copy-start | bytes 49156
  3.2 44.4 %copy-start.4 = (bf16[2,8,8,512]{3,2,1,0:T(8,128)(2,1)S(1)}, bf16[2,8,8,512]{3,2,1,0:T(8,128)(2,1)}, u32[]{:S(2)}) copy-start(bf16[2,8,8,512]{3,2,1,0:T(8,128)(2,1)} %param.16) | copy-start | bytes 393220
  3.2 44.4 %copy-start.5 = (bf16[3,112,256]{2,1,0:T(8,128)(2,1)S(1)}, bf16[3,112,256]{2,1,0:T(8,128)(2,1)}, u32[]{:S(2)}) copy-start(bf16[3,112,256]{2,1,0:T(8,128)(2,1)} %constant.39.clone.own_ref) | copy-start | bytes 516100
  3.3 44.4 %copy-start.6 = (bf16[3,112,256]{2,1,0:T(8,128)(2,1)S(1)}, bf16[3,112,256]{2,1,0:T(8,128)(2,1)}, u32[]{:S(2)}) copy-start(bf16[3,112,256]{2,1,0:T(8,128)(2,1)} %constant.40.clone.mirror_ref) | copy-start | bytes 516100
  3.3 45.5 %all-to-all-start = ((bf16[64,8,256]{2,1,0:T(8,128)(2,1)}), bf16[64,8,256]{2,1,0:T(8,128)(2,1)S(1)}, u32[]{:S(2)}, u32[]{:S(2)}) async-start(bf16[64,8,256]{2,1,0:T(8,128)(2,1)} %bitcast.17), calls=%async_computation | async-start | bytes 524288 | tf_op jit(solution)/shard_map/all_to_all | solution.py:303
  21.5 18.6 %collective-permute-start = (bf16[2,16,512]{2,1,0:T(8,128)(2,1)S(1)}, bf16[2,16,512]{2,1,0:T(8,128)(2,1)S(1)}, u32[]{:S(2)}, u32[]{:S(2)}) collective-permute-start(bf16[2,16,512]{2,1,0:T(8,128)(2,1)S(1)} %copy-done.10), channel_id=1, source_target_pairs={{0,63},{1,62},{2,61},{3,60},{4,59},{5,58},{6,57},{7,56},{8,55},{9,... | collective-permute-start | bytes 98312 | tf_op jit(solution)/shard_map/ppermute | solution.py:304
  40.1 7.5 %collective-permute-start.1 = (bf16[2,16,512]{2,1,0:T(8,128)(2,1)S(1)}, bf16[2,16,512]{2,1,0:T(8,128)(2,1)S(1)}, u32[]{:S(2)}, u32[]{:S(2)}) collective-permute-start(bf16[2,16,512]{2,1,0:T(8,128)(2,1)S(1)} %collective-permute-done.tail_ref), channel_id=1, source_target_pairs={{0,64},{64,0},{128,192},{192,128},{256,320},{320,256},{384,448},{4... | collective-permute-start | bytes 98312 | tf_op jit(solution)/shard_map/ppermute | solution.py:306
  44.5 3.2 %collective-permute-start.2 = (bf16[2,8,512]{2,1,0:T(8,128)(2,1)S(1)}, bf16[2,8,512]{2,1,0:T(8,128)(2,1)S(1)}, u32[]{:S(2)}, u32[]{:S(2)}) collective-permute-start(bf16[2,8,512]{2,1,0:T(8,128)(2,1)S(1)} %copy-done.11), channel_id=1, source_target_pairs={{0,31},{1,0},{2,1},{3,2},{4,3},{5,4},{6,5},{7,6},{8,7},{9,8},{10,9... | collective-permute-start | bytes 49160 | tf_op jit(solution)/shard_map/ppermute | solution.py:305
  44.5 4.3 %copy-start.2 = (bf16[512,512]{1,0:T(8,128)(2,1)S(1)}, bf16[512,512]{1,0:T(8,128)(2,1)}, u32[]{:S(2)}) copy-start(bf16[512,512]{1,0:T(8,128)(2,1)} %constant.34.clone.wc_ref) | copy-start | bytes 1572868
  44.5 4.3 %copy-start.3 = (bf16[512,512]{1,0:T(8,128)(2,1)S(1)}, bf16[512,512]{1,0:T(8,128)(2,1)}, u32[]{:S(2)}) copy-start(bf16[512,512]{1,0:T(8,128)(2,1)} %constant.35.clone.ws_ref) | copy-start | bytes 1572868
  44.6 4.3 %copy-start.7 = (bf16[2,2,48,256]{3,2,1,0:T(8,128)(2,1)S(1)}, bf16[2,2,48,256]{3,2,1,0:T(8,128)(2,1)}, u32[]{:S(2)}) copy-start(bf16[2,2,48,256]{3,2,1,0:T(8,128)(2,1)} %constant.43.clone.gather_ref) | copy-start | bytes 294916
  50.9 8.7 %copy-start.8 = (bf16[4,64,112]{2,1,0:T(8,128)(2,1)S(1)}, bf16[4,64,112]{2,1,0:T(8,128)(2,1)}, u32[]{:S(2)}) copy-start(bf16[4,64,112]{2,1,0:T(8,128)(2,1)} %constant.41.clone.own_ref) | copy-start | bytes 172036
  50.9 8.7 %copy-start.9 = (bf16[4,64,112]{2,1,0:T(8,128)(2,1)S(1)}, bf16[4,64,112]{2,1,0:T(8,128)(2,1)}, u32[]{:S(2)}) copy-start(bf16[4,64,112]{2,1,0:T(8,128)(2,1)} %constant.42.clone.mirror_ref) | copy-start | bytes 172036
  50.9 8.7 %collective-permute-start.3 = (bf16[2,32,512]{2,1,0:T(8,128)(2,1)S(1)}, bf16[2,32,512]{2,1,0:T(8,128)(2,1)S(1)}, u32[]{:S(2)}, u32[]{:S(2)}) collective-permute-start(bf16[2,32,512]{2,1,0:T(8,128)(2,1)S(1)} %slice.9), channel_id=1, source_target_pairs={{0,63},{1,62},{2,61},{3,60},{4,59},{5,58},{6,57},{7,56},{8,55},{9,... | collective-permute-start | bytes 196616 | tf_op jit(solution)/shard_map/ppermute | solution.py:327
  53.0 2.9 %collective-permute-start.4 = (bf16[2,8,512]{2,1,0:T(8,128)(2,1)S(1)}, bf16[2,8,512]{2,1,0:T(8,128)(2,1)S(1)}, u32[]{:S(2)}, u32[]{:S(2)}) collective-permute-start(bf16[2,8,512]{2,1,0:T(8,128)(2,1)S(1)} %slice_select_fusion), channel_id=1, source_target_pairs={{31,0},{0,1},{1,2},{2,3},{3,4},{4,5},{5,6},{6,7},{7,8},{8,9},{9,10... | collective-permute-start | bytes 49160 | tf_op jit(solution)/shard_map/ppermute | solution.py:329
  60.3 18.3 %collective-permute-start.5 = (bf16[2,64,512]{2,1,0:T(8,128)(2,1)S(1)}, bf16[2,64,512]{2,1,0:T(8,128)(2,1)S(1)}, u32[]{:S(2)}, u32[]{:S(2)}) collective-permute-start(bf16[2,64,512]{2,1,0:T(8,128)(2,1)S(1)} %shard_map.161), channel_id=1, source_target_pairs={{0,128},{64,192},{128,0},{192,64},{256,384},{320,448},{384,256},{4... | collective-permute-start | bytes 393224 | tf_op jit(solution)/shard_map/ppermute | solution.py:341
  63.5 37.3 %all-to-all-start.1 = ((bf16[64,8,256]{2,1,0:T(8,128)(2,1)}), bf16[64,8,256]{2,1,0:T(8,128)(2,1)S(1)}, u32[]{:S(2)}, u32[]{:S(2)}) async-start(bf16[64,8,256]{2,1,0:T(8,128)(2,1)} %bitcast.7), calls=%async_computation.1 | async-start | bytes 524288 | tf_op jit(solution)/shard_map/all_to_all | solution.py:330
  78.6 22.2 %copy-start.1 = (bf16[512,512]{1,0:T(8,128)(2,1)S(1)}, bf16[512,512]{1,0:T(8,128)(2,1)}, u32[]{:S(2)}) copy-start(bf16[512,512]{1,0:T(8,128)(2,1)} %constant.33.clone.t_ref) | copy-start | bytes 1572868
  78.7 8.1 %collective-permute-start.6 = (bf16[2,64,512]{2,1,0:T(8,128)(2,1)S(1)}, bf16[2,64,512]{2,1,0:T(8,128)(2,1)S(1)}, u32[]{:S(2)}, u32[]{:S(2)}) collective-permute-start(bf16[2,64,512]{2,1,0:T(8,128)(2,1)S(1)} %add_convert_fusion.2), channel_id=1, source_target_pairs={{0,256},{64,320},{128,384},{192,448},{256,0},{320,64},{384,128},{4... | collective-permute-start | bytes 393224 | tf_op jit(solution)/shard_map/ppermute | solution.py:341
  86.8 7.8 %collective-permute-start.7 = (bf16[2,64,512]{2,1,0:T(8,128)(2,1)S(1)}, bf16[2,64,512]{2,1,0:T(8,128)(2,1)S(1)}, u32[]{:S(2)}, u32[]{:S(2)}) collective-permute-start(bf16[2,64,512]{2,1,0:T(8,128)(2,1)S(1)} %add_convert_fusion.1), channel_id=1, source_target_pairs={{0,64},{64,0},{128,192},{192,128},{256,320},{320,256},{384,448},{4... | collective-permute-start | bytes 393224 | tf_op jit(solution)/shard_map/ppermute | solution.py:341

commit v9 on v7

--- a/solution.py
+++ b/solution.py
@@ -16,6 +16,7 @@
 F32 = jnp.float32
 VMEM = pl.BlockSpec(memory_space=pltpu.VMEM)
 SMEM = pl.BlockSpec(memory_space=pltpu.SMEM)
+HBM = pl.BlockSpec(memory_space=pltpu.HBM)
 PARAMS = pltpu.CompilerParams(vmem_limit_bytes=20 * 2**20)
 
 LAST = 31
@@ -140,14 +141,27 @@
     return (re[0], jnp.where(first, im[0], re[1])), (jnp.where(first, re[1], im[0]), im[1])
 
 
-def kernel_a(idx_ref, sig_ref, cot_ref, t_ref, f_ref, tail_ref, head_ref, out_ref, tails_ref,
-             heads_ref, yre, yim, z):
+def kernel_a(idx_ref, sig_hbm, cot_hbm, t_hbm, f_hbm, tail_hbm, head_hbm, out_ref, tails_ref,
+             heads_ref, x_ref, t_ref, f_ref, tail_ref, head_ref, yre, yim, z, sems):
+    moves = (
+        (sig_hbm, x_ref.at[pl.ds(0, 128)]),
+        (cot_hbm, x_ref.at[pl.ds(128, 128)]),
+        (t_hbm, t_ref),
+        (f_hbm, f_ref),
+        (tail_hbm, tail_ref),
+        (head_hbm, head_ref),
+    )
+    copies = [pltpu.make_async_copy(a, b, sems.at[k]) for k, (a, b) in enumerate(moves)]
+    for copy in copies:
+        copy.start()
+    turns = [turn(idx_ref, chan) for chan in range(2)]
+    for copy in copies:
+        copy.wait()
     upper = idx_ref[0] >> 5
     for ri in range(2):
         tails_ref[ri] = dot(tail_ref[upper], f_ref[ri]).astype(BF)
         heads_ref[ri] = dot(head_ref[...], f_ref[ri]).astype(BF)
-    turns = [turn(idx_ref, chan) for chan in range(2)]
-    both = dot(jnp.concatenate([sig_ref[...], cot_ref[...]], axis=0), t_ref[...])
+    both = dot(x_ref[...], t_ref[...])
     for half in range(2):
         part = both[half * 128 : (half + 1) * 128]
         re = part[:, :HALF].reshape(8, 2, ROWS, HALF)
@@ -284,7 +298,7 @@
     filt = filter_spec.reshape(2, 64, N)
     sent, tails, heads = pl.pallas_call(
         kernel_a,
-        in_specs=[SMEM] + [VMEM] * 6,
+        in_specs=[SMEM] + [HBM] * 6,
         out_specs=[VMEM] * 3,
         out_shape=[
             jax.ShapeDtypeStruct((N, HALF), BF),
@@ -292,9 +306,15 @@
             jax.ShapeDtypeStruct((2, 8, N), BF),
         ],
         scratch_shapes=[
+            pltpu.VMEM((256, N), BF),
+            pltpu.VMEM((N, N), BF),
+            pltpu.VMEM((2, 64, N), BF),
+            pltpu.VMEM((2, 32, 64), BF),
+            pltpu.VMEM((8, 64), BF),
             pltpu.VMEM((2, 256, 128), F32),
             pltpu.VMEM((2, 256, 128), F32),
             pltpu.VMEM((2, N, 128), F32),
+            pltpu.SemaphoreType.DMA((6,)),
         ],
     )(place, signal.reshape(128, N), cotangent.reshape(128, N), table, filt, tail, head)
     got = lax.all_to_all(sent.reshape(SEQ, ROWS, HALF), "seq", 0, 0, tiled=True)

time: 97.4 us -> 97.5 us (level)
  no operation moved by 1% of the time
where the time goes in v9:
time: 97.5 us; the launch traced here: 97 us
  starting transfers between devices  55.2 us (57%)
  waiting for transfers between devices  32.4 us (33%)
  Pallas kernels  7.74 us (8%)
    all_to_all x1, starting transfers between devices, body(): got = lax.all_to_all(sent.reshape(SEQ, ROWS, HALF), 'seq', 0, 0, tiled=True)  18.2 us
    all_to_all x1, starting transfers between devices, body(): mid = lax.all_to_all(back.reshape(SEQ, ROWS, HALF), 'seq', 0, 0, tiled=True)  14.8 us
    ppermute x3, starting transfers between devices, body(): other = lax.ppermute(grad, 'dp', [(d, d ^ bit) for d in range(8)])  12.2 us
    ppermute x1, waiting for transfers between devices, body(): heads = lax.ppermute(heads, 'seq', down)  12 us
    ppermute x3, waiting for transfers between devices, body(): other = lax.ppermute(grad, 'dp', [(d, d ^ bit) for d in range(8)])  6.8 us
    ppermute x1, starting transfers between devices, body(): tails = lax.ppermute(tails, 'seq', opposite)  5.95 us
    all_to_all x1, waiting for transfers between devices, body(): mid = lax.all_to_all(back.reshape(SEQ, ROWS, HALF), 'seq', 0, 0, tiled=True)  5.61 us
    ppermute x1, waiting for transfers between devices, body(): far = lax.ppermute(grad[:, :32], 'seq', opposite)  3.79 us
  transfers between devices with their start and end apart: 9, of which 7 were waited for; matrix products, arithmetic and copies ran while one was open for 1% of the time, Pallas kernels for 1%

profile of v9, /device:TPU:1, one launch (start us, length us, event | category | flops | bytes accessed | tf_op | source)
XLA Modules:
  0.0 97.0 jit_solution(467091468836569244)
XLA Ops:
  0.6 0.0 copy-start
  0.6 2.6 %shard_map.157 = (bf16[512,256]{1,0:T(8,128)(2,1)}, bf16[2,32,512]{2,1,0:T(8,128)(2,1)}, bf16[2,8,512]{2,1,0:T(8,128)(2,1)}) custom-call(s32[1]{0:T(128)} %bitcast.idx_ref, bf16[128,512]{1,0:T(8,128)(2,1)} %bitcast.17, bf16[128,512]{1,0:T(8,128)(2,1)} %bitcast.18, bf16[512,512]{1,0:T(8,128)(2,1)} %constant.28.clone.t_hbm.t_ref, ...), custom_call_target="tpu_custom_call" | custom-call | tf_op jit(solution)/shard_map/pallas_call | solution.py:299
  3.3 0.0 copy-start.10
  3.3 0.0 copy-start.1
  3.3 0.0 copy-start.5
  3.3 0.0 copy-start.6
  3.3 18.2 %all-to-all-start = ((bf16[64,8,256]{2,1,0:T(8,128)(2,1)}), bf16[64,8,256]{2,1,0:T(8,128)(2,1)S(1)}, u32[]{:S(2)}, u32[]{:S(2)}) async-start(bf16[64,8,256]{2,1,0:T(8,128)(2,1)} %bitcast.16), calls=%async_computation | async-start | bytes 524288 | tf_op jit(solution)/shard_map/all_to_all | solution.py:320
  21.5 6.0 %collective-permute-start = (bf16[2,32,512]{2,1,0:T(8,128)(2,1)}, bf16[2,32,512]{2,1,0:T(8,128)(2,1)S(1)}, u32[]{:S(2)}, u32[]{:S(2)}) collective-permute-start(bf16[2,32,512]{2,1,0:T(8,128)(2,1)} %get-tuple-element.11), channel_id=1, source_target_pairs={{0,63},{1,62},{2,61},{3,60},{4,59},{5,58},{6,57},{7,56},{8,55},{9,... | collective-permute-start | bytes 196616 | tf_op jit(solution)/shard_map/ppermute | solution.py:321
  27.5 0.1 collective-permute-start.1
  27.6 12.0 %collective-permute-done.1.head_ref = bf16[2,8,512]{2,1,0:T(8,128)(2,1)S(1)} collective-permute-done((bf16[2,8,512]{2,1,0:T(8,128)(2,1)S(1)}, bf16[2,8,512]{2,1,0:T(8,128)(2,1)S(1)}, u32[]{:S(2)}, u32[]{:S(2)}) %collective-permute-start.1) | collective-permute-done | bytes 16416 | tf_op jit(solution)/shard_map/ppermute | solution.py:322
  39.6 3.4 %collective-permute-done.tail_ref = bf16[2,32,512]{2,1,0:T(8,128)(2,1)S(1)} collective-permute-done((bf16[2,32,512]{2,1,0:T(8,128)(2,1)}, bf16[2,32,512]{2,1,0:T(8,128)(2,1)S(1)}, u32[]{:S(2)}, u32[]{:S(2)}) %collective-permute-start) | collective-permute-done | bytes 65568 | tf_op jit(solution)/shard_map/ppermute | solution.py:321
  43.0 0.0 copy-done.1
  43.0 1.1 %shard_map.158.h_ref = f32[512,512]{1,0:T(8,128)S(1)} custom-call(s32[1]{0:T(128)} %bitcast.idx_ref, bf16[2,64,512]{2,1,0:T(8,128)(2,1)S(1)} %bitcast.14, bf16[2,32,512]{2,1,0:T(8,128)(2,1)S(1)} %collective-permute-done.tail_ref, bf16[2,8,512]{2,1,0:T(8,128)(2,1)S(1)} %collective-permute-done.1.head_ref, bf16[3,112,256]{2,1,0:T(8,128)(2,1)S(1)} %copy-done.5, ...), custom_call_target="tpu_custom_call" | custom-call | flops 400000000 | bytes 2000000 | tf_op jit(solution)/shard_map/pallas_call | solution.py:323
  44.2 0.0 all-to-all-done
  44.2 2.1 %shard_map.159 = (bf16[512,256]{1,0:T(8,128)(2,1)}, bf16[2,48,512]{2,1,0:T(8,128)(2,1)S(1)}) custom-call(s32[1]{0:T(128)} %bitcast.idx_ref, bf16[512,256]{1,0:T(8,128)(2,1)S(1)} %bitcast.12, bf16[512,512]{1,0:T(8,128)(2,1)S(1)} %copy-done.3, bf16[512,512]{1,0:T(8,128)(2,1)S(1)} %copy-done.4, f32[512,512]{1,0:T(8,128)S(1)} %shard_map.158.h_ref, ...), custom_call_target="tpu_custom_call" | custom-call | tf_op jit(solution)/shard_map/pallas_call | solution.py:332
  46.3 2.1 %collective-permute-start.2 = (bf16[2,32,512]{2,1,0:T(8,128)(2,1)S(1)}, bf16[2,32,512]{2,1,0:T(8,128)(2,1)S(1)}, u32[]{:S(2)}, u32[]{:S(2)}) collective-permute-start(bf16[2,32,512]{2,1,0:T(8,128)(2,1)S(1)} %slice.9), channel_id=1, source_target_pairs={{0,63},{1,62},{2,61},{3,60},{4,59},{5,58},{6,57},{7,56},{8,55},{9,... | collective-permute-start | bytes 196616 | tf_op jit(solution)/shard_map/ppermute | solution.py:343
  48.4 1.8 %collective-permute-start.3 = (bf16[2,8,512]{2,1,0:T(8,128)(2,1)S(1)}, bf16[2,8,512]{2,1,0:T(8,128)(2,1)S(1)}, u32[]{:S(2)}, u32[]{:S(2)}) collective-permute-start(bf16[2,8,512]{2,1,0:T(8,128)(2,1)S(1)} %slice_select_fusion), channel_id=1, source_target_pairs={{31,0},{0,1},{1,2},{2,3},{3,4},{4,5},{5,6},{6,7},{7,8},{8,9},{9,10... | collective-permute-start | bytes 49160 | tf_op jit(solution)/shard_map/ppermute | solution.py:345
  50.2 0.9 collective-permute-done.3.head_ref
  51.0 3.8 %collective-permute-done.2.far_ref = bf16[2,32,512]{2,1,0:T(8,128)(2,1)S(1)} collective-permute-done((bf16[2,32,512]{2,1,0:T(8,128)(2,1)S(1)}, bf16[2,32,512]{2,1,0:T(8,128)(2,1)S(1)}, u32[]{:S(2)}, u32[]{:S(2)}) %collective-permute-start.2) | collective-permute-done | bytes 65568 | tf_op jit(solution)/shard_map/ppermute | solution.py:343
  54.8 0.0 copy-done.9
  54.8 0.6 shard_map.161
  55.5 3.2 %collective-permute-start.4 = (bf16[2,64,512]{2,1,0:T(8,128)(2,1)S(1)}, bf16[2,64,512]{2,1,0:T(8,128)(2,1)S(1)}, u32[]{:S(2)}, u32[]{:S(2)}) collective-permute-start(bf16[2,64,512]{2,1,0:T(8,128)(2,1)S(1)} %shard_map.161), channel_id=1, source_target_pairs={{0,128},{64,192},{128,0},{192,64},{256,384},{320,448},{384,256},{4... | collective-permute-start | bytes 393224 | tf_op jit(solution)/shard_map/ppermute | solution.py:357
  58.7 14.8 %all-to-all-start.1 = ((bf16[64,8,256]{2,1,0:T(8,128)(2,1)}), bf16[64,8,256]{2,1,0:T(8,128)(2,1)S(1)}, u32[]{:S(2)}, u32[]{:S(2)}) async-start(bf16[64,8,256]{2,1,0:T(8,128)(2,1)} %bitcast.6), calls=%async_computation.1 | async-start | bytes 524288 | tf_op jit(solution)/shard_map/all_to_all | solution.py:346
  73.5 0.0 copy-start.2
  73.5 0.0 collective-permute-done.4
  73.5 4.7 %collective-permute-start.5 = (bf16[2,64,512]{2,1,0:T(8,128)(2,1)S(1)}, bf16[2,64,512]{2,1,0:T(8,128)(2,1)S(1)}, u32[]{:S(2)}, u32[]{:S(2)}) collective-permute-start(bf16[2,64,512]{2,1,0:T(8,128)(2,1)S(1)} %add_convert_fusion.2), channel_id=1, source_target_pairs={{0,256},{64,320},{128,384},{192,448},{256,0},{320,64},{384,128},{4... | collective-permute-start | bytes 393224 | tf_op jit(solution)/shard_map/ppermute | solution.py:357
  78.2 3.5 %collective-permute-done.5 = bf16[2,64,512]{2,1,0:T(8,128)(2,1)S(1)} collective-permute-done((bf16[2,64,512]{2,1,0:T(8,128)(2,1)S(1)}, bf16[2,64,512]{2,1,0:T(8,128)(2,1)S(1)}, u32[]{:S(2)}, u32[]{:S(2)}) %collective-permute-start.5) | collective-permute-done | bytes 131104 | tf_op jit(solution)/shard_map/ppermute | solution.py:357
  81.7 4.4 %collective-permute-start.6 = (bf16[2,64,512]{2,1,0:T(8,128)(2,1)S(1)}, bf16[2,64,512]{2,1,0:T(8,128)(2,1)S(1)}, u32[]{:S(2)}, u32[]{:S(2)}) collective-permute-start(bf16[2,64,512]{2,1,0:T(8,128)(2,1)S(1)} %add_convert_fusion.1), channel_id=1, source_target_pairs={{0,64},{64,0},{128,192},{192,128},{256,320},{320,256},{384,448},{4... | collective-permute-start | bytes 393224 | tf_op jit(solution)/shard_map/ppermute | solution.py:357
  86.1 3.3 %collective-permute-done.6 = bf16[2,64,512]{2,1,0:T(8,128)(2,1)S(1)} collective-permute-done((bf16[2,64,512]{2,1,0:T(8,128)(2,1)S(1)}, bf16[2,64,512]{2,1,0:T(8,128)(2,1)S(1)}, u32[]{:S(2)}, u32[]{:S(2)}) %collective-permute-start.6) | collective-permute-done | bytes 131104 | tf_op jit(solution)/shard_map/ppermute | solution.py:357
  89.4 0.7 fusion
  90.1 5.6 %all-to-all-done.1 = bf16[64,8,256]{2,1,0:T(8,128)(2,1)S(1)} async-done(((bf16[64,8,256]{2,1,0:T(8,128)(2,1)}), bf16[64,8,256]{2,1,0:T(8,128)(2,1)S(1)}, u32[]{:S(2)}, u32[]{:S(2)}) %all-to-all-start.1) | async-done | bytes 262176 | tf_op jit(solution)/shard_map/all_to_all | solution.py:346
  95.7 1.3 %shard_map.160 = (bf16[128,512]{1,0:T(8,128)(2,1)}, bf16[128,512]{1,0:T(8,128)(2,1)}) custom-call(s32[1]{0:T(128)} %bitcast.idx_ref, bf16[512,256]{1,0:T(8,128)(2,1)S(1)} %bitcast.15, bf16[512,512]{1,0:T(8,128)(2,1)S(1)} %copy-done.2), custom_call_target="tpu_custom_call" | custom-call | flops 400000000 | bytes 2000000 | tf_op jit(solution)/shard_map/pallas_call | solution.py:359
  (18 shorter events, 0.1 us)
Async XLA Ops:
  0.6 42.4 %copy-start = (bf16[512,512]{1,0:T(8,128)(2,1)S(1)}, bf16[512,512]{1,0:T(8,128)(2,1)}, u32[]{:S(2)}) copy-start(bf16[512,512]{1,0:T(8,128)(2,1)} %constant.31.clone.flip_ref) | copy-start | bytes 1572868
  3.3 24.2 %copy-start.10 = (bf16[2,8,512]{2,1,0:T(8,128)(2,1)S(1)}, bf16[2,8,512]{2,1,0:T(8,128)(2,1)}, u32[]{:S(2)}) copy-start(bf16[2,8,512]{2,1,0:T(8,128)(2,1)} %get-tuple-element.12) | copy-start | bytes 49156
  3.3 39.7 %copy-start.1 = (bf16[2,8,8,512]{3,2,1,0:T(8,128)(2,1)S(1)}, bf16[2,8,8,512]{3,2,1,0:T(8,128)(2,1)}, u32[]{:S(2)}) copy-start(bf16[2,8,8,512]{3,2,1,0:T(8,128)(2,1)} %param.16) | copy-start | bytes 393220
  3.3 39.7 %copy-start.5 = (bf16[3,112,256]{2,1,0:T(8,128)(2,1)S(1)}, bf16[3,112,256]{2,1,0:T(8,128)(2,1)}, u32[]{:S(2)}) copy-start(bf16[3,112,256]{2,1,0:T(8,128)(2,1)} %constant.34.clone.own_ref) | copy-start | bytes 516100
  3.3 39.7 %copy-start.6 = (bf16[3,112,256]{2,1,0:T(8,128)(2,1)S(1)}, bf16[3,112,256]{2,1,0:T(8,128)(2,1)}, u32[]{:S(2)}) copy-start(bf16[3,112,256]{2,1,0:T(8,128)(2,1)} %constant.35.clone.mirror_ref) | copy-start | bytes 516100
  3.3 40.8 %all-to-all-start = ((bf16[64,8,256]{2,1,0:T(8,128)(2,1)}), bf16[64,8,256]{2,1,0:T(8,128)(2,1)S(1)}, u32[]{:S(2)}, u32[]{:S(2)}) async-start(bf16[64,8,256]{2,1,0:T(8,128)(2,1)} %bitcast.16), calls=%async_computation | async-start | bytes 524288 | tf_op jit(solution)/shard_map/all_to_all | solution.py:320
  21.5 21.5 %collective-permute-start = (bf16[2,32,512]{2,1,0:T(8,128)(2,1)}, bf16[2,32,512]{2,1,0:T(8,128)(2,1)S(1)}, u32[]{:S(2)}, u32[]{:S(2)}) collective-permute-start(bf16[2,32,512]{2,1,0:T(8,128)(2,1)} %get-tuple-element.11), channel_id=1, source_target_pairs={{0,63},{1,62},{2,61},{3,60},{4,59},{5,58},{6,57},{7,56},{8,55},{9,... | collective-permute-start | bytes 196616 | tf_op jit(solution)/shard_map/ppermute | solution.py:321
  27.5 12.1 %collective-permute-start.1 = (bf16[2,8,512]{2,1,0:T(8,128)(2,1)S(1)}, bf16[2,8,512]{2,1,0:T(8,128)(2,1)S(1)}, u32[]{:S(2)}, u32[]{:S(2)}) collective-permute-start(bf16[2,8,512]{2,1,0:T(8,128)(2,1)S(1)} %copy-done.10), channel_id=1, source_target_pairs={{0,31},{1,0},{2,1},{3,2},{4,3},{5,4},{6,5},{7,6},{8,7},{9,8},{10,9... | collective-permute-start | bytes 49160 | tf_op jit(solution)/shard_map/ppermute | solution.py:322
  27.6 16.5 %copy-start.3 = (bf16[512,512]{1,0:T(8,128)(2,1)S(1)}, bf16[512,512]{1,0:T(8,128)(2,1)}, u32[]{:S(2)}) copy-start(bf16[512,512]{1,0:T(8,128)(2,1)} %constant.29.clone.wc_ref) | copy-start | bytes 1572868
  27.6 16.5 %copy-start.4 = (bf16[512,512]{1,0:T(8,128)(2,1)S(1)}, bf16[512,512]{1,0:T(8,128)(2,1)}, u32[]{:S(2)}) copy-start(bf16[512,512]{1,0:T(8,128)(2,1)} %constant.30.clone.ws_ref) | copy-start | bytes 1572868
  27.6 16.5 %copy-start.7 = (bf16[2,2,48,256]{3,2,1,0:T(8,128)(2,1)S(1)}, bf16[2,2,48,256]{3,2,1,0:T(8,128)(2,1)}, u32[]{:S(2)}) copy-start(bf16[2,2,48,256]{3,2,1,0:T(8,128)(2,1)} %constant.38.clone.gather_ref) | copy-start | bytes 294916
  46.3 8.6 %copy-start.8 = (bf16[4,64,112]{2,1,0:T(8,128)(2,1)S(1)}, bf16[4,64,112]{2,1,0:T(8,128)(2,1)}, u32[]{:S(2)}) copy-start(bf16[4,64,112]{2,1,0:T(8,128)(2,1)} %constant.36.clone.own_ref) | copy-start | bytes 172036
  46.3 8.6 %copy-start.9 = (bf16[4,64,112]{2,1,0:T(8,128)(2,1)S(1)}, bf16[4,64,112]{2,1,0:T(8,128)(2,1)}, u32[]{:S(2)}) copy-start(bf16[4,64,112]{2,1,0:T(8,128)(2,1)} %constant.37.clone.mirror_ref) | copy-start | bytes 172036
  46.3 8.5 %collective-permute-start.2 = (bf16[2,32,512]{2,1,0:T(8,128)(2,1)S(1)}, bf16[2,32,512]{2,1,0:T(8,128)(2,1)S(1)}, u32[]{:S(2)}, u32[]{:S(2)}) collective-permute-start(bf16[2,32,512]{2,1,0:T(8,128)(2,1)S(1)} %slice.9), channel_id=1, source_target_pairs={{0,63},{1,62},{2,61},{3,60},{4,59},{5,58},{6,57},{7,56},{8,55},{9,... | collective-permute-start | bytes 196616 | tf_op jit(solution)/shard_map/ppermute | solution.py:343
  48.4 2.7 %collective-permute-start.3 = (bf16[2,8,512]{2,1,0:T(8,128)(2,1)S(1)}, bf16[2,8,512]{2,1,0:T(8,128)(2,1)S(1)}, u32[]{:S(2)}, u32[]{:S(2)}) collective-permute-start(bf16[2,8,512]{2,1,0:T(8,128)(2,1)S(1)} %slice_select_fusion), channel_id=1, source_target_pairs={{31,0},{0,1},{1,2},{2,3},{3,4},{4,5},{5,6},{6,7},{7,8},{8,9},{9,10... | collective-permute-start | bytes 49160 | tf_op jit(solution)/shard_map/ppermute | solution.py:345
  55.5 18.0 %collective-permute-start.4 = (bf16[2,64,512]{2,1,0:T(8,128)(2,1)S(1)}, bf16[2,64,512]{2,1,0:T(8,128)(2,1)S(1)}, u32[]{:S(2)}, u32[]{:S(2)}) collective-permute-start(bf16[2,64,512]{2,1,0:T(8,128)(2,1)S(1)} %shard_map.161), channel_id=1, source_target_pairs={{0,128},{64,192},{128,0},{192,64},{256,384},{320,448},{384,256},{4... | collective-permute-start | bytes 393224 | tf_op jit(solution)/shard_map/ppermute | solution.py:357
  58.7 37.0 %all-to-all-start.1 = ((bf16[64,8,256]{2,1,0:T(8,128)(2,1)}), bf16[64,8,256]{2,1,0:T(8,128)(2,1)S(1)}, u32[]{:S(2)}, u32[]{:S(2)}) async-start(bf16[64,8,256]{2,1,0:T(8,128)(2,1)} %bitcast.6), calls=%async_computation.1 | async-start | bytes 524288 | tf_op jit(solution)/shard_map/all_to_all | solution.py:346
  73.5 22.2 %copy-start.2 = (bf16[512,512]{1,0:T(8,128)(2,1)S(1)}, bf16[512,512]{1,0:T(8,128)(2,1)}, u32[]{:S(2)}) copy-start(bf16[512,512]{1,0:T(8,128)(2,1)} %constant.28.clone.t_hbm.t_ref) | copy-start | bytes 1572868
  73.5 8.1 %collective-permute-start.5 = (bf16[2,64,512]{2,1,0:T(8,128)(2,1)S(1)}, bf16[2,64,512]{2,1,0:T(8,128)(2,1)S(1)}, u32[]{:S(2)}, u32[]{:S(2)}) collective-permute-start(bf16[2,64,512]{2,1,0:T(8,128)(2,1)S(1)} %add_convert_fusion.2), channel_id=1, source_target_pairs={{0,256},{64,320},{128,384},{192,448},{256,0},{320,64},{384,128},{4... | collective-permute-start | bytes 393224 | tf_op jit(solution)/shard_map/ppermute | solution.py:357
  81.7 7.7 %collective-permute-start.6 = (bf16[2,64,512]{2,1,0:T(8,128)(2,1)S(1)}, bf16[2,64,512]{2,1,0:T(8,128)(2,1)S(1)}, u32[]{:S(2)}, u32[]{:S(2)}) collective-permute-start(bf16[2,64,512]{2,1,0:T(8,128)(2,1)S(1)} %add_convert_fusion.1), channel_id=1, source_target_pairs={{0,64},{64,0},{128,192},{192,128},{256,320},{320,256},{384,448},{4... | collective-permute-start | bytes 393224 | tf_op jit(solution)/shard_map/ppermute | solution.py:357

commit v10 on v7

--- a/solution.py
+++ b/solution.py
@@ -208,11 +208,7 @@
         pairs.append((pltpu.roll(x, 112, 1) * x, pltpu.roll(x, 48, 1) * x))
     for ri in range(2):
         terms = jnp.concatenate([pairs[0][ri], pairs[1][ri]], axis=1)
-        high = terms.astype(BF)
-        low = (terms - high.astype(F32)).astype(BF)
-        take = gather_ref[first, ri]
-        total = dot(take, high, ((1,), (1,))) + dot(take, low, ((1,), (1,)))
-        g_ref[ri] = total.astype(BF)
+        g_ref[ri] = dot(gather_ref[first, ri], terms.astype(BF), ((1,), (1,))).astype(BF)
     q1 = dot(wc_ref[...], prod[...])
     q2 = dot(ws_ref[...], prod[...])
     for p in range(2):

time: 97.4 us -> 97.4 us (level)
  no operation moved by 1% of the time
where the time goes in v10:
time: 97.4 us; the launch traced here: 97 us
  starting transfers between devices  55.2 us (57%)
  waiting for transfers between devices  32.4 us (33%)
  Pallas kernels  7.72 us (8%)
    all_to_all x1, starting transfers between devices, body(): got = lax.all_to_all(sent.reshape(SEQ, ROWS, HALF), 'seq', 0, 0, tiled=True)  18.2 us
    all_to_all x1, starting transfers between devices, body(): mid = lax.all_to_all(back.reshape(SEQ, ROWS, HALF), 'seq', 0, 0, tiled=True)  14.8 us
    ppermute x3, starting transfers between devices, body(): other = lax.ppermute(grad, 'dp', [(d, d ^ bit) for d in range(8)])  12.2 us
    ppermute x1, waiting for transfers between devices, body(): heads = lax.ppermute(heads, 'seq', down)  12 us
    ppermute x3, waiting for transfers between devices, body(): other = lax.ppermute(grad, 'dp', [(d, d ^ bit) for d in range(8)])  6.76 us
    ppermute x1, starting transfers between devices, body(): tails = lax.ppermute(tails, 'seq', opposite)  5.95 us
    all_to_all x1, waiting for transfers between devices, body(): mid = lax.all_to_all(back.reshape(SEQ, ROWS, HALF), 'seq', 0, 0, tiled=True)  5.63 us
    ppermute x1, waiting for transfers between devices, body(): far = lax.ppermute(grad[:, :32], 'seq', opposite)  3.78 us
  transfers between devices with their start and end apart: 9, of which 7 were waited for; matrix products, arithmetic and copies ran while one was open for 1% of the time, Pallas kernels for 1%

profile of v10, /device:TPU:1, one launch (start us, length us, event | category | flops | bytes accessed | tf_op | source)
XLA Modules:
  0.0 97.0 jit_solution(12656821693171000810)
XLA Ops:
  0.6 0.0 copy-start
  0.6 2.6 %shard_map.157 = (bf16[512,256]{1,0:T(8,128)(2,1)}, bf16[2,32,512]{2,1,0:T(8,128)(2,1)}, bf16[2,8,512]{2,1,0:T(8,128)(2,1)}) custom-call(s32[1]{0:T(128)} %bitcast.idx_ref, bf16[128,512]{1,0:T(8,128)(2,1)} %bitcast.17, bf16[128,512]{1,0:T(8,128)(2,1)} %bitcast.18, bf16[512,512]{1,0:T(8,128)(2,1)} %constant.28.clone.t_ref, bf16[2,64,512]{2,1,0:T(8,128)(2,1)} %bitcast.13, ...), custom_call_target="tpu_custom_call" | custom-call | tf_op jit(solution)/shard_map/pallas_call | solution.py:281
  3.3 0.0 copy-start.6
  3.3 18.2 %all-to-all-start = ((bf16[64,8,256]{2,1,0:T(8,128)(2,1)}), bf16[64,8,256]{2,1,0:T(8,128)(2,1)S(1)}, u32[]{:S(2)}, u32[]{:S(2)}) async-start(bf16[64,8,256]{2,1,0:T(8,128)(2,1)} %bitcast.16), calls=%async_computation | async-start | bytes 524288 | tf_op jit(solution)/shard_map/all_to_all | solution.py:296
  21.5 6.0 %collective-permute-start = (bf16[2,32,512]{2,1,0:T(8,128)(2,1)}, bf16[2,32,512]{2,1,0:T(8,128)(2,1)S(1)}, u32[]{:S(2)}, u32[]{:S(2)}) collective-permute-start(bf16[2,32,512]{2,1,0:T(8,128)(2,1)} %get-tuple-element.11), channel_id=1, source_target_pairs={{0,63},{1,62},{2,61},{3,60},{4,59},{5,58},{6,57},{7,56},{8,55},{9,... | collective-permute-start | bytes 196616 | tf_op jit(solution)/shard_map/ppermute | solution.py:297
  27.5 0.0 copy-done.10
  27.5 0.1 collective-permute-start.1
  27.6 12.0 %collective-permute-done.1.head_ref = bf16[2,8,512]{2,1,0:T(8,128)(2,1)S(1)} collective-permute-done((bf16[2,8,512]{2,1,0:T(8,128)(2,1)S(1)}, bf16[2,8,512]{2,1,0:T(8,128)(2,1)S(1)}, u32[]{:S(2)}, u32[]{:S(2)}) %collective-permute-start.1) | collective-permute-done | bytes 16416 | tf_op jit(solution)/shard_map/ppermute | solution.py:298
  39.6 3.4 %collective-permute-done.tail_ref = bf16[2,32,512]{2,1,0:T(8,128)(2,1)S(1)} collective-permute-done((bf16[2,32,512]{2,1,0:T(8,128)(2,1)}, bf16[2,32,512]{2,1,0:T(8,128)(2,1)S(1)}, u32[]{:S(2)}, u32[]{:S(2)}) %collective-permute-start) | collective-permute-done | bytes 65568 | tf_op jit(solution)/shard_map/ppermute | solution.py:297
  43.0 0.0 copy-done
  43.0 0.0 copy-done.5
  43.0 1.1 %shard_map.158.h_ref = f32[512,512]{1,0:T(8,128)S(1)} custom-call(s32[1]{0:T(128)} %bitcast.idx_ref, bf16[2,64,512]{2,1,0:T(8,128)(2,1)S(1)} %bitcast.14, bf16[2,32,512]{2,1,0:T(8,128)(2,1)S(1)} %collective-permute-done.tail_ref, bf16[2,8,512]{2,1,0:T(8,128)(2,1)S(1)} %collective-permute-done.1.head_ref, bf16[3,112,256]{2,1,0:T(8,128)(2,1)S(1)} %copy-done.5, ...), custom_call_target="tpu_custom_call" | custom-call | flops 400000000 | bytes 2000000 | tf_op jit(solution)/shard_map/pallas_call | solution.py:299
  44.1 0.0 all-to-all-done
  44.1 0.0 copy-done.3
  44.1 0.0 copy-done.4
  44.2 2.1 %shard_map.159 = (bf16[512,256]{1,0:T(8,128)(2,1)}, bf16[2,48,512]{2,1,0:T(8,128)(2,1)S(1)}) custom-call(s32[1]{0:T(128)} %bitcast.idx_ref, bf16[512,256]{1,0:T(8,128)(2,1)S(1)} %bitcast.12, bf16[512,512]{1,0:T(8,128)(2,1)S(1)} %copy-done.3, bf16[512,512]{1,0:T(8,128)(2,1)S(1)} %copy-done.4, f32[512,512]{1,0:T(8,128)S(1)} %shard_map.158.h_ref, ...), custom_call_target="tpu_custom_call" | custom-call | tf_op jit(solution)/shard_map/pallas_call | solution.py:308
  46.2 2.1 %collective-permute-start.2 = (bf16[2,32,512]{2,1,0:T(8,128)(2,1)S(1)}, bf16[2,32,512]{2,1,0:T(8,128)(2,1)S(1)}, u32[]{:S(2)}, u32[]{:S(2)}) collective-permute-start(bf16[2,32,512]{2,1,0:T(8,128)(2,1)S(1)} %slice.9), channel_id=1, source_target_pairs={{0,63},{1,62},{2,61},{3,60},{4,59},{5,58},{6,57},{7,56},{8,55},{9,... | collective-permute-start | bytes 196616 | tf_op jit(solution)/shard_map/ppermute | solution.py:319
  48.3 1.8 %collective-permute-start.3 = (bf16[2,8,512]{2,1,0:T(8,128)(2,1)S(1)}, bf16[2,8,512]{2,1,0:T(8,128)(2,1)S(1)}, u32[]{:S(2)}, u32[]{:S(2)}) collective-permute-start(bf16[2,8,512]{2,1,0:T(8,128)(2,1)S(1)} %slice_select_fusion), channel_id=1, source_target_pairs={{31,0},{0,1},{1,2},{2,3},{3,4},{4,5},{5,6},{6,7},{7,8},{8,9},{9,10... | collective-permute-start | bytes 49160 | tf_op jit(solution)/shard_map/ppermute | solution.py:321
  50.1 0.9 collective-permute-done.3.head_ref
  51.0 3.8 %collective-permute-done.2.far_ref = bf16[2,32,512]{2,1,0:T(8,128)(2,1)S(1)} collective-permute-done((bf16[2,32,512]{2,1,0:T(8,128)(2,1)S(1)}, bf16[2,32,512]{2,1,0:T(8,128)(2,1)S(1)}, u32[]{:S(2)}, u32[]{:S(2)}) %collective-permute-start.2) | collective-permute-done | bytes 65568 | tf_op jit(solution)/shard_map/ppermute | solution.py:319
  54.8 0.6 shard_map.161
  55.4 3.2 %collective-permute-start.4 = (bf16[2,64,512]{2,1,0:T(8,128)(2,1)S(1)}, bf16[2,64,512]{2,1,0:T(8,128)(2,1)S(1)}, u32[]{:S(2)}, u32[]{:S(2)}) collective-permute-start(bf16[2,64,512]{2,1,0:T(8,128)(2,1)S(1)} %shard_map.161), channel_id=1, source_target_pairs={{0,128},{64,192},{128,0},{192,64},{256,384},{320,448},{384,256},{4... | collective-permute-start | bytes 393224 | tf_op jit(solution)/shard_map/ppermute | solution.py:333
  58.6 14.8 %all-to-all-start.1 = ((bf16[64,8,256]{2,1,0:T(8,128)(2,1)}), bf16[64,8,256]{2,1,0:T(8,128)(2,1)S(1)}, u32[]{:S(2)}, u32[]{:S(2)}) async-start(bf16[64,8,256]{2,1,0:T(8,128)(2,1)} %bitcast.6), calls=%async_computation.1 | async-start | bytes 524288 | tf_op jit(solution)/shard_map/all_to_all | solution.py:322
  73.4 0.0 copy-start.2
  73.5 0.0 collective-permute-done.4
  73.5 4.7 %collective-permute-start.5 = (bf16[2,64,512]{2,1,0:T(8,128)(2,1)S(1)}, bf16[2,64,512]{2,1,0:T(8,128)(2,1)S(1)}, u32[]{:S(2)}, u32[]{:S(2)}) collective-permute-start(bf16[2,64,512]{2,1,0:T(8,128)(2,1)S(1)} %add_convert_fusion.2), channel_id=1, source_target_pairs={{0,256},{64,320},{128,384},{192,448},{256,0},{320,64},{384,128},{4... | collective-permute-start | bytes 393224 | tf_op jit(solution)/shard_map/ppermute | solution.py:333
  78.2 3.5 %collective-permute-done.5 = bf16[2,64,512]{2,1,0:T(8,128)(2,1)S(1)} collective-permute-done((bf16[2,64,512]{2,1,0:T(8,128)(2,1)S(1)}, bf16[2,64,512]{2,1,0:T(8,128)(2,1)S(1)}, u32[]{:S(2)}, u32[]{:S(2)}) %collective-permute-start.5) | collective-permute-done | bytes 131104 | tf_op jit(solution)/shard_map/ppermute | solution.py:333
  81.7 4.4 %collective-permute-start.6 = (bf16[2,64,512]{2,1,0:T(8,128)(2,1)S(1)}, bf16[2,64,512]{2,1,0:T(8,128)(2,1)S(1)}, u32[]{:S(2)}, u32[]{:S(2)}) collective-permute-start(bf16[2,64,512]{2,1,0:T(8,128)(2,1)S(1)} %add_convert_fusion.1), channel_id=1, source_target_pairs={{0,64},{64,0},{128,192},{192,128},{256,320},{320,256},{384,448},{4... | collective-permute-start | bytes 393224 | tf_op jit(solution)/shard_map/ppermute | solution.py:333
  86.1 3.3 %collective-permute-done.6 = bf16[2,64,512]{2,1,0:T(8,128)(2,1)S(1)} collective-permute-done((bf16[2,64,512]{2,1,0:T(8,128)(2,1)S(1)}, bf16[2,64,512]{2,1,0:T(8,128)(2,1)S(1)}, u32[]{:S(2)}, u32[]{:S(2)}) %collective-permute-start.6) | collective-permute-done | bytes 131104 | tf_op jit(solution)/shard_map/ppermute | solution.py:333
  89.4 0.7 fusion
  90.0 5.6 %all-to-all-done.1 = bf16[64,8,256]{2,1,0:T(8,128)(2,1)S(1)} async-done(((bf16[64,8,256]{2,1,0:T(8,128)(2,1)}), bf16[64,8,256]{2,1,0:T(8,128)(2,1)S(1)}, u32[]{:S(2)}, u32[]{:S(2)}) %all-to-all-start.1) | async-done | bytes 262176 | tf_op jit(solution)/shard_map/all_to_all | solution.py:322
  95.7 1.3 %shard_map.160 = (bf16[128,512]{1,0:T(8,128)(2,1)}, bf16[128,512]{1,0:T(8,128)(2,1)}) custom-call(s32[1]{0:T(128)} %bitcast.idx_ref, bf16[512,256]{1,0:T(8,128)(2,1)S(1)} %bitcast.15, bf16[512,512]{1,0:T(8,128)(2,1)S(1)} %copy-done.2), custom_call_target="tpu_custom_call" | custom-call | flops 400000000 | bytes 2000000 | tf_op jit(solution)/shard_map/pallas_call | solution.py:335
  (18 shorter events, 0.1 us)
Async XLA Ops:
  0.6 42.4 %copy-start = (bf16[512,512]{1,0:T(8,128)(2,1)S(1)}, bf16[512,512]{1,0:T(8,128)(2,1)}, u32[]{:S(2)}) copy-start(bf16[512,512]{1,0:T(8,128)(2,1)} %constant.31.clone.flip_ref) | copy-start | bytes 1572868
  3.3 24.2 %copy-start.10 = (bf16[2,8,512]{2,1,0:T(8,128)(2,1)S(1)}, bf16[2,8,512]{2,1,0:T(8,128)(2,1)}, u32[]{:S(2)}) copy-start(bf16[2,8,512]{2,1,0:T(8,128)(2,1)} %get-tuple-element.12) | copy-start | bytes 49156
  3.3 39.7 %copy-start.1 = (bf16[2,8,8,512]{3,2,1,0:T(8,128)(2,1)S(1)}, bf16[2,8,8,512]{3,2,1,0:T(8,128)(2,1)}, u32[]{:S(2)}) copy-start(bf16[2,8,8,512]{3,2,1,0:T(8,128)(2,1)} %param.16) | copy-start | bytes 393220
  3.3 39.7 %copy-start.5 = (bf16[3,112,256]{2,1,0:T(8,128)(2,1)S(1)}, bf16[3,112,256]{2,1,0:T(8,128)(2,1)}, u32[]{:S(2)}) copy-start(bf16[3,112,256]{2,1,0:T(8,128)(2,1)} %constant.34.clone.own_ref) | copy-start | bytes 516100
  3.3 39.7 %copy-start.6 = (bf16[3,112,256]{2,1,0:T(8,128)(2,1)S(1)}, bf16[3,112,256]{2,1,0:T(8,128)(2,1)}, u32[]{:S(2)}) copy-start(bf16[3,112,256]{2,1,0:T(8,128)(2,1)} %constant.35.clone.mirror_ref) | copy-start | bytes 516100
  3.3 40.8 %all-to-all-start = ((bf16[64,8,256]{2,1,0:T(8,128)(2,1)}), bf16[64,8,256]{2,1,0:T(8,128)(2,1)S(1)}, u32[]{:S(2)}, u32[]{:S(2)}) async-start(bf16[64,8,256]{2,1,0:T(8,128)(2,1)} %bitcast.16), calls=%async_computation | async-start | bytes 524288 | tf_op jit(solution)/shard_map/all_to_all | solution.py:296
  21.5 21.5 %collective-permute-start = (bf16[2,32,512]{2,1,0:T(8,128)(2,1)}, bf16[2,32,512]{2,1,0:T(8,128)(2,1)S(1)}, u32[]{:S(2)}, u32[]{:S(2)}) collective-permute-start(bf16[2,32,512]{2,1,0:T(8,128)(2,1)} %get-tuple-element.11), channel_id=1, source_target_pairs={{0,63},{1,62},{2,61},{3,60},{4,59},{5,58},{6,57},{7,56},{8,55},{9,... | collective-permute-start | bytes 196616 | tf_op jit(solution)/shard_map/ppermute | solution.py:297
  27.5 12.1 %collective-permute-start.1 = (bf16[2,8,512]{2,1,0:T(8,128)(2,1)S(1)}, bf16[2,8,512]{2,1,0:T(8,128)(2,1)S(1)}, u32[]{:S(2)}, u32[]{:S(2)}) collective-permute-start(bf16[2,8,512]{2,1,0:T(8,128)(2,1)S(1)} %copy-done.10), channel_id=1, source_target_pairs={{0,31},{1,0},{2,1},{3,2},{4,3},{5,4},{6,5},{7,6},{8,7},{9,8},{10,9... | collective-permute-start | bytes 49160 | tf_op jit(solution)/shard_map/ppermute | solution.py:298
  27.6 16.5 %copy-start.3 = (bf16[512,512]{1,0:T(8,128)(2,1)S(1)}, bf16[512,512]{1,0:T(8,128)(2,1)}, u32[]{:S(2)}) copy-start(bf16[512,512]{1,0:T(8,128)(2,1)} %constant.29.clone.wc_ref) | copy-start | bytes 1572868
  27.6 16.5 %copy-start.4 = (bf16[512,512]{1,0:T(8,128)(2,1)S(1)}, bf16[512,512]{1,0:T(8,128)(2,1)}, u32[]{:S(2)}) copy-start(bf16[512,512]{1,0:T(8,128)(2,1)} %constant.30.clone.ws_ref) | copy-start | bytes 1572868
  27.6 16.5 %copy-start.7 = (bf16[2,2,48,256]{3,2,1,0:T(8,128)(2,1)S(1)}, bf16[2,2,48,256]{3,2,1,0:T(8,128)(2,1)}, u32[]{:S(2)}) copy-start(bf16[2,2,48,256]{3,2,1,0:T(8,128)(2,1)} %constant.38.clone.gather_ref) | copy-start | bytes 294916
  46.2 8.6 %copy-start.8 = (bf16[4,64,112]{2,1,0:T(8,128)(2,1)S(1)}, bf16[4,64,112]{2,1,0:T(8,128)(2,1)}, u32[]{:S(2)}) copy-start(bf16[4,64,112]{2,1,0:T(8,128)(2,1)} %constant.36.clone.own_ref) | copy-start | bytes 172036
  46.2 8.6 %copy-start.9 = (bf16[4,64,112]{2,1,0:T(8,128)(2,1)S(1)}, bf16[4,64,112]{2,1,0:T(8,128)(2,1)}, u32[]{:S(2)}) copy-start(bf16[4,64,112]{2,1,0:T(8,128)(2,1)} %constant.37.clone.mirror_ref) | copy-start | bytes 172036
  46.2 8.5 %collective-permute-start.2 = (bf16[2,32,512]{2,1,0:T(8,128)(2,1)S(1)}, bf16[2,32,512]{2,1,0:T(8,128)(2,1)S(1)}, u32[]{:S(2)}, u32[]{:S(2)}) collective-permute-start(bf16[2,32,512]{2,1,0:T(8,128)(2,1)S(1)} %slice.9), channel_id=1, source_target_pairs={{0,63},{1,62},{2,61},{3,60},{4,59},{5,58},{6,57},{7,56},{8,55},{9,... | collective-permute-start | bytes 196616 | tf_op jit(solution)/shard_map/ppermute | solution.py:319
  48.3 2.7 %collective-permute-start.3 = (bf16[2,8,512]{2,1,0:T(8,128)(2,1)S(1)}, bf16[2,8,512]{2,1,0:T(8,128)(2,1)S(1)}, u32[]{:S(2)}, u32[]{:S(2)}) collective-permute-start(bf16[2,8,512]{2,1,0:T(8,128)(2,1)S(1)} %slice_select_fusion), channel_id=1, source_target_pairs={{31,0},{0,1},{1,2},{2,3},{3,4},{4,5},{5,6},{6,7},{7,8},{8,9},{9,10... | collective-permute-start | bytes 49160 | tf_op jit(solution)/shard_map/ppermute | solution.py:321
  55.4 18.0 %collective-permute-start.4 = (bf16[2,64,512]{2,1,0:T(8,128)(2,1)S(1)}, bf16[2,64,512]{2,1,0:T(8,128)(2,1)S(1)}, u32[]{:S(2)}, u32[]{:S(2)}) collective-permute-start(bf16[2,64,512]{2,1,0:T(8,128)(2,1)S(1)} %shard_map.161), channel_id=1, source_target_pairs={{0,128},{64,192},{128,0},{192,64},{256,384},{320,448},{384,256},{4... | collective-permute-start | bytes 393224 | tf_op jit(solution)/shard_map/ppermute | solution.py:333
  58.6 37.1 %all-to-all-start.1 = ((bf16[64,8,256]{2,1,0:T(8,128)(2,1)}), bf16[64,8,256]{2,1,0:T(8,128)(2,1)S(1)}, u32[]{:S(2)}, u32[]{:S(2)}) async-start(bf16[64,8,256]{2,1,0:T(8,128)(2,1)} %bitcast.6), calls=%async_computation.1 | async-start | bytes 524288 | tf_op jit(solution)/shard_map/all_to_all | solution.py:322
  73.4 22.2 %copy-start.2 = (bf16[512,512]{1,0:T(8,128)(2,1)S(1)}, bf16[512,512]{1,0:T(8,128)(2,1)}, u32[]{:S(2)}) copy-start(bf16[512,512]{1,0:T(8,128)(2,1)} %constant.28.clone.t_ref) | copy-start | bytes 1572868
  73.5 8.1 %collective-permute-start.5 = (bf16[2,64,512]{2,1,0:T(8,128)(2,1)S(1)}, bf16[2,64,512]{2,1,0:T(8,128)(2,1)S(1)}, u32[]{:S(2)}, u32[]{:S(2)}) collective-permute-start(bf16[2,64,512]{2,1,0:T(8,128)(2,1)S(1)} %add_convert_fusion.2), channel_id=1, source_target_pairs={{0,256},{64,320},{128,384},{192,448},{256,0},{320,64},{384,128},{4... | collective-permute-start | bytes 393224 | tf_op jit(solution)/shard_map/ppermute | solution.py:333
  81.7 7.7 %collective-permute-start.6 = (bf16[2,64,512]{2,1,0:T(8,128)(2,1)S(1)}, bf16[2,64,512]{2,1,0:T(8,128)(2,1)S(1)}, u32[]{:S(2)}, u32[]{:S(2)}) collective-permute-start(bf16[2,64,512]{2,1,0:T(8,128)(2,1)S(1)} %add_convert_fusion.1), channel_id=1, source_target_pairs={{0,64},{64,0},{128,192},{192,128},{256,320},{320,256},{384,448},{4... | collective-permute-start | bytes 393224 | tf_op jit(solution)/shard_map/ppermute | solution.py:333
